TPU v7x, 768 devices: a whole 4x8x12 slice. The times are simulated.
768 devices in a mesh: grid: 48 (over y, z_hi, core), band: 16 (over x, z_lo).
Axes of the slice: x: 4, y: 8, z: 12 (z_hi: 3, z_lo: 4; z = z_hi * 4 + z_lo), core: 2. Of those that a mesh axis runs over, the one named last changes fastest.
Arguments:
- orbitals: float32 [1024, 96, 8, 128], P('band', 'grid'), may hold values from -6 to 6
- potential: float32 [96, 8, 128], P('grid'), may hold values from -8 to 8
- rotation: float32 [1024, 1024], P(None, 'band'), may hold values from -0.1875 to 0.1875
Outputs:
- rotated: float32 [1024, 96, 8, 128], P('band', 'grid')
All inputs are finite; a program needn't handle non-finite values.
Results may differ from a plain program's by a relative error of at most 0.00007.
Values sent between devices are 32-bit elements; how exact they have to be, the bound alone decides.
No kernel may reach another device: no remote copies, remote signals or barrier semaphores. Data moves between devices by JAX's collectives and lax.ppermute only.
A program may use at most 32 MiB of HBM per device.

v0:
```python
import jax
import jax.numpy as jnp
from jax import lax
from jax.sharding import PartitionSpec as P

center_shift = 18.0
half_width = 16.0
spacing_square = 0.25


def padded_2(value, sides, width):
    for axis, dim in sides:
        devices, length = (lax.axis_size(axis), value.shape[dim])
        up = [(i, (i + 1) % devices) for i in range(devices)]
        down = [(j, i) for i, j in up]
        last = lax.slice_in_dim(value, length - width, length, axis=dim)
        leading = lax.slice_in_dim(value, 0, width, axis=dim)
        before = lax.ppermute(last, axis, up)
        after = lax.ppermute(leading, axis, down)
        value = jnp.concatenate([before, value, after], axis=dim)
    return value


def second_along(states, which_axis):
    nearer = jnp.roll(states, 1, which_axis) + jnp.roll(states, -1, which_axis)
    farther = jnp.roll(states, 2, which_axis) + jnp.roll(states, -2, which_axis)
    return (16.0 * nearer - farther - 30.0 * states) / (12.0 * spacing_square)


def scaled_apply(states, potential):
    padded = padded_2(states, (("grid", 1),), 2)
    thickness = states.shape[1]
    nearer = padded[:, 1 : thickness + 1] + padded[:, 3 : thickness + 3]
    farther = padded[:, 0:thickness] + padded[:, 4 : thickness + 4]
    along_x = (16.0 * nearer - farther - 30.0 * states) / (12.0 * spacing_square)
    laplace = along_x + second_along(states, 2) + second_along(states, 3)
    hamilton = -0.5 * laplace + potential[None] * states
    return (hamilton - center_shift * states) / half_width


def per_device(orbitals, potential, rotation):
    scaled_once = scaled_apply(orbitals, potential)
    filtered = 2.0 * scaled_apply(scaled_once, potential) - orbitals
    return jnp.einsum(
        "ob,oxyz->bxyz",
        rotation,
        lax.all_gather(filtered, "band", axis=0, tiled=True),
        precision=lax.Precision.HIGHEST,
    )


def solution(mesh):
    in_specs = (P("band", "grid", None, None), P("grid", None, None), P(None, "band"))
    out_specs = P("band", "grid", None, None)
    return jax.shard_map(
        per_device, mesh=mesh, in_specs=in_specs, out_specs=out_specs, check_vma=False
    )
```

profile of v0, /device:TPU:1, one launch (start us, length us, event | category | flops | bytes accessed | tf_op | source)
XLA Modules:
  0.0 294.2 jit_solution(7420116300213968869)
XLA Ops:
  6.5 0.0 copy-start
  6.5 0.0 copy-start.2
  6.5 0.0 all-gather.2.cloned.1.call-start
  6.5 1.3 copy.4
  7.8 12.0 %collective-permute-start = (f32[64,2,8,128]{3,0,2,1:T(8,128)S(1)}, f32[64,2,8,128]{3,0,2,1:T(8,128)S(1)}, u32[]{:S(2)}, u32[]{:S(2)}) collective-permute-start(f32[64,2,8,128]{3,0,2,1:T(8,128)S(1)} %copy.4), channel_id=1, source_target_pairs={{0,16},{16,32},{32,48},{48,64},{64,80},{80,96},{96,112},{112,128},... | collective-permute-start | bytes 1572872 | tf_op jit(solution)/shard_map/ppermute | solution.py:18
  19.8 2.3 collective-permute-start.1
  22.1 0.2 fusion.45
  22.3 0.2 fusion.46
  22.6 0.2 fusion.47
  22.8 0.1 fusion.44
  22.9 0.0 copy-done.2
  22.9 0.1 fusion.42
  23.0 0.2 fusion.48
  23.2 3.0 %collective-permute-done = f32[64,2,8,128]{3,0,2,1:T(8,128)S(1)} collective-permute-done((f32[64,2,8,128]{3,0,2,1:T(8,128)S(1)}, f32[64,2,8,128]{3,0,2,1:T(8,128)S(1)}, u32[]{:S(2)}, u32[]{:S(2)}) %collective-permute-start) | collective-permute-done | bytes 524320 | tf_op jit(solution)/shard_map/ppermute | solution.py:18
  26.3 21.5 %collective-permute-done.1 = f32[64,2,8,128]{3,0,2,1:T(8,128)S(1)} collective-permute-done((f32[64,2,8,128]{3,0,2,1:T(8,128)S(1)}, f32[64,2,8,128]{3,0,2,1:T(8,128)S(1)}, u32[]{:S(2)}, u32[]{:S(2)}) %collective-permute-start.1) | collective-permute-done | bytes 524320 | tf_op jit(solution)/shard_map/ppermute | solution.py:19
  47.8 0.9 broadcast_multiply_fusion
  48.7 0.0 copy-start.1
  48.7 0.2 fusion.34
  48.9 0.2 fusion.35
  49.2 0.2 fusion.36
  49.4 0.1 fusion.37
  49.5 1.9 collective-permute-start.2
  51.4 7.0 %collective-permute-start.3 = (f32[64,2,8,128]{3,0,2,1:T(8,128)S(1)}, f32[64,2,8,128]{3,0,2,1:T(8,128)S(1)}, u32[]{:S(2)}, u32[]{:S(2)}) collective-permute-start(f32[64,2,8,128]{3,0,2,1:T(8,128)S(1)} %get-tuple-element.5), channel_id=1, source_target_pairs={{16,0},{32,16},{48,32},{64,48},{80,64},{96,80},{112,96},{128,112},... | collective-permute-start | bytes 1572872 | tf_op jit(solution)/shard_map/ppermute | solution.py:19
  58.4 0.1 fusion.39
  58.5 0.2 fusion.33
  58.7 15.4 %collective-permute-done.2 = f32[64,2,8,128]{3,0,2,1:T(8,128)S(1)} collective-permute-done((f32[64,2,8,128]{3,0,2,1:T(8,128)S(1)}, f32[64,2,8,128]{3,0,2,1:T(8,128)S(1)}, u32[]{:S(2)}, u32[]{:S(2)}) %collective-permute-start.2) | collective-permute-done | bytes 524320 | tf_op jit(solution)/shard_map/ppermute | solution.py:18
  74.1 0.0 collective-permute-done.3
  74.1 0.0 copy-done.1
  74.1 1.8 fusion.10
  75.9 0.0 all-gather.2.cloned.1.call-update
  76.0 202.5 %all-gather.2.cloned.1.call-done = f32[1024,2,8,128]{3,0,2,1:T(8,128)} async-done(((f32[64,2,8,128]{3,0,2,1:T(8,128)}), f32[1024,2,8,128]{3,0,2,1:T(8,128)}) %all-gather.2.cloned.1.call-update) | async-done | bytes 8388624 | tf_op jit(solution)/shard_map/all_gather | solution.py:47
  278.4 0.0 copy-done
  278.5 7.8 %convolution_bitcast_fusion = f32[64,2,8,128]{3,0,2,1:T(8,128)S(1)} fusion(f32[1024,2,8,128]{3,0,2,1:T(8,128)} %all-gather.2.cloned.1.call-done, f32[1024,64]{0,1:T(8,128)S(1)} %copy-done), kind=kOutput, calls=%fused_computation | convolution fusion | flops 1610612736 | bytes 9175040 | tf_op jit(solution)/shard_map/ob,oxyz->bxyz/dot_general | solution.py:44
  286.3 1.1 copy.28
  (5 shorter events, 0.1 us)
Async XLA Ops:
  6.5 271.9 %copy-start = (f32[1024,64]{0,1:T(8,128)S(1)}, f32[1024,64]{0,1:T(8,128)}, u32[]{:S(2)}) copy-start(f32[1024,64]{0,1:T(8,128)} %param.5) | copy-start | bytes 786436
  6.5 16.4 %copy-start.2 = (f32[2,8,128]{2,1,0:T(8,128)S(1)}, f32[2,8,128]{2,1,0:T(8,128)}, u32[]{:S(2)}) copy-start(f32[2,8,128]{2,1,0:T(8,128)} %param.4) | copy-start | bytes 24580
  6.5 271.9 %all-gather.2.cloned.1.call-start = ((), (), s32[]{:S(2)}) async-start(), calls=%async_computation | async-start | bytes 8912896 | tf_op jit(solution)/shard_map/all_gather | solution.py:47
  7.8 18.5 %collective-permute-start = (f32[64,2,8,128]{3,0,2,1:T(8,128)S(1)}, f32[64,2,8,128]{3,0,2,1:T(8,128)S(1)}, u32[]{:S(2)}, u32[]{:S(2)}) collective-permute-start(f32[64,2,8,128]{3,0,2,1:T(8,128)S(1)} %copy.4), channel_id=1, source_target_pairs={{0,16},{16,32},{32,48},{48,64},{64,80},{80,96},{96,112},{112,128},... | collective-permute-start | bytes 1572872 | tf_op jit(solution)/shard_map/ppermute | solution.py:18
  19.8 27.9 %collective-permute-start.1 = (f32[64,2,8,128]{3,0,2,1:T(8,128)S(1)}, f32[64,2,8,128]{3,0,2,1:T(8,128)S(1)}, u32[]{:S(2)}, u32[]{:S(2)}) collective-permute-start(f32[64,2,8,128]{3,0,2,1:T(8,128)S(1)} %copy.4), channel_id=1, source_target_pairs={{16,0},{32,16},{48,32},{64,48},{80,64},{96,80},{112,96},{128,112},... | collective-permute-start | bytes 1572872 | tf_op jit(solution)/shard_map/ppermute | solution.py:19
  48.7 25.4 %copy-start.1 = (f32[64,2,8,128]{3,2,1,0:T(8,128)S(1)}, f32[64,2,8,128]{3,2,1,0:T(8,128)}, u32[]{:S(2)}) copy-start(f32[64,2,8,128]{3,2,1,0:T(8,128)} %param.3) | copy-start | bytes 1572868
  49.5 24.6 %collective-permute-start.2 = (f32[64,2,8,128]{3,0,2,1:T(8,128)S(1)}, f32[64,2,8,128]{3,0,2,1:T(8,128)S(1)}, u32[]{:S(2)}, u32[]{:S(2)}) collective-permute-start(f32[64,2,8,128]{3,0,2,1:T(8,128)S(1)} %get-tuple-element.5), channel_id=1, source_target_pairs={{0,16},{16,32},{32,48},{48,64},{64,80},{80,96},{96,112},{112,128},... | collective-permute-start | bytes 1572872 | tf_op jit(solution)/shard_map/ppermute | solution.py:18
  51.4 22.7 %collective-permute-start.3 = (f32[64,2,8,128]{3,0,2,1:T(8,128)S(1)}, f32[64,2,8,128]{3,0,2,1:T(8,128)S(1)}, u32[]{:S(2)}, u32[]{:S(2)}) collective-permute-start(f32[64,2,8,128]{3,0,2,1:T(8,128)S(1)} %get-tuple-element.5), channel_id=1, source_target_pairs={{16,0},{32,16},{48,32},{64,48},{80,64},{96,80},{112,96},{128,112},... | collective-permute-start | bytes 1572872 | tf_op jit(solution)/shard_map/ppermute | solution.py:19
Sparse Core Ops, SparseCore 0:
  76.1 202.3 all-gather.1
where the time goes:
time: 294 us
  waiting for transfers between devices  242 us (82%)
  starting transfers between devices  23.2 us (8%)
  between operations  13.5 us (5%)
  matrix products  7.81 us (3%)
  local copies, waits for them, and re-layouts  4.5 us (2%)
    all_gather x1, waiting for transfers between devices, per_device(): lax.all_gather(filtered, 'band', axis=0, tiled=True)  202 us
    ppermute x2, waiting for transfers between devices, padded_2(): after = lax.ppermute(leading, axis, down)  21.5 us
    ppermute x2, waiting for transfers between devices, padded_2(): before = lax.ppermute(last, axis, up)  18.4 us
    ppermute x2, starting transfers between devices, padded_2(): before = lax.ppermute(last, axis, up)  13.9 us
    ppermute x2, starting transfers between devices, padded_2(): after = lax.ppermute(leading, axis, down)  9.27 us
    dot_general x1, matrix products, per_device(): jnp.einsum('ob,oxyz->bxyz', rotation, lax.all_gather(filtered, 'band', ax...  7.81 us
  transfers between devices with their start and end apart: 5, of which 4 were waited for; matrix products, arithmetic and copies ran while one was open for 0% of the time, Pallas kernels for 0%

commit v1 on v0

v1 whole, which is shorter than its diff:
```python
import jax
import jax.numpy as jnp
from jax import lax
from jax.experimental import pallas as pl
from jax.experimental.pallas import tpu as pltpu
from jax.sharding import PartitionSpec as P

GROUP = 8


def shifted_sums(c, axis):
    n = c.shape[axis]
    near = pltpu.roll(c, 1, axis) + pltpu.roll(c, n - 1, axis)
    far = pltpu.roll(c, 2, axis) + pltpu.roll(c, n - 2, axis)
    return near, far


def apply_plane(c, near_x, far_x, pot):
    near_y, far_y = shifted_sums(c, 1)
    near_z, far_z = shifted_sums(c, 2)
    near = near_x + near_y + near_z
    far = far_x + far_y + far_z
    return c * pot - (1.0 / 6.0) * near + (1.0 / 96.0) * far


def stencil_kernel(combine, par_ref, own, outer, inner, pot_ref, *rest):
    base, out = rest if combine else (None, rest[0])
    par = par_ref[0]
    other = 1 - par
    pot_a = ((pot_ref[par] - 3.0) * 0.0625)[None]
    pot_b = ((pot_ref[other] - 3.0) * 0.0625)[None]

    @pl.loop(0, own.shape[0] // GROUP)
    def _(step):
        rows = pl.ds(step * GROUP, GROUP)
        a, b = own[rows, par], own[rows, other]
        o1, o2 = outer[rows, other], outer[rows, par]
        i1, i2 = inner[rows, par], inner[rows, other]
        sa = apply_plane(a, o1 + b, o2 + i1, pot_a)
        sb = apply_plane(b, a + i1, o1 + i2, pot_b)
        if combine:
            sa = 2.0 * sa - base[rows, par]
            sb = 2.0 * sb - base[rows, other]
        out[rows, par] = sa
        out[rows, other] = sb


def stencil(par, own, outer, inner, pot, base=None):
    combine = base is not None
    args = (own, outer, inner, pot) + ((base,) if combine else ())
    return pl.pallas_call(
        lambda *refs: stencil_kernel(combine, *refs),
        out_shape=jax.ShapeDtypeStruct(own.shape, own.dtype),
        in_specs=[pl.BlockSpec(memory_space=pltpu.SMEM)]
        + [pl.BlockSpec(memory_space=pltpu.VMEM)] * len(args),
        out_specs=pl.BlockSpec(memory_space=pltpu.VMEM),
        name="stencil",
    )(par, *args)


def swap(value, pairs):
    return lax.ppermute(value, "grid", pairs)


def per_device(orbitals, potential, rotation):
    devices = lax.axis_size("grid")
    outer_pairs = [(i, (i + 1 if i % 2 else i - 1) % devices) for i in range(devices)]
    inner_pairs = [(i, i ^ 1) for i in range(devices)]
    par = (lax.axis_index("grid") % 2).astype(jnp.int32).reshape(1)
    rot_t = lax.all_gather(rotation.T, "band", axis=0, tiled=True)

    first = stencil(
        par, orbitals, swap(orbitals, outer_pairs), swap(orbitals, inner_pairs), potential
    )
    filtered = stencil(
        par, first, swap(first, outer_pairs), swap(first, inner_pairs), potential, orbitals
    )
    orbs, planes, ny, nz = orbitals.shape
    groups = lax.axis_size("band")
    rows = planes * ny
    parts = filtered.reshape(orbs, rows, nz).transpose(1, 0, 2)
    parts = lax.all_to_all(parts, "band", 0, 0, tiled=True)
    mixed = jnp.dot(
        rot_t,
        parts.reshape(groups * orbs, nz),
        precision=lax.Precision.HIGH,
        preferred_element_type=jnp.float32,
    )
    back = lax.all_to_all(mixed.reshape(groups, orbs, nz), "band", 0, 0, tiled=True)
    return back.transpose(1, 0, 2).reshape(orbs, planes, ny, nz)


def solution(mesh):
    in_specs = (P("band", "grid", None, None), P("grid", None, None), P(None, "band"))
    out_specs = P("band", "grid", None, None)
    return jax.shard_map(
        per_device, mesh=mesh, in_specs=in_specs, out_specs=out_specs, check_vma=False
    )
```

time: 294 us -> 200 us (0.68)
  waiting for transfers between devices: 242 us -> 63.2 us
  blocking collectives: 0 us -> 76.7 us
  starting transfers between devices: 23.2 us -> 30.3 us
  Pallas kernels: 0 us -> 6.78 us
  matrix products: 7.81 us -> 4.45 us
    all_gather x1, waiting for transfers between devices: 202 us -> 30 us  [per_device(): rot_t = lax.all_gather(rotation.T, 'band', axis=0, tiled=True)]
    all_to_all x0 -> x2, blocking collectives: none -> 76.7 us  [the longest x1 54.6 us: per_device(): parts = lax.all_to_all(parts, 'band', 0, 0, tiled=True)]
    ppermute x4, waiting for transfers between devices: 39.9 us -> 32.4 us  [swap(): return lax.ppermute(value, 'grid', pairs)]
    ppermute x4, starting transfers between devices: 23.2 us -> 30.3 us  [swap(): return lax.ppermute(value, 'grid', pairs)]
    pallas_call x0 -> x2, Pallas kernels: none -> 6.78 us  [stencil(): pl.pallas_call(lambda *refs: stencil_kernel(combine, *refs), out_shape=ja...]
    dot_general x1, matrix products: 7.81 us -> 4.45 us  [per_device(): jnp.dot(rot_t, parts.reshape(groups * orbs, nz), precision=lax.Precision....]
  transfers between devices with their start and end apart: 5 -> 5, of which waited for: 4 -> 3; matrix products, arithmetic and copies ran while one was open for 0% -> 1% of each run, Pallas kernels for 0% -> 3%
where the time goes in v1:
time: 200 us
  blocking collectives  76.7 us (38%)
  waiting for transfers between devices  63.2 us (32%)
  starting transfers between devices  30.3 us (15%)
  between operations  13.5 us (7%)
  Pallas kernels  6.78 us (3%)
  local copies, waits for them, and re-layouts  5.05 us (3%)
  matrix products  4.45 us (2%)
    all_to_all x1, blocking collectives, per_device(): parts = lax.all_to_all(parts, 'band', 0, 0, tiled=True)  54.6 us
    ppermute x4, waiting for transfers between devices, swap(): return lax.ppermute(value, 'grid', pairs)  32.4 us
    ppermute x4, starting transfers between devices, swap(): return lax.ppermute(value, 'grid', pairs)  30.3 us
    all_gather x1, waiting for transfers between devices, per_device(): rot_t = lax.all_gather(rotation.T, 'band', axis=0, tiled=True)  30 us
    all_to_all x1, blocking collectives, per_device(): lax.all_to_all(mixed.reshape(groups, orbs, nz), 'band', 0, 0, tiled=True)  22.1 us
    pallas_call x2, Pallas kernels, stencil(): pl.pallas_call(lambda *refs: stencil_kernel(combine, *refs), out_shape=ja...  6.78 us
    dot_general x1, matrix products, per_device(): jnp.dot(rot_t, parts.reshape(groups * orbs, nz), precision=lax.Precision....  4.45 us
  transfers between devices with their start and end apart: 5, of which 3 were waited for; matrix products, arithmetic and copies ran while one was open for 1% of the time, Pallas kernels for 3%

profile of v1, /device:TPU:1, one launch (start us, length us, event | category | flops | bytes accessed | tf_op | source)
XLA Modules:
  0.0 199.9 jit_solution(565063067675394746)
XLA Ops:
  6.5 0.0 all-gather.2.cloned.1.call-start
  6.5 0.7 all-gather.2.cloned.1.call-update
  7.3 12.0 %collective-permute-start = (f32[64,2,8,128]{3,2,1,0:T(8,128)}, f32[64,2,8,128]{3,2,1,0:T(8,128)S(1)}, u32[]{:S(2)}, u32[]{:S(2)}) collective-permute-start(f32[64,2,8,128]{3,2,1,0:T(8,128)} %refs_5_.1), channel_id=1, source_target_pairs={{0,752},{16,32},{32,16},{48,64},{64,48},{80,96},{96,80},{112,128},... | collective-permute-start | bytes 1572872 | tf_op jit(solution)/shard_map/ppermute | solution.py:62
  19.3 8.3 %collective-permute-start.1 = (f32[64,2,8,128]{3,2,1,0:T(8,128)}, f32[64,2,8,128]{3,2,1,0:T(8,128)S(1)}, u32[]{:S(2)}, u32[]{:S(2)}) collective-permute-start(f32[64,2,8,128]{3,2,1,0:T(8,128)} %refs_5_.1), channel_id=1, source_target_pairs={{0,16},{16,0},{32,48},{48,32},{64,80},{80,64},{96,112},{112,96},{1... | collective-permute-start | bytes 1572872 | tf_op jit(solution)/shard_map/ppermute | solution.py:62
  27.6 16.0 %collective-permute-done.refs_2_ = f32[64,2,8,128]{3,2,1,0:T(8,128)S(1)} collective-permute-done((f32[64,2,8,128]{3,2,1,0:T(8,128)}, f32[64,2,8,128]{3,2,1,0:T(8,128)S(1)}, u32[]{:S(2)}, u32[]{:S(2)}) %collective-permute-start) | collective-permute-done | bytes 524320 | tf_op jit(solution)/shard_map/ppermute | solution.py:62
  43.6 0.0 copy-start
  43.6 0.0 collective-permute-done.1.refs_3_
  43.6 0.0 copy-start.1
  43.6 0.8 copy-done
  44.4 0.2 copy-done.1
  44.6 3.3 %stencil.2.refs_1_ = f32[64,2,8,128]{3,2,1,0:T(8,128)} custom-call(s32[1]{0:T(128)} %bitcast.refs_0_, f32[64,2,8,128]{3,2,1,0:T(8,128)} %refs_5_.1, f32[64,2,8,128]{3,2,1,0:T(8,128)} %copy-done, f32[64,2,8,128]{3,2,1,0:T(8,128)} %copy-done.1, f32[2,8,128]{2,1,0:T(8,128)} %refs_4_.3), custom_call_target="tpu_custom_call" | custom-call | tf_op jit(solution)/shard_map/stencil/pallas_call | solution.py:51
  47.9 1.9 collective-permute-start.2
  49.8 8.1 %collective-permute-start.3 = (f32[64,2,8,128]{3,2,1,0:T(8,128)}, f32[64,2,8,128]{3,2,1,0:T(8,128)S(1)}, u32[]{:S(2)}, u32[]{:S(2)}) collective-permute-start(f32[64,2,8,128]{3,2,1,0:T(8,128)} %stencil.2.refs_1_), channel_id=1, source_target_pairs={{0,16},{16,0},{32,48},{48,32},{64,80},{80,64},{96,112},{112,96},{1... | collective-permute-start | bytes 1572872 | tf_op jit(solution)/shard_map/ppermute | solution.py:62
  57.9 16.4 %collective-permute-done.2.refs_2_ = f32[64,2,8,128]{3,2,1,0:T(8,128)S(1)} collective-permute-done((f32[64,2,8,128]{3,2,1,0:T(8,128)}, f32[64,2,8,128]{3,2,1,0:T(8,128)S(1)}, u32[]{:S(2)}, u32[]{:S(2)}) %collective-permute-start.2) | collective-permute-done | bytes 524320 | tf_op jit(solution)/shard_map/ppermute | solution.py:62
  74.3 0.0 copy-start.2
  74.3 0.0 collective-permute-done.3.refs_3_
  74.3 0.8 copy-done.2
  75.1 0.0 copy-start.3
  75.1 0.8 copy-done.3
  75.9 3.5 %stencil.3 = f32[64,2,8,128]{3,2,1,0:T(8,128)} custom-call(s32[1]{0:T(128)} %bitcast.refs_0_, f32[64,2,8,128]{3,2,1,0:T(8,128)} %stencil.2.refs_1_, f32[64,2,8,128]{3,2,1,0:T(8,128)} %copy-done.2, f32[64,2,8,128]{3,2,1,0:T(8,128)} %copy-done.3, f32[2,8,128]{2,1,0:T(8,128)} %refs_4_.3, f32[64,2,8,128]{3,2,1,0:T(8,128)} %refs_5_.1), custom_call_target="tpu_custom_call" | custom-call | tf_op jit(solution)/shard_map/stencil/pallas_call | solution.py:51
  79.4 1.2 copy.9
  80.6 54.6 %all_to_all.10 = f32[16,64,128]{2,1,0:T(8,128)S(1)} all-to-all(f32[16,64,128]{2,1,0:T(8,128)S(1)} %bitcast.16), channel_id=1, replica_groups=mesh['grid'=48,'band'=16] {'band'}, dimensions={0} | all-to-all | bytes 1048576 | tf_op jit(solution)/shard_map/all_to_all | solution.py:82
  135.2 30.0 %all-gather.2.cloned.1.call-done = f32[1024,1024]{1,0:T(8,128)} async-done(((f32[64,1024]{1,0:T(8,128)}), f32[1024,1024]{1,0:T(8,128)}) %all-gather.2.cloned.1.call-update) | async-done | bytes 4194320 | tf_op jit(solution)/shard_map/all_gather | solution.py:70
  165.2 4.4 %convolution_bitcast_fusion = f32[1024,128]{0,1:T(8,128)S(1)} fusion(f32[1024,128]{1,0:T(8,128)S(1)} %bitcast.15, f32[1024,1024]{1,0:T(8,128)} %all-gather.2.cloned.1.call-done), kind=kOutput, calls=%fused_computation | convolution fusion | flops 805306368 | bytes 5242880 | tf_op jit(solution)/shard_map/dot_general | solution.py:83
  169.6 0.2 copy.6
  169.8 22.1 %all_to_all.11 = f32[16,64,128]{2,1,0:T(8,128)S(1)} all-to-all(f32[16,64,128]{2,1,0:T(8,128)S(1)} %bitcast.17), channel_id=1, replica_groups=mesh['grid'=48,'band'=16] {'band'}, dimensions={0} | all-to-all | bytes 1048576 | tf_op jit(solution)/shard_map/all_to_all | solution.py:89
  192.0 1.1 copy.7
Async XLA Ops:
  6.5 158.6 %all-gather.2.cloned.1.call-start = ((), (), s32[]{:S(2)}) async-start(), calls=%async_computation.2 | async-start | bytes 4456448 | tf_op jit(solution)/shard_map/all_gather | solution.py:70
  7.3 36.4 %collective-permute-start = (f32[64,2,8,128]{3,2,1,0:T(8,128)}, f32[64,2,8,128]{3,2,1,0:T(8,128)S(1)}, u32[]{:S(2)}, u32[]{:S(2)}) collective-permute-start(f32[64,2,8,128]{3,2,1,0:T(8,128)} %refs_5_.1), channel_id=1, source_target_pairs={{0,752},{16,32},{32,16},{48,64},{64,48},{80,96},{96,80},{112,128},... | collective-permute-start | bytes 1572872 | tf_op jit(solution)/shard_map/ppermute | solution.py:62
  19.3 24.4 %collective-permute-start.1 = (f32[64,2,8,128]{3,2,1,0:T(8,128)}, f32[64,2,8,128]{3,2,1,0:T(8,128)S(1)}, u32[]{:S(2)}, u32[]{:S(2)}) collective-permute-start(f32[64,2,8,128]{3,2,1,0:T(8,128)} %refs_5_.1), channel_id=1, source_target_pairs={{0,16},{16,0},{32,48},{48,32},{64,80},{80,64},{96,112},{112,96},{1... | collective-permute-start | bytes 1572872 | tf_op jit(solution)/shard_map/ppermute | solution.py:62
  43.6 0.8 copy-start
  43.6 1.0 copy-start.1
  47.9 26.4 %collective-permute-start.2 = (f32[64,2,8,128]{3,2,1,0:T(8,128)}, f32[64,2,8,128]{3,2,1,0:T(8,128)S(1)}, u32[]{:S(2)}, u32[]{:S(2)}) collective-permute-start(f32[64,2,8,128]{3,2,1,0:T(8,128)} %stencil.2.refs_1_), channel_id=1, source_target_pairs={{0,752},{16,32},{32,16},{48,64},{64,48},{80,96},{96,80},{112,128},... | collective-permute-start | bytes 1572872 | tf_op jit(solution)/shard_map/ppermute | solution.py:62
  49.8 24.5 %collective-permute-start.3 = (f32[64,2,8,128]{3,2,1,0:T(8,128)}, f32[64,2,8,128]{3,2,1,0:T(8,128)S(1)}, u32[]{:S(2)}, u32[]{:S(2)}) collective-permute-start(f32[64,2,8,128]{3,2,1,0:T(8,128)} %stencil.2.refs_1_), channel_id=1, source_target_pairs={{0,16},{16,0},{32,48},{48,32},{64,80},{80,64},{96,112},{112,96},{1... | collective-permute-start | bytes 1572872 | tf_op jit(solution)/shard_map/ppermute | solution.py:62
  74.3 0.8 copy-start.2
  75.1 0.8 copy-start.3
Sparse Core Ops, SparseCore 0:
  9.7 155.4 all-gather.1

commit v2 on v1

v2 whole, which is shorter than its diff:
```python
import jax
import jax.numpy as jnp
import numpy as np
from jax import lax
from jax.experimental import pallas as pl
from jax.experimental.pallas import tpu as pltpu
from jax.sharding import Mesh, PartitionSpec as P

GROUP = 8
GRID = ("y", "zh", "c")
BAND = ("x", "zl")


def shifted_sums(c, axis):
    n = c.shape[axis]
    near = pltpu.roll(c, 1, axis) + pltpu.roll(c, n - 1, axis)
    far = pltpu.roll(c, 2, axis) + pltpu.roll(c, n - 2, axis)
    return near, far


def apply_plane(c, near_x, far_x, pot):
    near_y, far_y = shifted_sums(c, 1)
    near_z, far_z = shifted_sums(c, 2)
    near = near_x + near_y + near_z
    far = far_x + far_y + far_z
    return c * pot - (1.0 / 6.0) * near + (1.0 / 96.0) * far


def stencil_kernel(combine, par_ref, own, outer, inner, pot_ref, *rest):
    base, out = rest if combine else (None, rest[0])
    par = par_ref[0]
    other = 1 - par
    pot_a = ((pot_ref[par] - 3.0) * 0.0625)[None]
    pot_b = ((pot_ref[other] - 3.0) * 0.0625)[None]

    @pl.loop(0, own.shape[0] // GROUP)
    def _(step):
        rows = pl.ds(step * GROUP, GROUP)
        a, b = own[rows, par], own[rows, other]
        o1, o2 = outer[rows, other], outer[rows, par]
        i1, i2 = inner[rows, par], inner[rows, other]
        sa = apply_plane(a, o1 + b, o2 + i1, pot_a)
        sb = apply_plane(b, a + i1, o1 + i2, pot_b)
        if combine:
            sa = 2.0 * sa - base[rows, par]
            sb = 2.0 * sb - base[rows, other]
            out[par, :, rows] = jnp.swapaxes(sa, 0, 1)
            out[other, :, rows] = jnp.swapaxes(sb, 0, 1)
        else:
            out[rows, par] = sa
            out[rows, other] = sb


def in_vmem(value):
    return pltpu.with_memory_space_constraint(value, pltpu.VMEM)


def stencil(par, own, outer, inner, pot, base=None):
    combine = base is not None
    orbs, planes, ny, nz = own.shape
    args = (own, outer, inner, pot) + ((base,) if combine else ())
    shape = (planes, ny, orbs, nz) if combine else own.shape
    return pl.pallas_call(
        lambda *refs: stencil_kernel(combine, *refs),
        out_shape=pltpu.VMEM(shape, own.dtype),
        in_specs=[pl.BlockSpec(memory_space=pltpu.SMEM)]
        + [pl.BlockSpec(memory_space=pltpu.VMEM)] * len(args),
        out_specs=pl.BlockSpec(memory_space=pltpu.VMEM),
        compiler_params=pltpu.CompilerParams(vmem_limit_bytes=4 << 20),
        name="stencil",
    )(par, *map(in_vmem, args))


def rotate_kernel(nx, ny, nzl, at_ref, v, own, own2, near, near2, far, far2, out, wide):
    core, x = at_ref[0], at_ref[1]
    half = own.shape[1]
    value = v[...]
    high = value.astype(jnp.bfloat16)
    low = (value - high.astype(jnp.float32)).astype(jnp.bfloat16)
    wide[...] = jnp.concatenate([high, low], axis=1)
    nz = v.shape[1]

    def product(piece, which):
        high = piece.astype(jnp.bfloat16)
        low = (piece - high.astype(jnp.float32)).astype(jnp.bfloat16)
        rows = pl.ds(pl.multiple_of(which * half, half), half)
        both = jnp.dot(high, wide[rows, :], preferred_element_type=jnp.float32)
        rest = jnp.dot(low, wide[rows, :nz], preferred_element_type=jnp.float32)
        return both[:, :nz] + both[:, nz:] + rest

    def slab(first, second, first_half, slab_x):
        total = product(first, first_half) + product(second, 1 - first_half)
        rows = total.shape[0] // (ny * nzl)
        for y in range(ny):
            for z in range(nzl):
                at = (y * nzl + z) * rows
                out[slab_x * nzl + z, pl.ds(y * rows, rows)] = total[at : at + rows]

    step = 1 - 2 * core
    slab(own[...], own2[...], core, x)
    slab(near[0], near[1], core, lax.rem(x - step + nx, nx))
    slab(near2[0], near2[1], 1 - core, lax.rem(x + step + nx, nx))
    slab(far[...], far2[...], core, lax.rem(x + 2, nx))


def rotate(sizes, at, v, pieces, shape):
    nx, ny, nzl = sizes
    return pl.pallas_call(
        lambda *refs: rotate_kernel(nx, ny, nzl, *refs),
        out_shape=pltpu.VMEM(shape, v.dtype),
        in_specs=[pl.BlockSpec(memory_space=pltpu.SMEM)]
        + [pl.BlockSpec(memory_space=pltpu.VMEM)] * (1 + len(pieces)),
        out_specs=pl.BlockSpec(memory_space=pltpu.VMEM),
        scratch_shapes=[pltpu.VMEM((v.shape[0], 2 * v.shape[1]), jnp.bfloat16)],
        compiler_params=pltpu.CompilerParams(vmem_limit_bytes=24 << 20),
        name="rotate",
    )(at, *map(in_vmem, (v, *pieces)))


def to_all(value, axis):
    copies = jnp.broadcast_to(value[None], (lax.axis_size(axis), *value.shape))
    return lax.all_to_all(copies, axis, 0, 0, tiled=True)


def gather_rotation(rot_t):
    nx, ny = lax.axis_size("x"), lax.axis_size("y")
    rows, cols = rot_t.shape[0] // ny, rot_t.shape[1] // 2
    y, core = lax.axis_index("y"), lax.axis_index("c")
    part = lax.dynamic_slice(rot_t, (y * rows, core * cols), (rows, cols))
    part = to_all(part, "zl")
    own = to_all(part, "y").reshape(-1, cols)
    flip = [(0, 1), (1, 0)]
    line = [(c * nx + i, c * nx + (i + 1 - 2 * c) % nx) for i in range(nx) for c in (0, 1)]
    own2 = lax.ppermute(own, "c", flip)
    near = lax.ppermute(jnp.stack([own, own2]), ("c", "x"), line)
    far = lax.ppermute(near[0], ("c", "x"), line)
    near2 = lax.ppermute(near, "c", flip)
    far2 = lax.ppermute(far, "c", flip)
    return own, own2, near, near2, far, far2


def swap(value, pairs):
    return lax.ppermute(value, GRID, pairs)


def per_device(orbitals, potential, rotation):
    devices = lax.axis_size(GRID)
    outer_pairs = [(i, (i + 1 if i % 2 else i - 1) % devices) for i in range(devices)]
    inner_pairs = [(i, i ^ 1) for i in range(devices)]
    core = lax.axis_index("c").astype(jnp.int32)
    at = jnp.stack([core, lax.axis_index("x").astype(jnp.int32)])
    pieces = gather_rotation(rotation.T)

    outer = swap(orbitals, outer_pairs)
    inner = swap(orbitals, inner_pairs)
    first = stencil(at, orbitals, outer, inner, potential)
    outer = swap(first, outer_pairs)
    inner = swap(first, inner_pairs)
    filtered = stencil(at, first, outer, inner, potential, orbitals)
    orbs, planes, ny, nz = orbitals.shape
    groups = lax.axis_size(BAND)
    parts = filtered.reshape(groups, -1, nz)
    parts = lax.all_to_all(parts, BAND, 0, 0, tiled=True)
    sizes = lax.axis_size("x"), lax.axis_size("y"), lax.axis_size("zl")
    mixed = rotate(sizes, at, parts.reshape(groups * orbs, nz), pieces, (groups, orbs, nz))
    back = lax.all_to_all(mixed, BAND, 0, 0, tiled=True)
    return back.transpose(1, 0, 2).reshape(orbs, planes, ny, nz)


def run(fine):
    in_specs = (P(BAND, GRID, None, None), P(GRID, None, None), P(None, BAND))
    return jax.shard_map(
        per_device, mesh=fine, in_specs=in_specs, out_specs=P(BAND, GRID, None, None), check_vma=False
    )


def solution(mesh):
    devices = np.asarray(mesh.devices).reshape(8, 3, 2, 4, 4)
    fine = Mesh(devices, GRID + BAND)
    return run(fine)
```

time: 200 us -> 165 us (0.82)
  the two profiles are of different devices: /device:TPU:1 before, /device:TPU:8 now
where the time goes in v2:
time: 165 us; the launch traced here: 164 us
  blocking collectives  58 us (35%)
  starting transfers between devices  50.6 us (31%)
  waiting for transfers between devices  44.8 us (27%)
  Pallas kernels  7.47 us (5%)
  local copies, waits for them, and re-layouts  2.16 us (1%)
    all_to_all x2, blocking collectives, to_all(): return lax.all_to_all(copies, axis, 0, 0, tiled=True)  34.9 us
    ppermute x4, waiting for transfers between devices, swap(): return lax.ppermute(value, GRID, pairs)  34.3 us
    ppermute x4, starting transfers between devices, swap(): return lax.ppermute(value, GRID, pairs)  25.4 us
    all_to_all x1, blocking collectives, per_device(): back = lax.all_to_all(mixed, BAND, 0, 0, tiled=True)  23.1 us
    all_to_all x1, starting transfers between devices, per_device(): parts = lax.all_to_all(parts, BAND, 0, 0, tiled=True)  11.4 us
    ppermute x1, waiting for transfers between devices, gather_rotation(): far = lax.ppermute(near[0], ('c', 'x'), line)  8.47 us
    pallas_call x2, Pallas kernels, stencil(): pl.pallas_call(lambda *refs: stencil_kernel(combine, *refs), out_shape=pl...  4.71 us
    ppermute x1, starting transfers between devices, gather_rotation(): far = lax.ppermute(near[0], ('c', 'x'), line)  3.83 us
  transfers between devices with their start and end apart: 10, of which 5 were waited for; matrix products, arithmetic and copies ran while one was open for 1% of the time, Pallas kernels for 3%

profile of v2, /device:TPU:8, one launch (start us, length us, event | category | flops | bytes accessed | tf_op | source)
XLA Modules:
  0.0 164.3 jit_solution(4740876396057630754)
XLA Ops:
  0.0 0.0 copy-start
  0.0 0.9 copy-done
  1.0 12.8 %all_to_all.20 = f32[4,8,512]{2,1,0:T(8,128)S(1)} all-to-all(f32[4,8,512]{2,1,0:T(8,128)S(1)} %broadcast_in_dim.4), channel_id=1, replica_groups=mesh['y'=8,'zh'=3,'c'=2,'x'=4,'zl'=4] {'zl'}, dimensions={0} | all-to-all | bytes 131072 | tf_op jit(solution)/shard_map/all_to_all | solution.py:122
  13.8 0.0 copy-start.1
  13.8 22.1 %all_to_all.21 = f32[8,4,8,512]{3,2,1,0:T(8,128)S(1)} all-to-all(f32[8,4,8,512]{3,2,1,0:T(8,128)S(1)} %broadcast_in_dim.5), channel_id=1, replica_groups=mesh['y'=8,'zh'=3,'c'=2,'x'=4,'zl'=4] {'y'}, dimensions={0} | all-to-all | bytes 1048576 | tf_op jit(solution)/shard_map/all_to_all | solution.py:122
  35.9 1.9 %collective-permute-start.4 = (f32[256,512]{1,0:T(8,128)S(1)}, f32[256,512]{1,0:T(8,128)S(1)}, u32[]{:S(2)}, u32[]{:S(2)}) collective-permute-start(f32[256,512]{1,0:T(8,128)S(1)} %bitcast.14), channel_id=1, source_target_pairs={{0,16},{16,0},{1,17},{17,1},{2,18},{18,2},{3,19},{19,3},{4,20},{20... | collective-permute-start | bytes 1572872 | tf_op jit(solution)/shard_map/ppermute | solution.py:134
  37.8 0.0 copy-done.1
  37.8 2.4 %collective-permute-start.1 = (f32[64,2,8,128]{3,2,1,0:T(8,128)S(1)}, f32[64,2,8,128]{3,2,1,0:T(8,128)S(1)}, u32[]{:S(2)}, u32[]{:S(2)}) collective-permute-start(f32[64,2,8,128]{3,2,1,0:T(8,128)S(1)} %copy-done.1), channel_id=1, source_target_pairs={{0,16},{16,0},{32,48},{48,32},{64,80},{80,64},{96,112},{112,96},{1... | collective-permute-start | bytes 1572872 | tf_op jit(solution)/shard_map/ppermute | solution.py:143
  40.3 12.4 %collective-permute-start = (f32[64,2,8,128]{3,2,1,0:T(8,128)S(1)}, f32[64,2,8,128]{3,2,1,0:T(8,128)}, u32[]{:S(2)}, u32[]{:S(2)}) collective-permute-start(f32[64,2,8,128]{3,2,1,0:T(8,128)S(1)} %copy-done.1), channel_id=1, source_target_pairs={{0,752},{16,32},{32,16},{48,64},{64,48},{80,96},{96,80},{112,128},... | collective-permute-start | bytes 1572872 | tf_op jit(solution)/shard_map/ppermute | solution.py:143
  52.6 0.0 collective-permute-done.4.refs_3_
  52.7 1.0 pad_maximum_fusion
  53.7 0.0 copy-start.2
  53.7 3.5 %collective-permute-start.5 = (f32[2,256,512]{2,1,0:T(8,128)}, f32[2,256,512]{2,1,0:T(8,128)S(1)}, u32[]{:S(2)}, u32[]{:S(2)}) collective-permute-start(f32[2,256,512]{2,1,0:T(8,128)} %pad_maximum_fusion), channel_id=1, source_target_pairs={{0,4},{16,28},{4,8},{20,16},{8,12},{24,20},{12,0},{28,24},{1,5},{1... | collective-permute-start | bytes 3145736 | tf_op jit(solution)/shard_map/ppermute | solution.py:135
  57.2 0.1 pad_add_fusion.refs_0_
  57.3 0.0 collective-permute-done.1.refs_3_
  57.3 16.9 %collective-permute-done.refs_2_ = f32[64,2,8,128]{3,2,1,0:T(8,128)} collective-permute-done((f32[64,2,8,128]{3,2,1,0:T(8,128)S(1)}, f32[64,2,8,128]{3,2,1,0:T(8,128)}, u32[]{:S(2)}, u32[]{:S(2)}) %collective-permute-start) | collective-permute-done | bytes 524320 | tf_op jit(solution)/shard_map/ppermute | solution.py:143
  74.2 0.0 copy-done.2
  74.2 2.2 %stencil.2.refs_1_ = f32[64,2,8,128]{3,2,1,0:T(8,128)S(1)} custom-call(s32[2]{0:T(128)S(1)} %pad_add_fusion.refs_0_, f32[64,2,8,128]{3,2,1,0:T(8,128)S(1)} %copy-done.1, f32[64,2,8,128]{3,2,1,0:T(8,128)} %collective-permute-done.refs_2_, f32[64,2,8,128]{3,2,1,0:T(8,128)S(1)} %collective-permute-done.1.refs_3_, f32[2,8,128]{2,1,0:T(8,128)S(1)} %copy-done.2), custom_call_target="tpu_custom_call" | custom-call | tf_op jit(solution)/shard_map/stencil/pallas_call | solution.py:63
  76.4 2.8 %collective-permute-start.3 = (f32[64,2,8,128]{3,2,1,0:T(8,128)S(1)}, f32[64,2,8,128]{3,2,1,0:T(8,128)S(1)}, u32[]{:S(2)}, u32[]{:S(2)}) collective-permute-start(f32[64,2,8,128]{3,2,1,0:T(8,128)S(1)} %stencil.2.refs_1_), channel_id=1, source_target_pairs={{0,16},{16,0},{32,48},{48,32},{64,80},{80,64},{96,112},{112,96},{1... | collective-permute-start | bytes 1572872 | tf_op jit(solution)/shard_map/ppermute | solution.py:143
  79.2 7.9 %collective-permute-start.2 = (f32[64,2,8,128]{3,2,1,0:T(8,128)S(1)}, f32[64,2,8,128]{3,2,1,0:T(8,128)S(1)}, u32[]{:S(2)}, u32[]{:S(2)}) collective-permute-start(f32[64,2,8,128]{3,2,1,0:T(8,128)S(1)} %stencil.2.refs_1_), channel_id=1, source_target_pairs={{0,752},{16,32},{32,16},{48,64},{64,48},{80,96},{96,80},{112,128},... | collective-permute-start | bytes 1572872 | tf_op jit(solution)/shard_map/ppermute | solution.py:143
  87.0 0.0 collective-permute-done.3.refs_3_
  87.0 17.4 %collective-permute-done.2.refs_2_ = f32[64,2,8,128]{3,2,1,0:T(8,128)S(1)} collective-permute-done((f32[64,2,8,128]{3,2,1,0:T(8,128)S(1)}, f32[64,2,8,128]{3,2,1,0:T(8,128)S(1)}, u32[]{:S(2)}, u32[]{:S(2)}) %collective-permute-start.2) | collective-permute-done | bytes 524320 | tf_op jit(solution)/shard_map/ppermute | solution.py:143
  104.5 2.5 %stencil.3 = f32[2,8,64,128]{3,2,1,0:T(8,128)} custom-call(s32[2]{0:T(128)S(1)} %pad_add_fusion.refs_0_, f32[64,2,8,128]{3,2,1,0:T(8,128)S(1)} %stencil.2.refs_1_, f32[64,2,8,128]{3,2,1,0:T(8,128)S(1)} %collective-permute-done.2.refs_2_, f32[64,2,8,128]{3,2,1,0:T(8,128)S(1)} %collective-permute-done.3.refs_3_, f32[2,8,128]{2,1,0:T(8,128)S(1)} %copy-done.2, ...), custom_call_target="tpu_custom_call" | custom-call | tf_op jit(solution)/shard_map/stencil/pallas_call | solution.py:63
  107.0 11.4 %all-to-all-start = ((f32[16,64,128]{2,1,0:T(8,128)}), f32[16,64,128]{2,1,0:T(8,128)S(1)}, u32[]{:S(2)}, u32[]{:S(2)}) async-start(f32[16,64,128]{2,1,0:T(8,128)} %bitcast.2), calls=%async_computation | async-start | bytes 1048576 | tf_op jit(solution)/shard_map/all_to_all | solution.py:163
  118.4 0.0 collective-permute-done.5.refs_4_
  118.5 3.8 %collective-permute-start.7 = (f32[256,512]{1,0:T(8,128)S(1)}, f32[256,512]{1,0:T(8,128)S(1)}, u32[]{:S(2)}, u32[]{:S(2)}) collective-permute-start(f32[256,512]{1,0:T(8,128)S(1)} %slice_bitcast_fusion), channel_id=1, source_target_pairs={{0,4},{16,28},{4,8},{20,16},{8,12},{24,20},{12,0},{28,24},{1,5},{1... | collective-permute-start | bytes 1572872 | tf_op jit(solution)/shard_map/ppermute | solution.py:136
  122.3 2.6 %collective-permute-start.6 = (f32[2,256,512]{2,1,0:T(8,128)S(1)}, f32[2,256,512]{2,1,0:T(8,128)}, u32[]{:S(2)}, u32[]{:S(2)}) collective-permute-start(f32[2,256,512]{2,1,0:T(8,128)S(1)} %collective-permute-done.5.refs_4_), channel_id=1, source_target_pairs={{0,16},{16,0},{1,17},{17,1},{2,18},{18,2},{3,19},{19,3},{4,20},{20... | collective-permute-start | bytes 3145736 | tf_op jit(solution)/shard_map/ppermute | solution.py:137
  125.0 8.5 %collective-permute-done.7.refs_6_ = f32[256,512]{1,0:T(8,128)S(1)} collective-permute-done((f32[256,512]{1,0:T(8,128)S(1)}, f32[256,512]{1,0:T(8,128)S(1)}, u32[]{:S(2)}, u32[]{:S(2)}) %collective-permute-start.7) | collective-permute-done | bytes 524320 | tf_op jit(solution)/shard_map/ppermute | solution.py:136
  133.4 1.9 %collective-permute-start.8 = (f32[256,512]{1,0:T(8,128)S(1)}, f32[256,512]{1,0:T(8,128)}, u32[]{:S(2)}, u32[]{:S(2)}) collective-permute-start(f32[256,512]{1,0:T(8,128)S(1)} %collective-permute-done.7.refs_6_), channel_id=1, source_target_pairs={{0,16},{16,0},{1,17},{17,1},{2,18},{18,2},{3,19},{19,3},{4,20},{20... | collective-permute-start | bytes 1572872 | tf_op jit(solution)/shard_map/ppermute | solution.py:138
  135.4 0.1 all-to-all-done
  135.4 1.9 %collective-permute-done.8.refs_7_ = f32[256,512]{1,0:T(8,128)} collective-permute-done((f32[256,512]{1,0:T(8,128)S(1)}, f32[256,512]{1,0:T(8,128)}, u32[]{:S(2)}, u32[]{:S(2)}) %collective-permute-start.8) | collective-permute-done | bytes 524320 | tf_op jit(solution)/shard_map/ppermute | solution.py:138
  137.4 0.0 collective-permute-done.6.refs_5_
  137.4 2.8 %rotate.1 = f32[16,64,128]{2,1,0:T(8,128)S(1)} custom-call(s32[2]{0:T(128)S(1)} %pad_add_fusion.refs_0_, f32[1024,128]{1,0:T(8,128)S(1)} %bitcast.17, f32[256,512]{1,0:T(8,128)S(1)} %bitcast.16, f32[256,512]{1,0:T(8,128)S(1)} %collective-permute-done.4.refs_3_, f32[2,256,512]{2,1,0:T(8,128)S(1)} %collective-permute-done.5.refs_4_, ...), custom_call_target="tpu_custom_call" | custom-call | tf_op jit(solution)/shard_map/rotate/pallas_call | solution.py:108
  140.1 23.1 %all_to_all.22 = f32[16,64,128]{2,1,0:T(8,128)S(1)} all-to-all(f32[16,64,128]{2,1,0:T(8,128)S(1)} %rotate.1), channel_id=1, replica_groups=mesh['y'=8,'zh'=3,'c'=2,'x'=4,'zl'=4] {'x','zl'}, dimensions={0} | all-to-all | bytes 1048576 | tf_op jit(solution)/shard_map/all_to_all | solution.py:166
  163.2 1.1 copy.4
  (4 shorter events, 0.1 us)
Async XLA Ops:
  0.0 1.0 copy-start
  13.8 24.0 %copy-start.1 = (f32[64,2,8,128]{3,2,1,0:T(8,128)S(1)}, f32[64,2,8,128]{3,2,1,0:T(8,128)}, u32[]{:S(2)}) copy-start(f32[64,2,8,128]{3,2,1,0:T(8,128)} %refs_5_.1) | copy-start | bytes 1572868
  35.9 16.7 %collective-permute-start.4 = (f32[256,512]{1,0:T(8,128)S(1)}, f32[256,512]{1,0:T(8,128)S(1)}, u32[]{:S(2)}, u32[]{:S(2)}) collective-permute-start(f32[256,512]{1,0:T(8,128)S(1)} %bitcast.14), channel_id=1, source_target_pairs={{0,16},{16,0},{1,17},{17,1},{2,18},{18,2},{3,19},{19,3},{4,20},{20... | collective-permute-start | bytes 1572872 | tf_op jit(solution)/shard_map/ppermute | solution.py:134
  37.8 19.5 %collective-permute-start.1 = (f32[64,2,8,128]{3,2,1,0:T(8,128)S(1)}, f32[64,2,8,128]{3,2,1,0:T(8,128)S(1)}, u32[]{:S(2)}, u32[]{:S(2)}) collective-permute-start(f32[64,2,8,128]{3,2,1,0:T(8,128)S(1)} %copy-done.1), channel_id=1, source_target_pairs={{0,16},{16,0},{32,48},{48,32},{64,80},{80,64},{96,112},{112,96},{1... | collective-permute-start | bytes 1572872 | tf_op jit(solution)/shard_map/ppermute | solution.py:143
  40.3 33.9 %collective-permute-start = (f32[64,2,8,128]{3,2,1,0:T(8,128)S(1)}, f32[64,2,8,128]{3,2,1,0:T(8,128)}, u32[]{:S(2)}, u32[]{:S(2)}) collective-permute-start(f32[64,2,8,128]{3,2,1,0:T(8,128)S(1)} %copy-done.1), channel_id=1, source_target_pairs={{0,752},{16,32},{32,16},{48,64},{64,48},{80,96},{96,80},{112,128},... | collective-permute-start | bytes 1572872 | tf_op jit(solution)/shard_map/ppermute | solution.py:143
  53.7 20.5 %copy-start.2 = (f32[2,8,128]{2,1,0:T(8,128)S(1)}, f32[2,8,128]{2,1,0:T(8,128)}, u32[]{:S(2)}) copy-start(f32[2,8,128]{2,1,0:T(8,128)} %refs_4_.3) | copy-start | bytes 24580
  53.7 64.7 %collective-permute-start.5 = (f32[2,256,512]{2,1,0:T(8,128)}, f32[2,256,512]{2,1,0:T(8,128)S(1)}, u32[]{:S(2)}, u32[]{:S(2)}) collective-permute-start(f32[2,256,512]{2,1,0:T(8,128)} %pad_maximum_fusion), channel_id=1, source_target_pairs={{0,4},{16,28},{4,8},{20,16},{8,12},{24,20},{12,0},{28,24},{1,5},{1... | collective-permute-start | bytes 3145736 | tf_op jit(solution)/shard_map/ppermute | solution.py:135
  76.4 10.7 %collective-permute-start.3 = (f32[64,2,8,128]{3,2,1,0:T(8,128)S(1)}, f32[64,2,8,128]{3,2,1,0:T(8,128)S(1)}, u32[]{:S(2)}, u32[]{:S(2)}) collective-permute-start(f32[64,2,8,128]{3,2,1,0:T(8,128)S(1)} %stencil.2.refs_1_), channel_id=1, source_target_pairs={{0,16},{16,0},{32,48},{48,32},{64,80},{80,64},{96,112},{112,96},{1... | collective-permute-start | bytes 1572872 | tf_op jit(solution)/shard_map/ppermute | solution.py:143
  79.2 25.3 %collective-permute-start.2 = (f32[64,2,8,128]{3,2,1,0:T(8,128)S(1)}, f32[64,2,8,128]{3,2,1,0:T(8,128)S(1)}, u32[]{:S(2)}, u32[]{:S(2)}) collective-permute-start(f32[64,2,8,128]{3,2,1,0:T(8,128)S(1)} %stencil.2.refs_1_), channel_id=1, source_target_pairs={{0,752},{16,32},{32,16},{48,64},{64,48},{80,96},{96,80},{112,128},... | collective-permute-start | bytes 1572872 | tf_op jit(solution)/shard_map/ppermute | solution.py:143
  107.0 28.4 %all-to-all-start = ((f32[16,64,128]{2,1,0:T(8,128)}), f32[16,64,128]{2,1,0:T(8,128)S(1)}, u32[]{:S(2)}, u32[]{:S(2)}) async-start(f32[16,64,128]{2,1,0:T(8,128)} %bitcast.2), calls=%async_computation | async-start | bytes 1048576 | tf_op jit(solution)/shard_map/all_to_all | solution.py:163
  118.5 14.9 %collective-permute-start.7 = (f32[256,512]{1,0:T(8,128)S(1)}, f32[256,512]{1,0:T(8,128)S(1)}, u32[]{:S(2)}, u32[]{:S(2)}) collective-permute-start(f32[256,512]{1,0:T(8,128)S(1)} %slice_bitcast_fusion), channel_id=1, source_target_pairs={{0,4},{16,28},{4,8},{20,16},{8,12},{24,20},{12,0},{28,24},{1,5},{1... | collective-permute-start | bytes 1572872 | tf_op jit(solution)/shard_map/ppermute | solution.py:136
  122.3 15.0 %collective-permute-start.6 = (f32[2,256,512]{2,1,0:T(8,128)S(1)}, f32[2,256,512]{2,1,0:T(8,128)}, u32[]{:S(2)}, u32[]{:S(2)}) collective-permute-start(f32[2,256,512]{2,1,0:T(8,128)S(1)} %collective-permute-done.5.refs_4_), channel_id=1, source_target_pairs={{0,16},{16,0},{1,17},{17,1},{2,18},{18,2},{3,19},{19,3},{4,20},{20... | collective-permute-start | bytes 3145736 | tf_op jit(solution)/shard_map/ppermute | solution.py:137
  133.4 3.9 %collective-permute-start.8 = (f32[256,512]{1,0:T(8,128)S(1)}, f32[256,512]{1,0:T(8,128)}, u32[]{:S(2)}, u32[]{:S(2)}) collective-permute-start(f32[256,512]{1,0:T(8,128)S(1)} %collective-permute-done.7.refs_6_), channel_id=1, source_target_pairs={{0,16},{16,0},{1,17},{17,1},{2,18},{18,2},{3,19},{19,3},{4,20},{20... | collective-permute-start | bytes 1572872 | tf_op jit(solution)/shard_map/ppermute | solution.py:138

commit v3 on v2

--- a/solution.py
+++ b/solution.py
@@ -71,9 +71,9 @@
     )(par, *map(in_vmem, args))
 
 
-def rotate_kernel(nx, ny, nzl, at_ref, v, own, own2, near, near2, far, far2, out, wide):
-    core, x = at_ref[0], at_ref[1]
-    half = own.shape[1]
+def rotate_kernel(nx, at_ref, v, own, own2, near, near2, far, far2, out, wide):
+    core, x, odd = at_ref[0], at_ref[1], at_ref[2]
+    _, nzl, rows, half = own.shape
     value = v[...]
     high = value.astype(jnp.bfloat16)
     low = (value - high.astype(jnp.float32)).astype(jnp.bfloat16)
@@ -89,24 +89,23 @@
         return both[:, :nz] + both[:, nz:] + rest
 
     def slab(first, second, first_half, slab_x):
-        total = product(first, first_half) + product(second, 1 - first_half)
-        rows = total.shape[0] // (ny * nzl)
-        for y in range(ny):
+        for pair in (0, 1):
+            total = product(first[pair].reshape(nzl * rows, half), first_half)
+            total += product(second[pair].reshape(nzl * rows, half), 1 - first_half)
+            place = pl.ds(pl.multiple_of((odd ^ pair) * rows, rows), rows)
             for z in range(nzl):
-                at = (y * nzl + z) * rows
-                out[slab_x * nzl + z, pl.ds(y * rows, rows)] = total[at : at + rows]
+                out[slab_x * nzl + z, place] = total[z * rows : (z + 1) * rows]
 
     step = 1 - 2 * core
-    slab(own[...], own2[...], core, x)
-    slab(near[0], near[1], core, lax.rem(x - step + nx, nx))
-    slab(near2[0], near2[1], 1 - core, lax.rem(x + step + nx, nx))
-    slab(far[...], far2[...], core, lax.rem(x + 2, nx))
+    slab(own, own2, core, x)
+    slab(near.at[0], near.at[1], core, lax.rem(x - step + nx, nx))
+    slab(near2.at[0], near2.at[1], 1 - core, lax.rem(x + step + nx, nx))
+    slab(far, far2, core, lax.rem(x + 2, nx))
 
 
-def rotate(sizes, at, v, pieces, shape):
-    nx, ny, nzl = sizes
+def rotate(nx, at, v, pieces, shape):
     return pl.pallas_call(
-        lambda *refs: rotate_kernel(nx, ny, nzl, *refs),
+        lambda *refs: rotate_kernel(nx, *refs),
         out_shape=pltpu.VMEM(shape, v.dtype),
         in_specs=[pl.BlockSpec(memory_space=pltpu.SMEM)]
         + [pl.BlockSpec(memory_space=pltpu.VMEM)] * (1 + len(pieces)),
@@ -124,13 +123,14 @@
 
 def gather_rotation(rot_t):
     nx, ny = lax.axis_size("x"), lax.axis_size("y")
-    rows, cols = rot_t.shape[0] // ny, rot_t.shape[1] // 2
+    rows, cols = rot_t.shape[0] // 2, rot_t.shape[1] // 2
     y, core = lax.axis_index("y"), lax.axis_index("c")
-    part = lax.dynamic_slice(rot_t, (y * rows, core * cols), (rows, cols))
+    part = lax.dynamic_slice(rot_t, ((y % 2) * rows, core * cols), (rows, cols))
     part = to_all(part, "zl")
-    own = to_all(part, "y").reshape(-1, cols)
+    pair = lax.ppermute(part, "y", [(i, i ^ 1) for i in range(ny)])
     flip = [(0, 1), (1, 0)]
     line = [(c * nx + i, c * nx + (i + 1 - 2 * c) % nx) for i in range(nx) for c in (0, 1)]
+    own = jnp.stack([part, pair])
     own2 = lax.ppermute(own, "c", flip)
     near = lax.ppermute(jnp.stack([own, own2]), ("c", "x"), line)
     far = lax.ppermute(near[0], ("c", "x"), line)
@@ -147,8 +147,8 @@
     devices = lax.axis_size(GRID)
     outer_pairs = [(i, (i + 1 if i % 2 else i - 1) % devices) for i in range(devices)]
     inner_pairs = [(i, i ^ 1) for i in range(devices)]
-    core = lax.axis_index("c").astype(jnp.int32)
-    at = jnp.stack([core, lax.axis_index("x").astype(jnp.int32)])
+    core = lax.axis_index("c")
+    at = jnp.stack([core, lax.axis_index("x"), lax.axis_index("y") % 2]).astype(jnp.int32)
     pieces = gather_rotation(rotation.T)
 
     outer = swap(orbitals, outer_pairs)
@@ -161,8 +161,7 @@
     groups = lax.axis_size(BAND)
     parts = filtered.reshape(groups, -1, nz)
     parts = lax.all_to_all(parts, BAND, 0, 0, tiled=True)
-    sizes = lax.axis_size("x"), lax.axis_size("y"), lax.axis_size("zl")
-    mixed = rotate(sizes, at, parts.reshape(groups * orbs, nz), pieces, (groups, orbs, nz))
+    mixed = rotate(lax.axis_size("x"), at, parts.reshape(groups * orbs, nz), pieces, (groups, orbs, nz))
     back = lax.all_to_all(mixed, BAND, 0, 0, tiled=True)
     return back.transpose(1, 0, 2).reshape(orbs, planes, ny, nz)
 

time: 165 us -> 154 us (0.933)
  the two profiles are of different devices: /device:TPU:8 before, /device:TPU:1 now
where the time goes in v3:
time: 154 us; the launch traced here: 152 us
  starting transfers between devices  58.6 us (38%)
  waiting for transfers between devices  47.6 us (31%)
  blocking collectives  34.3 us (22%)
  Pallas kernels  7.47 us (5%)
  local copies, waits for them, and re-layouts  2.12 us (1%)
    ppermute x4, waiting for transfers between devices, swap(): return lax.ppermute(value, GRID, pairs)  35.8 us
    all_to_all x1, blocking collectives, per_device(): back = lax.all_to_all(mixed, BAND, 0, 0, tiled=True)  20.7 us
    ppermute x4, starting transfers between devices, swap(): return lax.ppermute(value, GRID, pairs)  19.2 us
    all_to_all x1, blocking collectives, to_all(): return lax.all_to_all(copies, axis, 0, 0, tiled=True)  13.6 us
    all_to_all x1, starting transfers between devices, per_device(): parts = lax.all_to_all(parts, BAND, 0, 0, tiled=True)  9.8 us
    ppermute x1, starting transfers between devices, gather_rotation(): own2 = lax.ppermute(own, 'c', flip)  8.91 us
    ppermute x1, waiting for transfers between devices, gather_rotation(): far = lax.ppermute(near[0], ('c', 'x'), line)  6.48 us
    pallas_call x2, Pallas kernels, stencil(): pl.pallas_call(lambda *refs: stencil_kernel(combine, *refs), out_shape=pl...  4.71 us
  transfers between devices with their start and end apart: 11, of which 5 were waited for; matrix products, arithmetic and copies ran while one was open for 1% of the time, Pallas kernels for 3%

profile of v3, /device:TPU:1, one launch (start us, length us, event | category | flops | bytes accessed | tf_op | source)
XLA Modules:
  0.0 151.5 jit_solution(18325432243773818483)
XLA Ops:
  0.0 0.0 copy-start
  0.0 0.9 copy-done
  1.0 13.6 %all_to_all.15 = f32[4,32,512]{2,1,0:T(8,128)S(1)} all-to-all(f32[4,32,512]{2,1,0:T(8,128)S(1)} %broadcast_in_dim.2), channel_id=1, replica_groups=mesh['y'=8,'zh'=3,'c'=2,'x'=4,'zl'=4] {'zl'}, dimensions={0} | all-to-all | bytes 524288 | tf_op jit(solution)/shard_map/all_to_all | solution.py:121
  14.6 4.0 %collective-permute-start.4 = (f32[4,32,512]{2,1,0:T(8,128)S(1)}, f32[4,32,512]{2,1,0:T(8,128)S(1)}, u32[]{:S(2)}, u32[]{:S(2)}) collective-permute-start(f32[4,32,512]{2,1,0:T(8,128)S(1)} %all_to_all.15), channel_id=1, source_target_pairs={{0,96},{96,0},{192,288},{288,192},{384,480},{480,384},{576,672},{6... | collective-permute-start | bytes 786440 | tf_op jit(solution)/shard_map/ppermute | solution.py:130
  18.6 3.7 %collective-permute-done.4 = f32[4,32,512]{2,1,0:T(8,128)S(1)} collective-permute-done((f32[4,32,512]{2,1,0:T(8,128)S(1)}, f32[4,32,512]{2,1,0:T(8,128)S(1)}, u32[]{:S(2)}, u32[]{:S(2)}) %collective-permute-start.4) | collective-permute-done | bytes 262176 | tf_op jit(solution)/shard_map/ppermute | solution.py:130
  22.4 0.0 copy-start.1
  22.4 0.1 fusion
  22.5 8.9 %collective-permute-start.5 = (f32[2,4,32,512]{3,2,1,0:T(8,128)S(1)}, f32[2,4,32,512]{3,2,1,0:T(8,128)S(1)}, u32[]{:S(2)}, u32[]{:S(2)}) collective-permute-start(f32[2,4,32,512]{3,2,1,0:T(8,128)S(1)} %get-tuple-element.6.refs_2_), channel_id=1, source_target_pairs={{0,16},{16,0},{1,17},{17,1},{2,18},{18,2},{3,19},{19,3},{4,20},{20... | collective-permute-start | bytes 1572872 | tf_op jit(solution)/shard_map/ppermute | solution.py:134
  31.4 0.0 copy-done.1
  31.4 1.9 %collective-permute-start.1 = (f32[64,2,8,128]{3,2,1,0:T(8,128)S(1)}, f32[64,2,8,128]{3,2,1,0:T(8,128)S(1)}, u32[]{:S(2)}, u32[]{:S(2)}) collective-permute-start(f32[64,2,8,128]{3,2,1,0:T(8,128)S(1)} %copy-done.1), channel_id=1, source_target_pairs={{0,16},{16,0},{32,48},{48,32},{64,80},{80,64},{96,112},{112,96},{1... | collective-permute-start | bytes 1572872 | tf_op jit(solution)/shard_map/ppermute | solution.py:143
  33.3 8.2 %collective-permute-start = (f32[64,2,8,128]{3,2,1,0:T(8,128)S(1)}, f32[64,2,8,128]{3,2,1,0:T(8,128)}, u32[]{:S(2)}, u32[]{:S(2)}) collective-permute-start(f32[64,2,8,128]{3,2,1,0:T(8,128)S(1)} %copy-done.1), channel_id=1, source_target_pairs={{0,752},{16,32},{32,16},{48,64},{64,48},{80,96},{96,80},{112,128},... | collective-permute-start | bytes 1572872 | tf_op jit(solution)/shard_map/ppermute | solution.py:143
  41.5 0.0 collective-permute-done.5.refs_3_
  41.5 1.1 pad_maximum_fusion
  42.6 0.0 copy-start.2
  42.6 4.5 %collective-permute-start.6 = (f32[2,2,4,32,512]{4,3,2,1,0:T(8,128)}, f32[2,2,4,32,512]{4,3,2,1,0:T(8,128)S(1)}, u32[]{:S(2)}, u32[]{:S(2)}) collective-permute-start(f32[2,2,4,32,512]{4,3,2,1,0:T(8,128)} %pad_maximum_fusion), channel_id=1, source_target_pairs={{0,4},{16,28},{4,8},{20,16},{8,12},{24,20},{12,0},{28,24},{1,5},{1... | collective-permute-start | bytes 3145736 | tf_op jit(solution)/shard_map/ppermute | solution.py:135
  47.1 0.1 pad_add_fusion.refs_0_
  47.2 0.0 collective-permute-done.1.refs_3_
  47.2 18.3 %collective-permute-done.refs_2_ = f32[64,2,8,128]{3,2,1,0:T(8,128)} collective-permute-done((f32[64,2,8,128]{3,2,1,0:T(8,128)S(1)}, f32[64,2,8,128]{3,2,1,0:T(8,128)}, u32[]{:S(2)}, u32[]{:S(2)}) %collective-permute-start) | collective-permute-done | bytes 524320 | tf_op jit(solution)/shard_map/ppermute | solution.py:143
  65.5 0.0 copy-done.2
  65.5 2.2 %stencil.2.refs_1_ = f32[64,2,8,128]{3,2,1,0:T(8,128)S(1)} custom-call(s32[3]{0:T(128)S(1)} %pad_add_fusion.refs_0_, f32[64,2,8,128]{3,2,1,0:T(8,128)S(1)} %copy-done.1, f32[64,2,8,128]{3,2,1,0:T(8,128)} %collective-permute-done.refs_2_, f32[64,2,8,128]{3,2,1,0:T(8,128)S(1)} %collective-permute-done.1.refs_3_, f32[2,8,128]{2,1,0:T(8,128)S(1)} %copy-done.2), custom_call_target="tpu_custom_call" | custom-call | tf_op jit(solution)/shard_map/stencil/pallas_call | solution.py:63
  67.6 1.9 %collective-permute-start.3 = (f32[64,2,8,128]{3,2,1,0:T(8,128)S(1)}, f32[64,2,8,128]{3,2,1,0:T(8,128)S(1)}, u32[]{:S(2)}, u32[]{:S(2)}) collective-permute-start(f32[64,2,8,128]{3,2,1,0:T(8,128)S(1)} %stencil.2.refs_1_), channel_id=1, source_target_pairs={{0,16},{16,0},{32,48},{48,32},{64,80},{80,64},{96,112},{112,96},{1... | collective-permute-start | bytes 1572872 | tf_op jit(solution)/shard_map/ppermute | solution.py:143
  69.6 7.2 %collective-permute-start.2 = (f32[64,2,8,128]{3,2,1,0:T(8,128)S(1)}, f32[64,2,8,128]{3,2,1,0:T(8,128)S(1)}, u32[]{:S(2)}, u32[]{:S(2)}) collective-permute-start(f32[64,2,8,128]{3,2,1,0:T(8,128)S(1)} %stencil.2.refs_1_), channel_id=1, source_target_pairs={{0,752},{16,32},{32,16},{48,64},{64,48},{80,96},{96,80},{112,128},... | collective-permute-start | bytes 1572872 | tf_op jit(solution)/shard_map/ppermute | solution.py:143
  76.8 0.0 collective-permute-done.3.refs_3_
  76.8 17.5 %collective-permute-done.2.refs_2_ = f32[64,2,8,128]{3,2,1,0:T(8,128)S(1)} collective-permute-done((f32[64,2,8,128]{3,2,1,0:T(8,128)S(1)}, f32[64,2,8,128]{3,2,1,0:T(8,128)S(1)}, u32[]{:S(2)}, u32[]{:S(2)}) %collective-permute-start.2) | collective-permute-done | bytes 524320 | tf_op jit(solution)/shard_map/ppermute | solution.py:143
  94.3 2.5 %stencil.3 = f32[2,8,64,128]{3,2,1,0:T(8,128)} custom-call(s32[3]{0:T(128)S(1)} %pad_add_fusion.refs_0_, f32[64,2,8,128]{3,2,1,0:T(8,128)S(1)} %stencil.2.refs_1_, f32[64,2,8,128]{3,2,1,0:T(8,128)S(1)} %collective-permute-done.2.refs_2_, f32[64,2,8,128]{3,2,1,0:T(8,128)S(1)} %collective-permute-done.3.refs_3_, f32[2,8,128]{2,1,0:T(8,128)S(1)} %copy-done.2, ...), custom_call_target="tpu_custom_call" | custom-call | tf_op jit(solution)/shard_map/stencil/pallas_call | solution.py:63
  96.8 9.8 %all-to-all-start = ((f32[16,64,128]{2,1,0:T(8,128)}), f32[16,64,128]{2,1,0:T(8,128)S(1)}, u32[]{:S(2)}, u32[]{:S(2)}) async-start(f32[16,64,128]{2,1,0:T(8,128)} %bitcast.3), calls=%async_computation | async-start | bytes 1048576 | tf_op jit(solution)/shard_map/all_to_all | solution.py:163
  106.6 0.0 collective-permute-done.6.refs_4_
  106.7 4.5 %collective-permute-start.8 = (f32[2,4,32,512]{3,2,1,0:T(8,128)S(1)}, f32[2,4,32,512]{3,2,1,0:T(8,128)S(1)}, u32[]{:S(2)}, u32[]{:S(2)}) collective-permute-start(f32[2,4,32,512]{3,2,1,0:T(8,128)S(1)} %slice_bitcast_fusion), channel_id=1, source_target_pairs={{0,4},{16,28},{4,8},{20,16},{8,12},{24,20},{12,0},{28,24},{1,5},{1... | collective-permute-start | bytes 1572872 | tf_op jit(solution)/shard_map/ppermute | solution.py:136
  111.2 3.6 %collective-permute-start.7 = (f32[2,2,4,32,512]{4,3,2,1,0:T(8,128)S(1)}, f32[2,2,4,32,512]{4,3,2,1,0:T(8,128)}, u32[]{:S(2)}, u32[]{:S(2)}) collective-permute-start(f32[2,2,4,32,512]{4,3,2,1,0:T(8,128)S(1)} %collective-permute-done.6.refs_4_), channel_id=1, source_target_pairs={{0,16},{16,0},{1,17},{17,1},{2,18},{18,2},{3,19},{19,3},{4,20},{20... | collective-permute-start | bytes 3145736 | tf_op jit(solution)/shard_map/ppermute | solution.py:137
  114.8 6.5 %collective-permute-done.8.refs_6_ = f32[2,4,32,512]{3,2,1,0:T(8,128)S(1)} collective-permute-done((f32[2,4,32,512]{3,2,1,0:T(8,128)S(1)}, f32[2,4,32,512]{3,2,1,0:T(8,128)S(1)}, u32[]{:S(2)}, u32[]{:S(2)}) %collective-permute-start.8) | collective-permute-done | bytes 524320 | tf_op jit(solution)/shard_map/ppermute | solution.py:136
  121.2 4.1 %collective-permute-start.9 = (f32[2,4,32,512]{3,2,1,0:T(8,128)S(1)}, f32[2,4,32,512]{3,2,1,0:T(8,128)}, u32[]{:S(2)}, u32[]{:S(2)}) collective-permute-start(f32[2,4,32,512]{3,2,1,0:T(8,128)S(1)} %collective-permute-done.8.refs_6_), channel_id=1, source_target_pairs={{0,16},{16,0},{1,17},{17,1},{2,18},{18,2},{3,19},{19,3},{4,20},{20... | collective-permute-start | bytes 1572872 | tf_op jit(solution)/shard_map/ppermute | solution.py:138
  125.3 0.0 all-to-all-done
  125.3 1.6 %collective-permute-done.9.refs_7_ = f32[2,4,32,512]{3,2,1,0:T(8,128)} collective-permute-done((f32[2,4,32,512]{3,2,1,0:T(8,128)S(1)}, f32[2,4,32,512]{3,2,1,0:T(8,128)}, u32[]{:S(2)}, u32[]{:S(2)}) %collective-permute-start.9) | collective-permute-done | bytes 524320 | tf_op jit(solution)/shard_map/ppermute | solution.py:138
  127.0 0.0 collective-permute-done.7.refs_5_
  127.0 2.8 %rotate.1 = f32[16,64,128]{2,1,0:T(8,128)S(1)} custom-call(s32[3]{0:T(128)S(1)} %pad_add_fusion.refs_0_, f32[1024,128]{1,0:T(8,128)S(1)} %bitcast.17, f32[2,4,32,512]{3,2,1,0:T(8,128)S(1)} %get-tuple-element.6.refs_2_, f32[2,4,32,512]{3,2,1,0:T(8,128)S(1)} %collective-permute-done.5.refs_3_, f32[2,2,4,32,512]{4,3,2,1,0:T(8,128)S(1)} %collective-permute-done.6.refs_4_, ...), custom_call_target="tpu_custom_call" | custom-call | tf_op jit(solution)/shard_map/rotate/pallas_call | solution.py:107
  129.7 20.7 %all_to_all.16 = f32[16,64,128]{2,1,0:T(8,128)S(1)} all-to-all(f32[16,64,128]{2,1,0:T(8,128)S(1)} %rotate.1), channel_id=1, replica_groups=mesh['y'=8,'zh'=3,'c'=2,'x'=4,'zl'=4] {'x','zl'}, dimensions={0} | all-to-all | bytes 1048576 | tf_op jit(solution)/shard_map/all_to_all | solution.py:165
  150.4 1.1 copy.4
  (3 shorter events, 0.1 us)
Async XLA Ops:
  0.0 1.0 copy-start
  14.6 7.8 %collective-permute-start.4 = (f32[4,32,512]{2,1,0:T(8,128)S(1)}, f32[4,32,512]{2,1,0:T(8,128)S(1)}, u32[]{:S(2)}, u32[]{:S(2)}) collective-permute-start(f32[4,32,512]{2,1,0:T(8,128)S(1)} %all_to_all.15), channel_id=1, source_target_pairs={{0,96},{96,0},{192,288},{288,192},{384,480},{480,384},{576,672},{6... | collective-permute-start | bytes 786440 | tf_op jit(solution)/shard_map/ppermute | solution.py:130
  22.4 9.1 %copy-start.1 = (f32[64,2,8,128]{3,2,1,0:T(8,128)S(1)}, f32[64,2,8,128]{3,2,1,0:T(8,128)}, u32[]{:S(2)}) copy-start(f32[64,2,8,128]{3,2,1,0:T(8,128)} %refs_5_.1) | copy-start | bytes 1572868
  22.5 19.0 %collective-permute-start.5 = (f32[2,4,32,512]{3,2,1,0:T(8,128)S(1)}, f32[2,4,32,512]{3,2,1,0:T(8,128)S(1)}, u32[]{:S(2)}, u32[]{:S(2)}) collective-permute-start(f32[2,4,32,512]{3,2,1,0:T(8,128)S(1)} %get-tuple-element.6.refs_2_), channel_id=1, source_target_pairs={{0,16},{16,0},{1,17},{17,1},{2,18},{18,2},{3,19},{19,3},{4,20},{20... | collective-permute-start | bytes 1572872 | tf_op jit(solution)/shard_map/ppermute | solution.py:134
  31.4 15.8 %collective-permute-start.1 = (f32[64,2,8,128]{3,2,1,0:T(8,128)S(1)}, f32[64,2,8,128]{3,2,1,0:T(8,128)S(1)}, u32[]{:S(2)}, u32[]{:S(2)}) collective-permute-start(f32[64,2,8,128]{3,2,1,0:T(8,128)S(1)} %copy-done.1), channel_id=1, source_target_pairs={{0,16},{16,0},{32,48},{48,32},{64,80},{80,64},{96,112},{112,96},{1... | collective-permute-start | bytes 1572872 | tf_op jit(solution)/shard_map/ppermute | solution.py:143
  33.3 32.1 %collective-permute-start = (f32[64,2,8,128]{3,2,1,0:T(8,128)S(1)}, f32[64,2,8,128]{3,2,1,0:T(8,128)}, u32[]{:S(2)}, u32[]{:S(2)}) collective-permute-start(f32[64,2,8,128]{3,2,1,0:T(8,128)S(1)} %copy-done.1), channel_id=1, source_target_pairs={{0,752},{16,32},{32,16},{48,64},{64,48},{80,96},{96,80},{112,128},... | collective-permute-start | bytes 1572872 | tf_op jit(solution)/shard_map/ppermute | solution.py:143
  42.6 22.9 %copy-start.2 = (f32[2,8,128]{2,1,0:T(8,128)S(1)}, f32[2,8,128]{2,1,0:T(8,128)}, u32[]{:S(2)}) copy-start(f32[2,8,128]{2,1,0:T(8,128)} %refs_4_.3) | copy-start | bytes 24580
  42.6 64.0 %collective-permute-start.6 = (f32[2,2,4,32,512]{4,3,2,1,0:T(8,128)}, f32[2,2,4,32,512]{4,3,2,1,0:T(8,128)S(1)}, u32[]{:S(2)}, u32[]{:S(2)}) collective-permute-start(f32[2,2,4,32,512]{4,3,2,1,0:T(8,128)} %pad_maximum_fusion), channel_id=1, source_target_pairs={{0,4},{16,28},{4,8},{20,16},{8,12},{24,20},{12,0},{28,24},{1,5},{1... | collective-permute-start | bytes 3145736 | tf_op jit(solution)/shard_map/ppermute | solution.py:135
  67.6 9.1 %collective-permute-start.3 = (f32[64,2,8,128]{3,2,1,0:T(8,128)S(1)}, f32[64,2,8,128]{3,2,1,0:T(8,128)S(1)}, u32[]{:S(2)}, u32[]{:S(2)}) collective-permute-start(f32[64,2,8,128]{3,2,1,0:T(8,128)S(1)} %stencil.2.refs_1_), channel_id=1, source_target_pairs={{0,16},{16,0},{32,48},{48,32},{64,80},{80,64},{96,112},{112,96},{1... | collective-permute-start | bytes 1572872 | tf_op jit(solution)/shard_map/ppermute | solution.py:143
  69.6 24.7 %collective-permute-start.2 = (f32[64,2,8,128]{3,2,1,0:T(8,128)S(1)}, f32[64,2,8,128]{3,2,1,0:T(8,128)S(1)}, u32[]{:S(2)}, u32[]{:S(2)}) collective-permute-start(f32[64,2,8,128]{3,2,1,0:T(8,128)S(1)} %stencil.2.refs_1_), channel_id=1, source_target_pairs={{0,752},{16,32},{32,16},{48,64},{64,48},{80,96},{96,80},{112,128},... | collective-permute-start | bytes 1572872 | tf_op jit(solution)/shard_map/ppermute | solution.py:143
  96.8 28.5 %all-to-all-start = ((f32[16,64,128]{2,1,0:T(8,128)}), f32[16,64,128]{2,1,0:T(8,128)S(1)}, u32[]{:S(2)}, u32[]{:S(2)}) async-start(f32[16,64,128]{2,1,0:T(8,128)} %bitcast.3), calls=%async_computation | async-start | bytes 1048576 | tf_op jit(solution)/shard_map/all_to_all | solution.py:163
  106.7 14.5 %collective-permute-start.8 = (f32[2,4,32,512]{3,2,1,0:T(8,128)S(1)}, f32[2,4,32,512]{3,2,1,0:T(8,128)S(1)}, u32[]{:S(2)}, u32[]{:S(2)}) collective-permute-start(f32[2,4,32,512]{3,2,1,0:T(8,128)S(1)} %slice_bitcast_fusion), channel_id=1, source_target_pairs={{0,4},{16,28},{4,8},{20,16},{8,12},{24,20},{12,0},{28,24},{1,5},{1... | collective-permute-start | bytes 1572872 | tf_op jit(solution)/shard_map/ppermute | solution.py:136
  111.2 15.8 %collective-permute-start.7 = (f32[2,2,4,32,512]{4,3,2,1,0:T(8,128)S(1)}, f32[2,2,4,32,512]{4,3,2,1,0:T(8,128)}, u32[]{:S(2)}, u32[]{:S(2)}) collective-permute-start(f32[2,2,4,32,512]{4,3,2,1,0:T(8,128)S(1)} %collective-permute-done.6.refs_4_), channel_id=1, source_target_pairs={{0,16},{16,0},{1,17},{17,1},{2,18},{18,2},{3,19},{19,3},{4,20},{20... | collective-permute-start | bytes 3145736 | tf_op jit(solution)/shard_map/ppermute | solution.py:137
  121.2 5.7 %collective-permute-start.9 = (f32[2,4,32,512]{3,2,1,0:T(8,128)S(1)}, f32[2,4,32,512]{3,2,1,0:T(8,128)}, u32[]{:S(2)}, u32[]{:S(2)}) collective-permute-start(f32[2,4,32,512]{3,2,1,0:T(8,128)S(1)} %collective-permute-done.8.refs_6_), channel_id=1, source_target_pairs={{0,16},{16,0},{1,17},{17,1},{2,18},{18,2},{3,19},{19,3},{4,20},{20... | collective-permute-start | bytes 1572872 | tf_op jit(solution)/shard_map/ppermute | solution.py:138

commit v4 on v3

--- a/solution.py
+++ b/solution.py
@@ -7,7 +7,7 @@
 from jax.sharding import Mesh, PartitionSpec as P
 
 GROUP = 8
-GRID = ("y", "zh", "c")
+GRID = ("yh", "yp", "zh", "c")
 BAND = ("x", "zl")
 
 
@@ -27,7 +27,7 @@
 
 
 def stencil_kernel(combine, par_ref, own, outer, inner, pot_ref, *rest):
-    base, out = rest if combine else (None, rest[0])
+    base, out = (rest[0], rest[-1]) if combine else (None, rest[0])
     par = par_ref[0]
     other = 1 - par
     pot_a = ((pot_ref[par] - 3.0) * 0.0625)[None]
@@ -55,10 +55,10 @@
     return pltpu.with_memory_space_constraint(value, pltpu.VMEM)
 
 
-def stencil(par, own, outer, inner, pot, base=None):
+def stencil(par, own, outer, inner, pot, base=None, token=None):
     combine = base is not None
     orbs, planes, ny, nz = own.shape
-    args = (own, outer, inner, pot) + ((base,) if combine else ())
+    args = (own, outer, inner, pot) + ((base, token) if combine else ())
     shape = (planes, ny, orbs, nz) if combine else own.shape
     return pl.pallas_call(
         lambda *refs: stencil_kernel(combine, *refs),
@@ -71,8 +71,8 @@
     )(par, *map(in_vmem, args))
 
 
-def rotate_kernel(nx, at_ref, v, own, own2, near, near2, far, far2, out, wide):
-    core, x, odd = at_ref[0], at_ref[1], at_ref[2]
+def rotate_kernel(nx, at_ref, v, own, near, near2, far, out, wide):
+    core, x = at_ref[0], at_ref[1]
     _, nzl, rows, half = own.shape
     value = v[...]
     high = value.astype(jnp.bfloat16)
@@ -83,24 +83,23 @@
     def product(piece, which):
         high = piece.astype(jnp.bfloat16)
         low = (piece - high.astype(jnp.float32)).astype(jnp.bfloat16)
-        rows = pl.ds(pl.multiple_of(which * half, half), half)
-        both = jnp.dot(high, wide[rows, :], preferred_element_type=jnp.float32)
-        rest = jnp.dot(low, wide[rows, :nz], preferred_element_type=jnp.float32)
+        at = which * half
+        both = jnp.dot(high, wide[at : at + half, :], preferred_element_type=jnp.float32)
+        rest = jnp.dot(low, wide[at : at + half, :nz], preferred_element_type=jnp.float32)
         return both[:, :nz] + both[:, nz:] + rest
 
-    def slab(first, second, first_half, slab_x):
+    def slab(ref, slab_x):
         for pair in (0, 1):
-            total = product(first[pair].reshape(nzl * rows, half), first_half)
-            total += product(second[pair].reshape(nzl * rows, half), 1 - first_half)
-            place = pl.ds(pl.multiple_of((odd ^ pair) * rows, rows), rows)
+            total = product(ref[2 * pair].reshape(nzl * rows, half), 0)
+            total += product(ref[2 * pair + 1].reshape(nzl * rows, half), 1)
             for z in range(nzl):
-                out[slab_x * nzl + z, place] = total[z * rows : (z + 1) * rows]
+                out[slab_x * nzl + z, pair * rows : (pair + 1) * rows] = total[z * rows : (z + 1) * rows]
 
     step = 1 - 2 * core
-    slab(own, own2, core, x)
-    slab(near.at[0], near.at[1], core, lax.rem(x - step + nx, nx))
-    slab(near2.at[0], near2.at[1], 1 - core, lax.rem(x + step + nx, nx))
-    slab(far, far2, core, lax.rem(x + 2, nx))
+    slab(own, x)
+    slab(near, lax.rem(x - step + nx, nx))
+    slab(near2, lax.rem(x + step + nx, nx))
+    slab(far, lax.rem(x + 2, nx))
 
 
 def rotate(nx, at, v, pieces, shape):
@@ -122,21 +121,17 @@
 
 
 def gather_rotation(rot_t):
-    nx, ny = lax.axis_size("x"), lax.axis_size("y")
+    nx = lax.axis_size("x")
     rows, cols = rot_t.shape[0] // 2, rot_t.shape[1] // 2
-    y, core = lax.axis_index("y"), lax.axis_index("c")
-    part = lax.dynamic_slice(rot_t, ((y % 2) * rows, core * cols), (rows, cols))
-    part = to_all(part, "zl")
-    pair = lax.ppermute(part, "y", [(i, i ^ 1) for i in range(ny)])
-    flip = [(0, 1), (1, 0)]
+    at = (lax.axis_index("yp") * rows, lax.axis_index("c") * cols)
+    part = to_all(lax.dynamic_slice(rot_t, at, (rows, cols)), "zl")
+    own = to_all(part, ("yp", "c"))
     line = [(c * nx + i, c * nx + (i + 1 - 2 * c) % nx) for i in range(nx) for c in (0, 1)]
-    own = jnp.stack([part, pair])
-    own2 = lax.ppermute(own, "c", flip)
-    near = lax.ppermute(jnp.stack([own, own2]), ("c", "x"), line)
-    far = lax.ppermute(near[0], ("c", "x"), line)
-    near2 = lax.ppermute(near, "c", flip)
-    far2 = lax.ppermute(far, "c", flip)
-    return own, own2, near, near2, far, far2
+    near = lax.ppermute(own, ("c", "x"), line)
+    far = lax.ppermute(near, ("c", "x"), line)
+    near2 = lax.ppermute(near, "c", [(0, 1), (1, 0)])
+    token = near[0, 0, :8, :128] * 2.0
+    return (own, near, near2, far), token
 
 
 def swap(value, pairs):
@@ -148,15 +143,15 @@
     outer_pairs = [(i, (i + 1 if i % 2 else i - 1) % devices) for i in range(devices)]
     inner_pairs = [(i, i ^ 1) for i in range(devices)]
     core = lax.axis_index("c")
-    at = jnp.stack([core, lax.axis_index("x"), lax.axis_index("y") % 2]).astype(jnp.int32)
-    pieces = gather_rotation(rotation.T)
+    at = jnp.stack([core, lax.axis_index("x")]).astype(jnp.int32)
+    pieces, token = gather_rotation(rotation.T)
 
     outer = swap(orbitals, outer_pairs)
     inner = swap(orbitals, inner_pairs)
     first = stencil(at, orbitals, outer, inner, potential)
     outer = swap(first, outer_pairs)
     inner = swap(first, inner_pairs)
-    filtered = stencil(at, first, outer, inner, potential, orbitals)
+    filtered = stencil(at, first, outer, inner, potential, orbitals, token)
     orbs, planes, ny, nz = orbitals.shape
     groups = lax.axis_size(BAND)
     parts = filtered.reshape(groups, -1, nz)
@@ -174,6 +169,6 @@
 
 
 def solution(mesh):
-    devices = np.asarray(mesh.devices).reshape(8, 3, 2, 4, 4)
+    devices = np.asarray(mesh.devices).reshape(4, 2, 3, 2, 4, 4)
     fine = Mesh(devices, GRID + BAND)
     return run(fine)

time: 154 us -> 166 us (1.078)
  blocking collectives: 34.3 us -> 58.1 us
  starting transfers between devices: 58.6 us -> 41.2 us
  waiting for transfers between devices: 47.6 us -> 52.2 us
  local copies, waits for them, and re-layouts: 2.12 us -> 6.62 us
    all_to_all x1 -> x2, blocking collectives: 13.6 us -> 35.9 us  [to_all(): return lax.all_to_all(copies, axis, 0, 0, tiled=True)]
    ppermute x6 -> x3, starting transfers between devices: 29.6 us -> 12.5 us  [the longest x1 5.81 us: gather_rotation(): near2 = lax.ppermute(near, 'c', [(0, 1), (1, 0)])]
    ppermute x4, waiting for transfers between devices: 35.8 us -> 42.3 us  [swap(): return lax.ppermute(value, GRID, pairs)]
    unnamed x6 -> x14, local copies, waits for them, and re-layouts: 0.96 us -> 5.38 us
    all_to_all x1, starting transfers between devices: 9.8 us -> 6.89 us  [per_device(): parts = lax.all_to_all(parts, BAND, 0, 0, tiled=True)]
    ppermute x4, starting transfers between devices: 19.2 us -> 21.9 us  [swap(): return lax.ppermute(value, GRID, pairs)]
    ppermute x6 -> x3, waiting for transfers between devices: 11.9 us -> 9.92 us  [the longest x1 9.92 us: gather_rotation(): far = lax.ppermute(near, ('c', 'x'), line)]
  transfers between devices with their start and end apart: 11 -> 8, of which waited for: 5 -> 3; matrix products, arithmetic and copies ran while one was open for 1% -> 0% of each run, Pallas kernels for 3% -> 1%
where the time goes in v4:
time: 166 us; the launch traced here: 165 us
  blocking collectives  58.1 us (35%)
  waiting for transfers between devices  52.2 us (31%)
  starting transfers between devices  41.2 us (25%)
  local copies, waits for them, and re-layouts  6.62 us (4%)
  Pallas kernels  6.56 us (4%)
    ppermute x4, waiting for transfers between devices, swap(): return lax.ppermute(value, GRID, pairs)  42.3 us
    all_to_all x2, blocking collectives, to_all(): return lax.all_to_all(copies, axis, 0, 0, tiled=True)  35.9 us
    all_to_all x1, blocking collectives, per_device(): back = lax.all_to_all(mixed, BAND, 0, 0, tiled=True)  22.1 us
    ppermute x4, starting transfers between devices, swap(): return lax.ppermute(value, GRID, pairs)  21.9 us
    ppermute x1, waiting for transfers between devices, gather_rotation(): far = lax.ppermute(near, ('c', 'x'), line)  9.92 us
    all_to_all x1, starting transfers between devices, per_device(): parts = lax.all_to_all(parts, BAND, 0, 0, tiled=True)  6.89 us
    ppermute x1, starting transfers between devices, gather_rotation(): near2 = lax.ppermute(near, 'c', [(0, 1), (1, 0)])  5.81 us
    unnamed x14, local copies, waits for them, and re-layouts  5.38 us
  transfers between devices with their start and end apart: 8, of which 3 were waited for; matrix products, arithmetic and copies ran while one was open for 0% of the time, Pallas kernels for 1%

profile of v4, /device:TPU:1, one launch (start us, length us, event | category | flops | bytes accessed | tf_op | source)
XLA Modules:
  0.0 164.9 jit_solution(17567209100985756180)
XLA Ops:
  0.0 0.0 copy-start
  0.0 0.9 copy-done
  1.0 13.6 %all_to_all.20 = f32[4,32,512]{2,1,0:T(8,128)S(1)} all-to-all(f32[4,32,512]{2,1,0:T(8,128)S(1)} %broadcast_in_dim.4), channel_id=1, replica_groups=mesh['yh'=4,'yp'=2,'zh'=3,'c'=2,'x'=4,'zl'=4] {'zl'}, dimensions={0} | all-to-all | bytes 524288 | tf_op jit(solution)/shard_map/all_to_all | solution.py:120
  14.6 0.1 broadcast_in_dim.5
  14.7 0.0 copy-start.1
  14.7 22.4 %all_to_all.21.refs_2_ = f32[4,4,32,512]{3,2,1,0:T(8,128)S(1)} all-to-all(f32[4,4,32,512]{3,2,1,0:T(8,128)S(1)} %broadcast_in_dim.5), channel_id=1, replica_groups=mesh['yh'=4,'yp'=2,'zh'=3,'c'=2,'x'=4,'zl'=4] {'yp','c'}, dimensions={0} | all-to-all | bytes 2097152 | tf_op jit(solution)/shard_map/all_to_all | solution.py:120
  37.1 0.0 copy-start.6
  37.1 2.2 %collective-permute-start.4 = (f32[4,4,32,512]{3,2,1,0:T(8,128)S(1)}, f32[4,4,32,512]{3,2,1,0:T(8,128)S(1)}, u32[]{:S(2)}, u32[]{:S(2)}) collective-permute-start(f32[4,4,32,512]{3,2,1,0:T(8,128)S(1)} %all_to_all.21.refs_2_), channel_id=1, source_target_pairs={{0,4},{16,28},{4,8},{20,16},{8,12},{24,20},{12,0},{28,24},{1,5},{1... | collective-permute-start | bytes 3145736 | tf_op jit(solution)/shard_map/ppermute | solution.py:130
  39.2 0.0 copy-done.1
  39.2 2.8 %collective-permute-start.1 = (f32[64,2,8,128]{3,2,1,0:T(8,128)S(1)}, f32[64,2,8,128]{3,2,1,0:T(8,128)S(1)}, u32[]{:S(2)}, u32[]{:S(2)}) collective-permute-start(f32[64,2,8,128]{3,2,1,0:T(8,128)S(1)} %copy-done.1), channel_id=1, source_target_pairs={{0,16},{16,0},{32,48},{48,32},{64,80},{80,64},{96,112},{112,96},{1... | collective-permute-start | bytes 1572872 | tf_op jit(solution)/shard_map/ppermute | solution.py:138
  42.1 9.8 %collective-permute-start = (f32[64,2,8,128]{3,2,1,0:T(8,128)S(1)}, f32[64,2,8,128]{3,2,1,0:T(8,128)}, u32[]{:S(2)}, u32[]{:S(2)}) collective-permute-start(f32[64,2,8,128]{3,2,1,0:T(8,128)S(1)} %copy-done.1), channel_id=1, source_target_pairs={{0,752},{16,32},{32,16},{48,64},{64,48},{80,96},{96,80},{112,128},... | collective-permute-start | bytes 1572872 | tf_op jit(solution)/shard_map/ppermute | solution.py:138
  51.9 0.1 pad_add_fusion.refs_0_
  52.0 0.0 collective-permute-done.1.refs_3_
  52.0 23.6 %collective-permute-done.refs_2_ = f32[64,2,8,128]{3,2,1,0:T(8,128)} collective-permute-done((f32[64,2,8,128]{3,2,1,0:T(8,128)S(1)}, f32[64,2,8,128]{3,2,1,0:T(8,128)}, u32[]{:S(2)}, u32[]{:S(2)}) %collective-permute-start) | collective-permute-done | bytes 524320 | tf_op jit(solution)/shard_map/ppermute | solution.py:138
  75.6 0.0 copy-done.6
  75.6 2.2 %stencil.2.refs_1_ = f32[64,2,8,128]{3,2,1,0:T(8,128)S(1)} custom-call(s32[2]{0:T(128)S(1)} %pad_add_fusion.refs_0_, f32[64,2,8,128]{3,2,1,0:T(8,128)S(1)} %copy-done.1, f32[64,2,8,128]{3,2,1,0:T(8,128)} %collective-permute-done.refs_2_, f32[64,2,8,128]{3,2,1,0:T(8,128)S(1)} %collective-permute-done.1.refs_3_, f32[2,8,128]{2,1,0:T(8,128)S(1)} %copy-done.6), custom_call_target="tpu_custom_call" | custom-call | tf_op jit(solution)/shard_map/stencil/pallas_call | solution.py:63
  77.8 1.9 %collective-permute-start.3 = (f32[64,2,8,128]{3,2,1,0:T(8,128)S(1)}, f32[64,2,8,128]{3,2,1,0:T(8,128)S(1)}, u32[]{:S(2)}, u32[]{:S(2)}) collective-permute-start(f32[64,2,8,128]{3,2,1,0:T(8,128)S(1)} %stencil.2.refs_1_), channel_id=1, source_target_pairs={{0,16},{16,0},{32,48},{48,32},{64,80},{80,64},{96,112},{112,96},{1... | collective-permute-start | bytes 1572872 | tf_op jit(solution)/shard_map/ppermute | solution.py:138
  79.7 7.3 %collective-permute-start.2 = (f32[64,2,8,128]{3,2,1,0:T(8,128)S(1)}, f32[64,2,8,128]{3,2,1,0:T(8,128)S(1)}, u32[]{:S(2)}, u32[]{:S(2)}) collective-permute-start(f32[64,2,8,128]{3,2,1,0:T(8,128)S(1)} %stencil.2.refs_1_), channel_id=1, source_target_pairs={{0,752},{16,32},{32,16},{48,64},{64,48},{80,96},{96,80},{112,128},... | collective-permute-start | bytes 1572872 | tf_op jit(solution)/shard_map/ppermute | solution.py:138
  87.1 0.0 collective-permute-done.4.refs_3_
  87.1 0.0 collective-permute-done.3.refs_3_
  87.1 18.7 %collective-permute-done.2.refs_2_ = f32[64,2,8,128]{3,2,1,0:T(8,128)S(1)} collective-permute-done((f32[64,2,8,128]{3,2,1,0:T(8,128)S(1)}, f32[64,2,8,128]{3,2,1,0:T(8,128)S(1)}, u32[]{:S(2)}, u32[]{:S(2)}) %collective-permute-start.2) | collective-permute-done | bytes 524320 | tf_op jit(solution)/shard_map/ppermute | solution.py:138
  105.8 2.5 %stencil.3 = f32[2,8,64,128]{3,2,1,0:T(8,128)} custom-call(s32[2]{0:T(128)S(1)} %pad_add_fusion.refs_0_, f32[64,2,8,128]{3,2,1,0:T(8,128)S(1)} %stencil.2.refs_1_, f32[64,2,8,128]{3,2,1,0:T(8,128)S(1)} %collective-permute-done.2.refs_2_, f32[64,2,8,128]{3,2,1,0:T(8,128)S(1)} %collective-permute-done.3.refs_3_, f32[2,8,128]{2,1,0:T(8,128)S(1)} %copy-done.6, ...), custom_call_target="tpu_custom_call" | custom-call | tf_op jit(solution)/shard_map/stencil/pallas_call | solution.py:63
  108.3 6.9 %all-to-all-start.2 = ((f32[16,64,128]{2,1,0:T(8,128)}), f32[16,64,128]{2,1,0:T(8,128)S(1)}, u32[]{:S(2)}, u32[]{:S(2)}) async-start(f32[16,64,128]{2,1,0:T(8,128)} %bitcast.4), calls=%async_computation.2 | async-start | bytes 1048576 | tf_op jit(solution)/shard_map/all_to_all | solution.py:158
  115.2 4.5 %collective-permute-start.6 = (f32[4,4,32,512]{3,2,1,0:T(8,128)S(1)}, f32[4,4,32,512]{3,2,1,0:T(8,128)S(1)}, u32[]{:S(2)}, u32[]{:S(2)}) collective-permute-start(f32[4,4,32,512]{3,2,1,0:T(8,128)S(1)} %collective-permute-done.4.refs_3_), channel_id=1, source_target_pairs={{0,4},{16,28},{4,8},{20,16},{8,12},{24,20},{12,0},{28,24},{1,5},{1... | collective-permute-start | bytes 3145736 | tf_op jit(solution)/shard_map/ppermute | solution.py:131
  119.7 5.8 %collective-permute-start.5 = (f32[4,4,32,512]{3,2,1,0:T(8,128)S(1)}, f32[4,4,32,512]{3,2,1,0:T(8,128)S(1)}, u32[]{:S(2)}, u32[]{:S(2)}) collective-permute-start(f32[4,4,32,512]{3,2,1,0:T(8,128)S(1)} %collective-permute-done.4.refs_3_), channel_id=1, source_target_pairs={{0,16},{16,0},{1,17},{17,1},{2,18},{18,2},{3,19},{19,3},{4,20},{20... | collective-permute-start | bytes 3145736 | tf_op jit(solution)/shard_map/ppermute | solution.py:132
  125.5 9.9 %collective-permute-done.6.refs_5_ = f32[4,4,32,512]{3,2,1,0:T(8,128)S(1)} collective-permute-done((f32[4,4,32,512]{3,2,1,0:T(8,128)S(1)}, f32[4,4,32,512]{3,2,1,0:T(8,128)S(1)}, u32[]{:S(2)}, u32[]{:S(2)}) %collective-permute-start.6) | collective-permute-done | bytes 1048608 | tf_op jit(solution)/shard_map/ppermute | solution.py:131
  135.4 0.0 copy-start.2
  135.4 1.0 copy-done.2
  136.4 0.0 collective-permute-done.5.refs_4_
  136.4 0.0 copy-start.4
  136.4 1.0 copy-done.4
  137.4 0.0 all-to-all-done.2
  137.4 0.0 copy-start.3
  137.4 1.2 copy-done.3
  138.6 0.0 copy-start.5
  138.6 1.2 copy-done.5
  139.8 1.9 %rotate.1 = f32[16,64,128]{2,1,0:T(8,128)S(1)} custom-call(s32[2]{0:T(128)S(1)} %pad_add_fusion.refs_0_, f32[1024,128]{1,0:T(8,128)S(1)} %bitcast.11, f32[4,4,32,512]{3,2,1,0:T(8,128)S(1)} %all_to_all.21.refs_2_, f32[4,4,32,512]{3,2,1,0:T(8,128)S(1)} %collective-permute-done.4.refs_3_, f32[4,4,32,512]{3,2,1,0:T(8,128)S(1)} %copy-done.5, ...), custom_call_target="tpu_custom_call" | custom-call | tf_op jit(solution)/shard_map/rotate/pallas_call | solution.py:106
  141.7 22.1 %all_to_all.22 = f32[16,64,128]{2,1,0:T(8,128)S(1)} all-to-all(f32[16,64,128]{2,1,0:T(8,128)S(1)} %rotate.1), channel_id=1, replica_groups=mesh['yh'=4,'yp'=2,'zh'=3,'c'=2,'x'=4,'zl'=4] {'x','zl'}, dimensions={0} | all-to-all | bytes 1048576 | tf_op jit(solution)/shard_map/all_to_all | solution.py:160
  163.8 1.1 copy.4
  (3 shorter events, 0.0 us)
Async XLA Ops:
  0.0 1.0 copy-start
  14.7 24.6 %copy-start.1 = (f32[64,2,8,128]{3,2,1,0:T(8,128)S(1)}, f32[64,2,8,128]{3,2,1,0:T(8,128)}, u32[]{:S(2)}) copy-start(f32[64,2,8,128]{3,2,1,0:T(8,128)} %refs_5_.1) | copy-start | bytes 1572868
  37.1 38.6 %copy-start.6 = (f32[2,8,128]{2,1,0:T(8,128)S(1)}, f32[2,8,128]{2,1,0:T(8,128)}, u32[]{:S(2)}) copy-start(f32[2,8,128]{2,1,0:T(8,128)} %refs_4_.3) | copy-start | bytes 24580
  37.1 50.0 %collective-permute-start.4 = (f32[4,4,32,512]{3,2,1,0:T(8,128)S(1)}, f32[4,4,32,512]{3,2,1,0:T(8,128)S(1)}, u32[]{:S(2)}, u32[]{:S(2)}) collective-permute-start(f32[4,4,32,512]{3,2,1,0:T(8,128)S(1)} %all_to_all.21.refs_2_), channel_id=1, source_target_pairs={{0,4},{16,28},{4,8},{20,16},{8,12},{24,20},{12,0},{28,24},{1,5},{1... | collective-permute-start | bytes 3145736 | tf_op jit(solution)/shard_map/ppermute | solution.py:130
  39.2 12.7 %collective-permute-start.1 = (f32[64,2,8,128]{3,2,1,0:T(8,128)S(1)}, f32[64,2,8,128]{3,2,1,0:T(8,128)S(1)}, u32[]{:S(2)}, u32[]{:S(2)}) collective-permute-start(f32[64,2,8,128]{3,2,1,0:T(8,128)S(1)} %copy-done.1), channel_id=1, source_target_pairs={{0,16},{16,0},{32,48},{48,32},{64,80},{80,64},{96,112},{112,96},{1... | collective-permute-start | bytes 1572872 | tf_op jit(solution)/shard_map/ppermute | solution.py:138
  42.1 33.5 %collective-permute-start = (f32[64,2,8,128]{3,2,1,0:T(8,128)S(1)}, f32[64,2,8,128]{3,2,1,0:T(8,128)}, u32[]{:S(2)}, u32[]{:S(2)}) collective-permute-start(f32[64,2,8,128]{3,2,1,0:T(8,128)S(1)} %copy-done.1), channel_id=1, source_target_pairs={{0,752},{16,32},{32,16},{48,64},{64,48},{80,96},{96,80},{112,128},... | collective-permute-start | bytes 1572872 | tf_op jit(solution)/shard_map/ppermute | solution.py:138
  77.8 9.3 %collective-permute-start.3 = (f32[64,2,8,128]{3,2,1,0:T(8,128)S(1)}, f32[64,2,8,128]{3,2,1,0:T(8,128)S(1)}, u32[]{:S(2)}, u32[]{:S(2)}) collective-permute-start(f32[64,2,8,128]{3,2,1,0:T(8,128)S(1)} %stencil.2.refs_1_), channel_id=1, source_target_pairs={{0,16},{16,0},{32,48},{48,32},{64,80},{80,64},{96,112},{112,96},{1... | collective-permute-start | bytes 1572872 | tf_op jit(solution)/shard_map/ppermute | solution.py:138
  79.7 26.0 %collective-permute-start.2 = (f32[64,2,8,128]{3,2,1,0:T(8,128)S(1)}, f32[64,2,8,128]{3,2,1,0:T(8,128)S(1)}, u32[]{:S(2)}, u32[]{:S(2)}) collective-permute-start(f32[64,2,8,128]{3,2,1,0:T(8,128)S(1)} %stencil.2.refs_1_), channel_id=1, source_target_pairs={{0,752},{16,32},{32,16},{48,64},{64,48},{80,96},{96,80},{112,128},... | collective-permute-start | bytes 1572872 | tf_op jit(solution)/shard_map/ppermute | solution.py:138
  108.3 29.1 %all-to-all-start.2 = ((f32[16,64,128]{2,1,0:T(8,128)}), f32[16,64,128]{2,1,0:T(8,128)S(1)}, u32[]{:S(2)}, u32[]{:S(2)}) async-start(f32[16,64,128]{2,1,0:T(8,128)} %bitcast.4), calls=%async_computation.2 | async-start | bytes 1048576 | tf_op jit(solution)/shard_map/all_to_all | solution.py:158
  115.2 20.2 %collective-permute-start.6 = (f32[4,4,32,512]{3,2,1,0:T(8,128)S(1)}, f32[4,4,32,512]{3,2,1,0:T(8,128)S(1)}, u32[]{:S(2)}, u32[]{:S(2)}) collective-permute-start(f32[4,4,32,512]{3,2,1,0:T(8,128)S(1)} %collective-permute-done.4.refs_3_), channel_id=1, source_target_pairs={{0,4},{16,28},{4,8},{20,16},{8,12},{24,20},{12,0},{28,24},{1,5},{1... | collective-permute-start | bytes 3145736 | tf_op jit(solution)/shard_map/ppermute | solution.py:131
  119.7 16.7 %collective-permute-start.5 = (f32[4,4,32,512]{3,2,1,0:T(8,128)S(1)}, f32[4,4,32,512]{3,2,1,0:T(8,128)S(1)}, u32[]{:S(2)}, u32[]{:S(2)}) collective-permute-start(f32[4,4,32,512]{3,2,1,0:T(8,128)S(1)} %collective-permute-done.4.refs_3_), channel_id=1, source_target_pairs={{0,16},{16,0},{1,17},{17,1},{2,18},{18,2},{3,19},{19,3},{4,20},{20... | collective-permute-start | bytes 3145736 | tf_op jit(solution)/shard_map/ppermute | solution.py:132
  135.4 1.0 copy-start.2
  136.4 1.0 copy-start.4
  137.4 1.2 copy-start.3
  138.6 1.2 copy-start.5

commit v5 on v4

--- a/solution.py
+++ b/solution.py
@@ -27,7 +27,7 @@
 
 
 def stencil_kernel(combine, par_ref, own, outer, inner, pot_ref, *rest):
-    base, out = (rest[0], rest[-1]) if combine else (None, rest[0])
+    base, out = rest if combine else (None, rest[0])
     par = par_ref[0]
     other = 1 - par
     pot_a = ((pot_ref[par] - 3.0) * 0.0625)[None]
@@ -55,10 +55,10 @@
     return pltpu.with_memory_space_constraint(value, pltpu.VMEM)
 
 
-def stencil(par, own, outer, inner, pot, base=None, token=None):
+def stencil(par, own, outer, inner, pot, base=None):
     combine = base is not None
     orbs, planes, ny, nz = own.shape
-    args = (own, outer, inner, pot) + ((base, token) if combine else ())
+    args = (own, outer, inner, pot) + ((base,) if combine else ())
     shape = (planes, ny, orbs, nz) if combine else own.shape
     return pl.pallas_call(
         lambda *refs: stencil_kernel(combine, *refs),
@@ -130,8 +130,7 @@
     near = lax.ppermute(own, ("c", "x"), line)
     far = lax.ppermute(near, ("c", "x"), line)
     near2 = lax.ppermute(near, "c", [(0, 1), (1, 0)])
-    token = near[0, 0, :8, :128] * 2.0
-    return (own, near, near2, far), token
+    return own, near, near2, far
 
 
 def swap(value, pairs):
@@ -144,14 +143,14 @@
     inner_pairs = [(i, i ^ 1) for i in range(devices)]
     core = lax.axis_index("c")
     at = jnp.stack([core, lax.axis_index("x")]).astype(jnp.int32)
-    pieces, token = gather_rotation(rotation.T)
+    pieces = gather_rotation(rotation.T)
 
     outer = swap(orbitals, outer_pairs)
     inner = swap(orbitals, inner_pairs)
     first = stencil(at, orbitals, outer, inner, potential)
     outer = swap(first, outer_pairs)
     inner = swap(first, inner_pairs)
-    filtered = stencil(at, first, outer, inner, potential, orbitals, token)
+    filtered = stencil(at, first, outer, inner, potential, orbitals)
     orbs, planes, ny, nz = orbitals.shape
     groups = lax.axis_size(BAND)
     parts = filtered.reshape(groups, -1, nz)

time: 166 us -> 149 us (0.90)
  blocking collectives: 58.1 us -> 35.8 us
  starting transfers between devices: 41.2 us -> 49.8 us
  local copies, waits for them, and re-layouts: 6.62 us -> 3.19 us
    all_to_all x2 -> x1, blocking collectives: 35.9 us -> 13.6 us  [to_all(): return lax.all_to_all(copies, axis, 0, 0, tiled=True)]
    all_to_all x0 -> x1, starting transfers between devices: none -> 10 us  [to_all(): return lax.all_to_all(copies, axis, 0, 0, tiled=True)]
    all_to_all x1, waiting for transfers between devices: 0.01 us -> 6.84 us  [per_device(): parts = lax.all_to_all(parts, BAND, 0, 0, tiled=True)]
    ppermute x4, waiting for transfers between devices: 42.3 us -> 37.2 us  [swap(): return lax.ppermute(value, GRID, pairs)]
    ppermute x1, waiting for transfers between devices: 9.92 us -> 4.99 us  [gather_rotation(): far = lax.ppermute(near, ('c', 'x'), line)]
    unnamed x14 -> x6, local copies, waits for them, and re-layouts: 5.38 us -> 0.96 us
    all_to_all x0 -> x1, waiting for transfers between devices: none -> 3.24 us  [to_all(): return lax.all_to_all(copies, axis, 0, 0, tiled=True)]
    all_to_all x1, starting transfers between devices: 6.89 us -> 9.97 us  [per_device(): parts = lax.all_to_all(parts, BAND, 0, 0, tiled=True)]
  transfers between devices with their start and end apart: 8 -> 9, of which waited for: 3 -> 5; matrix products, arithmetic and copies ran while one was open for 0% -> 0% of each run, Pallas kernels for 1% -> 3%
where the time goes in v5:
time: 149 us
  waiting for transfers between devices  52.3 us (35%)
  starting transfers between devices  49.8 us (33%)
  blocking collectives  35.8 us (24%)
  Pallas kernels  7.53 us (5%)
  local copies, waits for them, and re-layouts  3.19 us (2%)
    ppermute x4, waiting for transfers between devices, swap(): return lax.ppermute(value, GRID, pairs)  37.2 us
    all_to_all x1, blocking collectives, per_device(): back = lax.all_to_all(mixed, BAND, 0, 0, tiled=True)  22.3 us
    ppermute x4, starting transfers between devices, swap(): return lax.ppermute(value, GRID, pairs)  19.4 us
    all_to_all x1, blocking collectives, to_all(): return lax.all_to_all(copies, axis, 0, 0, tiled=True)  13.6 us
    all_to_all x1, starting transfers between devices, to_all(): return lax.all_to_all(copies, axis, 0, 0, tiled=True)  10 us
    all_to_all x1, starting transfers between devices, per_device(): parts = lax.all_to_all(parts, BAND, 0, 0, tiled=True)  9.97 us
    all_to_all x1, waiting for transfers between devices, per_device(): parts = lax.all_to_all(parts, BAND, 0, 0, tiled=True)  6.84 us
    ppermute x1, waiting for transfers between devices, gather_rotation(): far = lax.ppermute(near, ('c', 'x'), line)  4.99 us
  transfers between devices with their start and end apart: 9, of which 5 were waited for; matrix products, arithmetic and copies ran while one was open for 0% of the time, Pallas kernels for 3%

profile of v5, /device:TPU:1, one launch (start us, length us, event | category | flops | bytes accessed | tf_op | source)
XLA Modules:
  0.0 148.8 jit_solution(2432210319875975024)
XLA Ops:
  0.0 0.0 copy-start
  0.0 0.9 copy-done
  1.0 13.6 %all_to_all.20 = f32[4,32,512]{2,1,0:T(8,128)S(1)} all-to-all(f32[4,32,512]{2,1,0:T(8,128)S(1)} %broadcast_in_dim.4), channel_id=1, replica_groups=mesh['yh'=4,'yp'=2,'zh'=3,'c'=2,'x'=4,'zl'=4] {'zl'}, dimensions={0} | all-to-all | bytes 524288 | tf_op jit(solution)/shard_map/all_to_all | solution.py:120
  14.6 1.1 broadcast_in_dim.5
  15.7 0.0 copy-start.1
  15.7 10.0 %all-to-all-start.2 = ((f32[4,4,32,512]{3,2,1,0:T(8,128)}), f32[4,4,32,512]{3,2,1,0:T(8,128)S(1)}, u32[]{:S(2)}, u32[]{:S(2)}) async-start(f32[4,4,32,512]{3,2,1,0:T(8,128)} %broadcast_in_dim.5), calls=%async_computation.2 | async-start | bytes 2097152 | tf_op jit(solution)/shard_map/all_to_all | solution.py:120
  25.7 0.0 copy-done.1
  25.7 0.0 copy-start.2
  25.7 2.0 %collective-permute-start.1 = (f32[64,2,8,128]{3,2,1,0:T(8,128)S(1)}, f32[64,2,8,128]{3,2,1,0:T(8,128)S(1)}, u32[]{:S(2)}, u32[]{:S(2)}) collective-permute-start(f32[64,2,8,128]{3,2,1,0:T(8,128)S(1)} %copy-done.1), channel_id=1, source_target_pairs={{0,16},{16,0},{32,48},{48,32},{64,80},{80,64},{96,112},{112,96},{1... | collective-permute-start | bytes 1572872 | tf_op jit(solution)/shard_map/ppermute | solution.py:137
  27.7 8.2 %collective-permute-start = (f32[64,2,8,128]{3,2,1,0:T(8,128)S(1)}, f32[64,2,8,128]{3,2,1,0:T(8,128)}, u32[]{:S(2)}, u32[]{:S(2)}) collective-permute-start(f32[64,2,8,128]{3,2,1,0:T(8,128)S(1)} %copy-done.1), channel_id=1, source_target_pairs={{0,752},{16,32},{32,16},{48,64},{64,48},{80,96},{96,80},{112,128},... | collective-permute-start | bytes 1572872 | tf_op jit(solution)/shard_map/ppermute | solution.py:137
  35.9 3.2 %all-to-all-done.2.refs_2_ = f32[4,4,32,512]{3,2,1,0:T(8,128)S(1)} async-done(((f32[4,4,32,512]{3,2,1,0:T(8,128)}), f32[4,4,32,512]{3,2,1,0:T(8,128)S(1)}, u32[]{:S(2)}, u32[]{:S(2)}) %all-to-all-start.2) | async-done | bytes 1048608 | tf_op jit(solution)/shard_map/all_to_all | solution.py:120
  39.2 1.9 %collective-permute-start.4 = (f32[4,4,32,512]{3,2,1,0:T(8,128)S(1)}, f32[4,4,32,512]{3,2,1,0:T(8,128)S(1)}, u32[]{:S(2)}, u32[]{:S(2)}) collective-permute-start(f32[4,4,32,512]{3,2,1,0:T(8,128)S(1)} %all-to-all-done.2.refs_2_), channel_id=1, source_target_pairs={{0,4},{16,28},{4,8},{20,16},{8,12},{24,20},{12,0},{28,24},{1,5},{1... | collective-permute-start | bytes 3145736 | tf_op jit(solution)/shard_map/ppermute | solution.py:130
  41.1 0.1 pad_add_fusion.refs_0_
  41.2 0.0 collective-permute-done.1.refs_3_
  41.2 18.5 %collective-permute-done.refs_2_ = f32[64,2,8,128]{3,2,1,0:T(8,128)} collective-permute-done((f32[64,2,8,128]{3,2,1,0:T(8,128)S(1)}, f32[64,2,8,128]{3,2,1,0:T(8,128)}, u32[]{:S(2)}, u32[]{:S(2)}) %collective-permute-start) | collective-permute-done | bytes 524320 | tf_op jit(solution)/shard_map/ppermute | solution.py:137
  59.6 0.0 copy-done.2
  59.6 2.2 %stencil.2.refs_1_ = f32[64,2,8,128]{3,2,1,0:T(8,128)S(1)} custom-call(s32[2]{0:T(128)S(1)} %pad_add_fusion.refs_0_, f32[64,2,8,128]{3,2,1,0:T(8,128)S(1)} %copy-done.1, f32[64,2,8,128]{3,2,1,0:T(8,128)} %collective-permute-done.refs_2_, f32[64,2,8,128]{3,2,1,0:T(8,128)S(1)} %collective-permute-done.1.refs_3_, f32[2,8,128]{2,1,0:T(8,128)S(1)} %copy-done.2), custom_call_target="tpu_custom_call" | custom-call | tf_op jit(solution)/shard_map/stencil/pallas_call | solution.py:63
  61.8 1.9 %collective-permute-start.3 = (f32[64,2,8,128]{3,2,1,0:T(8,128)S(1)}, f32[64,2,8,128]{3,2,1,0:T(8,128)S(1)}, u32[]{:S(2)}, u32[]{:S(2)}) collective-permute-start(f32[64,2,8,128]{3,2,1,0:T(8,128)S(1)} %stencil.2.refs_1_), channel_id=1, source_target_pairs={{0,16},{16,0},{32,48},{48,32},{64,80},{80,64},{96,112},{112,96},{1... | collective-permute-start | bytes 1572872 | tf_op jit(solution)/shard_map/ppermute | solution.py:137
  63.7 7.3 %collective-permute-start.2 = (f32[64,2,8,128]{3,2,1,0:T(8,128)S(1)}, f32[64,2,8,128]{3,2,1,0:T(8,128)S(1)}, u32[]{:S(2)}, u32[]{:S(2)}) collective-permute-start(f32[64,2,8,128]{3,2,1,0:T(8,128)S(1)} %stencil.2.refs_1_), channel_id=1, source_target_pairs={{0,752},{16,32},{32,16},{48,64},{64,48},{80,96},{96,80},{112,128},... | collective-permute-start | bytes 1572872 | tf_op jit(solution)/shard_map/ppermute | solution.py:137
  71.0 0.0 collective-permute-done.3.refs_3_
  71.0 18.7 %collective-permute-done.2.refs_2_ = f32[64,2,8,128]{3,2,1,0:T(8,128)S(1)} collective-permute-done((f32[64,2,8,128]{3,2,1,0:T(8,128)S(1)}, f32[64,2,8,128]{3,2,1,0:T(8,128)S(1)}, u32[]{:S(2)}, u32[]{:S(2)}) %collective-permute-start.2) | collective-permute-done | bytes 524320 | tf_op jit(solution)/shard_map/ppermute | solution.py:137
  89.8 2.5 %stencil.3 = f32[2,8,64,128]{3,2,1,0:T(8,128)} custom-call(s32[2]{0:T(128)S(1)} %pad_add_fusion.refs_0_, f32[64,2,8,128]{3,2,1,0:T(8,128)S(1)} %stencil.2.refs_1_, f32[64,2,8,128]{3,2,1,0:T(8,128)S(1)} %collective-permute-done.2.refs_2_, f32[64,2,8,128]{3,2,1,0:T(8,128)S(1)} %collective-permute-done.3.refs_3_, f32[2,8,128]{2,1,0:T(8,128)S(1)} %copy-done.2, ...), custom_call_target="tpu_custom_call" | custom-call | tf_op jit(solution)/shard_map/stencil/pallas_call | solution.py:63
  92.3 10.0 %all-to-all-start = ((f32[16,64,128]{2,1,0:T(8,128)}), f32[16,64,128]{2,1,0:T(8,128)S(1)}, u32[]{:S(2)}, u32[]{:S(2)}) async-start(f32[16,64,128]{2,1,0:T(8,128)} %bitcast.2), calls=%async_computation | async-start | bytes 1048576 | tf_op jit(solution)/shard_map/all_to_all | solution.py:157
  102.3 0.0 collective-permute-done.4.refs_3_
  102.3 4.5 %collective-permute-start.6 = (f32[4,4,32,512]{3,2,1,0:T(8,128)S(1)}, f32[4,4,32,512]{3,2,1,0:T(8,128)}, u32[]{:S(2)}, u32[]{:S(2)}) collective-permute-start(f32[4,4,32,512]{3,2,1,0:T(8,128)S(1)} %collective-permute-done.4.refs_3_), channel_id=1, source_target_pairs={{0,4},{16,28},{4,8},{20,16},{8,12},{24,20},{12,0},{28,24},{1,5},{1... | collective-permute-start | bytes 3145736 | tf_op jit(solution)/shard_map/ppermute | solution.py:131
  106.8 4.0 %collective-permute-start.5 = (f32[4,4,32,512]{3,2,1,0:T(8,128)S(1)}, f32[4,4,32,512]{3,2,1,0:T(8,128)}, u32[]{:S(2)}, u32[]{:S(2)}) collective-permute-start(f32[4,4,32,512]{3,2,1,0:T(8,128)S(1)} %collective-permute-done.4.refs_3_), channel_id=1, source_target_pairs={{0,16},{16,0},{1,17},{17,1},{2,18},{18,2},{3,19},{19,3},{4,20},{20... | collective-permute-start | bytes 3145736 | tf_op jit(solution)/shard_map/ppermute | solution.py:132
  110.8 6.8 %all-to-all-done = f32[16,64,128]{2,1,0:T(8,128)S(1)} async-done(((f32[16,64,128]{2,1,0:T(8,128)}), f32[16,64,128]{2,1,0:T(8,128)S(1)}, u32[]{:S(2)}, u32[]{:S(2)}) %all-to-all-start) | async-done | bytes 524320 | tf_op jit(solution)/shard_map/all_to_all | solution.py:157
  117.6 5.0 %collective-permute-done.6.refs_5_ = f32[4,4,32,512]{3,2,1,0:T(8,128)} collective-permute-done((f32[4,4,32,512]{3,2,1,0:T(8,128)S(1)}, f32[4,4,32,512]{3,2,1,0:T(8,128)}, u32[]{:S(2)}, u32[]{:S(2)}) %collective-permute-start.6) | collective-permute-done | bytes 1048608 | tf_op jit(solution)/shard_map/ppermute | solution.py:131
  122.6 0.0 collective-permute-done.5.refs_4_
  122.6 2.8 %rotate.1 = f32[16,64,128]{2,1,0:T(8,128)S(1)} custom-call(s32[2]{0:T(128)S(1)} %pad_add_fusion.refs_0_, f32[1024,128]{1,0:T(8,128)S(1)} %bitcast.9, f32[4,4,32,512]{3,2,1,0:T(8,128)S(1)} %all-to-all-done.2.refs_2_, f32[4,4,32,512]{3,2,1,0:T(8,128)S(1)} %collective-permute-done.4.refs_3_, f32[4,4,32,512]{3,2,1,0:T(8,128)} %collective-permute-done.5.refs_4_, ...), custom_call_target="tpu_custom_call" | custom-call | tf_op jit(solution)/shard_map/rotate/pallas_call | solution.py:106
  125.4 22.3 %all_to_all.21 = f32[16,64,128]{2,1,0:T(8,128)S(1)} all-to-all(f32[16,64,128]{2,1,0:T(8,128)S(1)} %rotate.1), channel_id=1, replica_groups=mesh['yh'=4,'yp'=2,'zh'=3,'c'=2,'x'=4,'zl'=4] {'x','zl'}, dimensions={0} | all-to-all | bytes 1048576 | tf_op jit(solution)/shard_map/all_to_all | solution.py:159
  147.7 1.1 copy.4
  (2 shorter events, 0.0 us)
Async XLA Ops:
  0.0 1.0 copy-start
  15.7 10.0 %copy-start.1 = (f32[64,2,8,128]{3,2,1,0:T(8,128)S(1)}, f32[64,2,8,128]{3,2,1,0:T(8,128)}, u32[]{:S(2)}) copy-start(f32[64,2,8,128]{3,2,1,0:T(8,128)} %refs_5_.1) | copy-start | bytes 1572868
  15.7 23.5 %all-to-all-start.2 = ((f32[4,4,32,512]{3,2,1,0:T(8,128)}), f32[4,4,32,512]{3,2,1,0:T(8,128)S(1)}, u32[]{:S(2)}, u32[]{:S(2)}) async-start(f32[4,4,32,512]{3,2,1,0:T(8,128)} %broadcast_in_dim.5), calls=%async_computation.2 | async-start | bytes 2097152 | tf_op jit(solution)/shard_map/all_to_all | solution.py:120
  25.7 33.9 %copy-start.2 = (f32[2,8,128]{2,1,0:T(8,128)S(1)}, f32[2,8,128]{2,1,0:T(8,128)}, u32[]{:S(2)}) copy-start(f32[2,8,128]{2,1,0:T(8,128)} %refs_4_.3) | copy-start | bytes 24580
  25.7 15.5 %collective-permute-start.1 = (f32[64,2,8,128]{3,2,1,0:T(8,128)S(1)}, f32[64,2,8,128]{3,2,1,0:T(8,128)S(1)}, u32[]{:S(2)}, u32[]{:S(2)}) collective-permute-start(f32[64,2,8,128]{3,2,1,0:T(8,128)S(1)} %copy-done.1), channel_id=1, source_target_pairs={{0,16},{16,0},{32,48},{48,32},{64,80},{80,64},{96,112},{112,96},{1... | collective-permute-start | bytes 1572872 | tf_op jit(solution)/shard_map/ppermute | solution.py:137
  27.7 31.9 %collective-permute-start = (f32[64,2,8,128]{3,2,1,0:T(8,128)S(1)}, f32[64,2,8,128]{3,2,1,0:T(8,128)}, u32[]{:S(2)}, u32[]{:S(2)}) collective-permute-start(f32[64,2,8,128]{3,2,1,0:T(8,128)S(1)} %copy-done.1), channel_id=1, source_target_pairs={{0,752},{16,32},{32,16},{48,64},{64,48},{80,96},{96,80},{112,128},... | collective-permute-start | bytes 1572872 | tf_op jit(solution)/shard_map/ppermute | solution.py:137
  39.2 63.1 %collective-permute-start.4 = (f32[4,4,32,512]{3,2,1,0:T(8,128)S(1)}, f32[4,4,32,512]{3,2,1,0:T(8,128)S(1)}, u32[]{:S(2)}, u32[]{:S(2)}) collective-permute-start(f32[4,4,32,512]{3,2,1,0:T(8,128)S(1)} %all-to-all-done.2.refs_2_), channel_id=1, source_target_pairs={{0,4},{16,28},{4,8},{20,16},{8,12},{24,20},{12,0},{28,24},{1,5},{1... | collective-permute-start | bytes 3145736 | tf_op jit(solution)/shard_map/ppermute | solution.py:130
  61.8 9.2 %collective-permute-start.3 = (f32[64,2,8,128]{3,2,1,0:T(8,128)S(1)}, f32[64,2,8,128]{3,2,1,0:T(8,128)S(1)}, u32[]{:S(2)}, u32[]{:S(2)}) collective-permute-start(f32[64,2,8,128]{3,2,1,0:T(8,128)S(1)} %stencil.2.refs_1_), channel_id=1, source_target_pairs={{0,16},{16,0},{32,48},{48,32},{64,80},{80,64},{96,112},{112,96},{1... | collective-permute-start | bytes 1572872 | tf_op jit(solution)/shard_map/ppermute | solution.py:137
  63.7 26.0 %collective-permute-start.2 = (f32[64,2,8,128]{3,2,1,0:T(8,128)S(1)}, f32[64,2,8,128]{3,2,1,0:T(8,128)S(1)}, u32[]{:S(2)}, u32[]{:S(2)}) collective-permute-start(f32[64,2,8,128]{3,2,1,0:T(8,128)S(1)} %stencil.2.refs_1_), channel_id=1, source_target_pairs={{0,752},{16,32},{32,16},{48,64},{64,48},{80,96},{96,80},{112,128},... | collective-permute-start | bytes 1572872 | tf_op jit(solution)/shard_map/ppermute | solution.py:137
  92.3 25.3 %all-to-all-start = ((f32[16,64,128]{2,1,0:T(8,128)}), f32[16,64,128]{2,1,0:T(8,128)S(1)}, u32[]{:S(2)}, u32[]{:S(2)}) async-start(f32[16,64,128]{2,1,0:T(8,128)} %bitcast.2), calls=%async_computation | async-start | bytes 1048576 | tf_op jit(solution)/shard_map/all_to_all | solution.py:157
  102.3 20.3 %collective-permute-start.6 = (f32[4,4,32,512]{3,2,1,0:T(8,128)S(1)}, f32[4,4,32,512]{3,2,1,0:T(8,128)}, u32[]{:S(2)}, u32[]{:S(2)}) collective-permute-start(f32[4,4,32,512]{3,2,1,0:T(8,128)S(1)} %collective-permute-done.4.refs_3_), channel_id=1, source_target_pairs={{0,4},{16,28},{4,8},{20,16},{8,12},{24,20},{12,0},{28,24},{1,5},{1... | collective-permute-start | bytes 3145736 | tf_op jit(solution)/shard_map/ppermute | solution.py:131
  106.8 15.8 %collective-permute-start.5 = (f32[4,4,32,512]{3,2,1,0:T(8,128)S(1)}, f32[4,4,32,512]{3,2,1,0:T(8,128)}, u32[]{:S(2)}, u32[]{:S(2)}) collective-permute-start(f32[4,4,32,512]{3,2,1,0:T(8,128)S(1)} %collective-permute-done.4.refs_3_), channel_id=1, source_target_pairs={{0,16},{16,0},{1,17},{17,1},{2,18},{18,2},{3,19},{19,3},{4,20},{20... | collective-permute-start | bytes 3145736 | tf_op jit(solution)/shard_map/ppermute | solution.py:132

commit v6 on v5

--- a/solution.py
+++ b/solution.py
@@ -7,7 +7,7 @@
 from jax.sharding import Mesh, PartitionSpec as P
 
 GROUP = 8
-GRID = ("yh", "yp", "zh", "c")
+GRID = ("y", "zh", "c")
 BAND = ("x", "zl")
 
 
@@ -27,7 +27,7 @@
 
 
 def stencil_kernel(combine, par_ref, own, outer, inner, pot_ref, *rest):
-    base, out = rest if combine else (None, rest[0])
+    base, out = (rest[0], rest[-1]) if combine else (None, rest[0])
     par = par_ref[0]
     other = 1 - par
     pot_a = ((pot_ref[par] - 3.0) * 0.0625)[None]
@@ -71,9 +71,9 @@
     )(par, *map(in_vmem, args))
 
 
-def rotate_kernel(nx, at_ref, v, own, near, near2, far, out, wide):
-    core, x = at_ref[0], at_ref[1]
-    _, nzl, rows, half = own.shape
+def rotate_kernel(at_ref, v, own, other, out, wide):
+    core = at_ref[0]
+    ny, nx, nzl, rows, half = own.shape
     value = v[...]
     high = value.astype(jnp.bfloat16)
     low = (value - high.astype(jnp.float32)).astype(jnp.bfloat16)
@@ -81,30 +81,25 @@
     nz = v.shape[1]
 
     def product(piece, which):
+        piece = piece.reshape(ny * nzl * rows, half)
         high = piece.astype(jnp.bfloat16)
         low = (piece - high.astype(jnp.float32)).astype(jnp.bfloat16)
-        at = which * half
-        both = jnp.dot(high, wide[at : at + half, :], preferred_element_type=jnp.float32)
-        rest = jnp.dot(low, wide[at : at + half, :nz], preferred_element_type=jnp.float32)
+        at = pl.ds(pl.multiple_of(which * half, half), half)
+        both = jnp.dot(high, wide[at, :], preferred_element_type=jnp.float32)
+        rest = jnp.dot(low, wide[at, :nz], preferred_element_type=jnp.float32)
         return both[:, :nz] + both[:, nz:] + rest
 
-    def slab(ref, slab_x):
-        for pair in (0, 1):
-            total = product(ref[2 * pair].reshape(nzl * rows, half), 0)
-            total += product(ref[2 * pair + 1].reshape(nzl * rows, half), 1)
+    for x in range(nx):
+        total = product(own[:, x], core) + product(other[:, x], 1 - core)
+        for y in range(ny):
             for z in range(nzl):
-                out[slab_x * nzl + z, pair * rows : (pair + 1) * rows] = total[z * rows : (z + 1) * rows]
-
-    step = 1 - 2 * core
-    slab(own, x)
-    slab(near, lax.rem(x - step + nx, nx))
-    slab(near2, lax.rem(x + step + nx, nx))
-    slab(far, lax.rem(x + 2, nx))
+                at = (y * nzl + z) * rows
+                out[x * nzl + z, y * rows : (y + 1) * rows] = total[at : at + rows]
 
 
-def rotate(nx, at, v, pieces, shape):
+def rotate(at, v, pieces, shape):
     return pl.pallas_call(
-        lambda *refs: rotate_kernel(nx, *refs),
+        rotate_kernel,
         out_shape=pltpu.VMEM(shape, v.dtype),
         in_specs=[pl.BlockSpec(memory_space=pltpu.SMEM)]
         + [pl.BlockSpec(memory_space=pltpu.VMEM)] * (1 + len(pieces)),
@@ -121,16 +116,13 @@
 
 
 def gather_rotation(rot_t):
-    nx = lax.axis_size("x")
-    rows, cols = rot_t.shape[0] // 2, rot_t.shape[1] // 2
-    at = (lax.axis_index("yp") * rows, lax.axis_index("c") * cols)
+    rows, cols = rot_t.shape[0] // lax.axis_size("y"), rot_t.shape[1] // 2
+    at = (lax.axis_index("y") * rows, lax.axis_index("c") * cols)
     part = to_all(lax.dynamic_slice(rot_t, at, (rows, cols)), "zl")
-    own = to_all(part, ("yp", "c"))
-    line = [(c * nx + i, c * nx + (i + 1 - 2 * c) % nx) for i in range(nx) for c in (0, 1)]
-    near = lax.ppermute(own, ("c", "x"), line)
-    far = lax.ppermute(near, ("c", "x"), line)
-    near2 = lax.ppermute(near, "c", [(0, 1), (1, 0)])
-    return own, near, near2, far
+    part = to_all(part, "x")
+    own = to_all(part, "y")
+    other = lax.ppermute(own, "c", [(0, 1), (1, 0)])
+    return own, other
 
 
 def swap(value, pairs):
@@ -142,7 +134,7 @@
     outer_pairs = [(i, (i + 1 if i % 2 else i - 1) % devices) for i in range(devices)]
     inner_pairs = [(i, i ^ 1) for i in range(devices)]
     core = lax.axis_index("c")
-    at = jnp.stack([core, lax.axis_index("x")]).astype(jnp.int32)
+    at = core.astype(jnp.int32).reshape(1)
     pieces = gather_rotation(rotation.T)
 
     outer = swap(orbitals, outer_pairs)
@@ -155,7 +147,7 @@
     groups = lax.axis_size(BAND)
     parts = filtered.reshape(groups, -1, nz)
     parts = lax.all_to_all(parts, BAND, 0, 0, tiled=True)
-    mixed = rotate(lax.axis_size("x"), at, parts.reshape(groups * orbs, nz), pieces, (groups, orbs, nz))
+    mixed = rotate(at, parts.reshape(groups * orbs, nz), pieces, (groups, orbs, nz))
     back = lax.all_to_all(mixed, BAND, 0, 0, tiled=True)
     return back.transpose(1, 0, 2).reshape(orbs, planes, ny, nz)
 
@@ -168,6 +160,6 @@
 
 
 def solution(mesh):
-    devices = np.asarray(mesh.devices).reshape(4, 2, 3, 2, 4, 4)
+    devices = np.asarray(mesh.devices).reshape(8, 3, 2, 4, 4)
     fine = Mesh(devices, GRID + BAND)
     return run(fine)

time: 149 us -> 168 us (1.13)
  blocking collectives: 35.8 us -> 58.7 us
  starting transfers between devices: 49.8 us -> 35.8 us
  waiting for transfers between devices: 52.3 us -> 64.3 us
  Pallas kernels: 7.53 us -> 4.76 us
    all_to_all x1, waiting for transfers between devices: 3.24 us -> 37.8 us  [to_all(): return lax.all_to_all(copies, axis, 0, 0, tiled=True)]
    all_to_all x0 -> x1, blocking collectives: none -> 18.3 us  [per_device(): parts = lax.all_to_all(parts, BAND, 0, 0, tiled=True)]
    ppermute x4, waiting for transfers between devices: 37.2 us -> 26.5 us  [swap(): return lax.ppermute(value, GRID, pairs)]
    all_to_all x1 -> x0, starting transfers between devices: 9.97 us -> none  [per_device(): parts = lax.all_to_all(parts, BAND, 0, 0, tiled=True)]
    all_to_all x1 -> x2, blocking collectives: 13.6 us -> 21.5 us  [to_all(): return lax.all_to_all(copies, axis, 0, 0, tiled=True)]
    all_to_all x1 -> x0, waiting for transfers between devices: 6.84 us -> none  [per_device(): parts = lax.all_to_all(parts, BAND, 0, 0, tiled=True)]
    ppermute x3 -> x1, waiting for transfers between devices: 4.99 us -> 0.01 us  [gather_rotation(): other = lax.ppermute(own, 'c', [(0, 1), (1, 0)])]
    ppermute x3 -> x1, starting transfers between devices: 10.4 us -> 5.88 us  [gather_rotation(): other = lax.ppermute(own, 'c', [(0, 1), (1, 0)])]
  transfers between devices with their start and end apart: 9 -> 6, of which waited for: 5 -> 2; matrix products, arithmetic and copies ran while one was open for 0% -> 0% of each run, Pallas kernels for 3% -> 2%
where the time goes in v6:
time: 168 us; the launch traced here: 167 us
  waiting for transfers between devices  64.3 us (38%)
  blocking collectives  58.7 us (35%)
  starting transfers between devices  35.8 us (21%)
  Pallas kernels  4.76 us (3%)
  local copies, waits for them, and re-layouts  3.69 us (2%)
    all_to_all x1, waiting for transfers between devices, to_all(): return lax.all_to_all(copies, axis, 0, 0, tiled=True)  37.8 us
    ppermute x4, waiting for transfers between devices, swap(): return lax.ppermute(value, GRID, pairs)  26.5 us
    ppermute x4, starting transfers between devices, swap(): return lax.ppermute(value, GRID, pairs)  23 us
    all_to_all x2, blocking collectives, to_all(): return lax.all_to_all(copies, axis, 0, 0, tiled=True)  21.5 us
    all_to_all x1, blocking collectives, per_device(): back = lax.all_to_all(mixed, BAND, 0, 0, tiled=True)  18.8 us
    all_to_all x1, blocking collectives, per_device(): parts = lax.all_to_all(parts, BAND, 0, 0, tiled=True)  18.3 us
    all_to_all x1, starting transfers between devices, to_all(): return lax.all_to_all(copies, axis, 0, 0, tiled=True)  6.95 us
    ppermute x1, starting transfers between devices, gather_rotation(): other = lax.ppermute(own, 'c', [(0, 1), (1, 0)])  5.88 us
  transfers between devices with their start and end apart: 6, of which 2 were waited for; matrix products, arithmetic and copies ran while one was open for 0% of the time, Pallas kernels for 2%

profile of v6, /device:TPU:1, one launch (start us, length us, event | category | flops | bytes accessed | tf_op | source)
XLA Modules:
  0.0 167.3 jit_solution(17581187070081972507)
XLA Ops:
  0.0 0.0 copy-start
  0.0 0.9 copy-done
  1.0 12.2 %all_to_all.25 = f32[4,8,512]{2,1,0:T(8,128)S(1)} all-to-all(f32[4,8,512]{2,1,0:T(8,128)S(1)} %broadcast_in_dim.6), channel_id=1, replica_groups=mesh['y'=8,'zh'=3,'c'=2,'x'=4,'zl'=4] {'zl'}, dimensions={0} | all-to-all | bytes 131072 | tf_op jit(solution)/shard_map/all_to_all | solution.py:115
  13.2 9.3 %all_to_all.26 = f32[4,4,8,512]{3,2,1,0:T(8,128)S(1)} all-to-all(f32[4,4,8,512]{3,2,1,0:T(8,128)S(1)} %broadcast_in_dim.7), channel_id=1, replica_groups=mesh['y'=8,'zh'=3,'c'=2,'x'=4,'zl'=4] {'x'}, dimensions={0} | all-to-all | bytes 524288 | tf_op jit(solution)/shard_map/all_to_all | solution.py:115
  22.5 1.6 broadcast_in_dim.8
  24.1 0.0 copy-start.1
  24.1 0.0 copy-start.2
  24.1 7.0 %all-to-all-start.3 = ((f32[8,4,4,8,512]{4,3,2,1,0:T(8,128)}), f32[8,4,4,8,512]{4,3,2,1,0:T(8,128)S(1)}, u32[]{:S(2)}, u32[]{:S(2)}) async-start(f32[8,4,4,8,512]{4,3,2,1,0:T(8,128)} %broadcast_in_dim.8), calls=%async_computation.3 | async-start | bytes 4194304 | tf_op jit(solution)/shard_map/all_to_all | solution.py:115
  31.1 0.0 copy-done.1
  31.1 5.7 %collective-permute-start.1 = (f32[64,2,8,128]{3,2,1,0:T(8,128)S(1)}, f32[64,2,8,128]{3,2,1,0:T(8,128)S(1)}, u32[]{:S(2)}, u32[]{:S(2)}) collective-permute-start(f32[64,2,8,128]{3,2,1,0:T(8,128)S(1)} %copy-done.1), channel_id=1, source_target_pairs={{0,16},{16,0},{32,48},{48,32},{64,80},{80,64},{96,112},{112,96},{1... | collective-permute-start | bytes 1572872 | tf_op jit(solution)/shard_map/ppermute | solution.py:129
  36.8 10.2 %collective-permute-start = (f32[64,2,8,128]{3,2,1,0:T(8,128)S(1)}, f32[64,2,8,128]{3,2,1,0:T(8,128)}, u32[]{:S(2)}, u32[]{:S(2)}) collective-permute-start(f32[64,2,8,128]{3,2,1,0:T(8,128)S(1)} %copy-done.1), channel_id=1, source_target_pairs={{0,752},{16,32},{32,16},{48,64},{64,48},{80,96},{96,80},{112,128},... | collective-permute-start | bytes 1572872 | tf_op jit(solution)/shard_map/ppermute | solution.py:129
  47.1 37.8 %all-to-all-done.3.own = f32[8,4,4,8,512]{4,3,2,1,0:T(8,128)S(1)} async-done(((f32[8,4,4,8,512]{4,3,2,1,0:T(8,128)}), f32[8,4,4,8,512]{4,3,2,1,0:T(8,128)S(1)}, u32[]{:S(2)}, u32[]{:S(2)}) %all-to-all-start.3) | async-done | bytes 2097184 | tf_op jit(solution)/shard_map/all_to_all | solution.py:115
  84.9 5.9 %collective-permute-start.4 = (f32[8,4,4,8,512]{4,3,2,1,0:T(8,128)S(1)}, f32[8,4,4,8,512]{4,3,2,1,0:T(8,128)S(1)}, u32[]{:S(2)}, u32[]{:S(2)}) collective-permute-start(f32[8,4,4,8,512]{4,3,2,1,0:T(8,128)S(1)} %all-to-all-done.3.own), channel_id=1, source_target_pairs={{0,16},{16,0},{1,17},{17,1},{2,18},{18,2},{3,19},{19,3},{4,20},{20... | collective-permute-start | bytes 6291464 | tf_op jit(solution)/shard_map/ppermute | solution.py:124
  90.8 0.0 collective-permute-done.1.refs_3_
  90.8 0.0 collective-permute-done.refs_2_
  90.8 0.0 copy-done.2
  90.8 2.2 %stencil.2.refs_1_ = f32[64,2,8,128]{3,2,1,0:T(8,128)S(1)} custom-call(s32[1]{0:T(128)} %bitcast.refs_0_.at_ref, f32[64,2,8,128]{3,2,1,0:T(8,128)S(1)} %copy-done.1, f32[64,2,8,128]{3,2,1,0:T(8,128)} %collective-permute-done.refs_2_, f32[64,2,8,128]{3,2,1,0:T(8,128)S(1)} %collective-permute-done.1.refs_3_, f32[2,8,128]{2,1,0:T(8,128)S(1)} %copy-done.2), custom_call_target="tpu_custom_call" | custom-call | tf_op jit(solution)/shard_map/stencil/pallas_call | solution.py:63
  93.0 1.9 %collective-permute-start.3 = (f32[64,2,8,128]{3,2,1,0:T(8,128)S(1)}, f32[64,2,8,128]{3,2,1,0:T(8,128)S(1)}, u32[]{:S(2)}, u32[]{:S(2)}) collective-permute-start(f32[64,2,8,128]{3,2,1,0:T(8,128)S(1)} %stencil.2.refs_1_), channel_id=1, source_target_pairs={{0,16},{16,0},{32,48},{48,32},{64,80},{80,64},{96,112},{112,96},{1... | collective-permute-start | bytes 1572872 | tf_op jit(solution)/shard_map/ppermute | solution.py:129
  94.9 5.1 %collective-permute-start.2 = (f32[64,2,8,128]{3,2,1,0:T(8,128)S(1)}, f32[64,2,8,128]{3,2,1,0:T(8,128)S(1)}, u32[]{:S(2)}, u32[]{:S(2)}) collective-permute-start(f32[64,2,8,128]{3,2,1,0:T(8,128)S(1)} %stencil.2.refs_1_), channel_id=1, source_target_pairs={{0,752},{16,32},{32,16},{48,64},{64,48},{80,96},{96,80},{112,128},... | collective-permute-start | bytes 1572872 | tf_op jit(solution)/shard_map/ppermute | solution.py:129
  100.0 0.0 collective-permute-done.3.refs_3_
  100.0 26.5 %collective-permute-done.2.refs_2_ = f32[64,2,8,128]{3,2,1,0:T(8,128)S(1)} collective-permute-done((f32[64,2,8,128]{3,2,1,0:T(8,128)S(1)}, f32[64,2,8,128]{3,2,1,0:T(8,128)S(1)}, u32[]{:S(2)}, u32[]{:S(2)}) %collective-permute-start.2) | collective-permute-done | bytes 524320 | tf_op jit(solution)/shard_map/ppermute | solution.py:129
  126.5 1.2 stencil.3
  127.7 18.3 %all_to_all.27 = f32[16,64,128]{2,1,0:T(8,128)S(1)} all-to-all(f32[16,64,128]{2,1,0:T(8,128)S(1)} %bitcast.8), channel_id=1, replica_groups=mesh['y'=8,'zh'=3,'c'=2,'x'=4,'zl'=4] {'x','zl'}, dimensions={0} | all-to-all | bytes 1048576 | tf_op jit(solution)/shard_map/all_to_all | solution.py:149
  146.0 0.0 collective-permute-done.4.other
  146.0 1.4 rotate.1
  147.4 18.8 %all_to_all.28 = f32[16,64,128]{2,1,0:T(8,128)S(1)} all-to-all(f32[16,64,128]{2,1,0:T(8,128)S(1)} %rotate.1), channel_id=1, replica_groups=mesh['y'=8,'zh'=3,'c'=2,'x'=4,'zl'=4] {'x','zl'}, dimensions={0} | all-to-all | bytes 1048576 | tf_op jit(solution)/shard_map/all_to_all | solution.py:151
  166.2 1.1 copy.4
  (3 shorter events, 0.0 us)
Async XLA Ops:
  0.0 1.0 copy-start
  24.1 7.0 %copy-start.1 = (f32[64,2,8,128]{3,2,1,0:T(8,128)S(1)}, f32[64,2,8,128]{3,2,1,0:T(8,128)}, u32[]{:S(2)}) copy-start(f32[64,2,8,128]{3,2,1,0:T(8,128)} %refs_5_.1) | copy-start | bytes 1572868
  24.1 66.7 %copy-start.2 = (f32[2,8,128]{2,1,0:T(8,128)S(1)}, f32[2,8,128]{2,1,0:T(8,128)}, u32[]{:S(2)}) copy-start(f32[2,8,128]{2,1,0:T(8,128)} %refs_4_.3) | copy-start | bytes 24580
  24.1 60.7 %all-to-all-start.3 = ((f32[8,4,4,8,512]{4,3,2,1,0:T(8,128)}), f32[8,4,4,8,512]{4,3,2,1,0:T(8,128)S(1)}, u32[]{:S(2)}, u32[]{:S(2)}) async-start(f32[8,4,4,8,512]{4,3,2,1,0:T(8,128)} %broadcast_in_dim.8), calls=%async_computation.3 | async-start | bytes 4194304 | tf_op jit(solution)/shard_map/all_to_all | solution.py:115
  31.1 59.7 %collective-permute-start.1 = (f32[64,2,8,128]{3,2,1,0:T(8,128)S(1)}, f32[64,2,8,128]{3,2,1,0:T(8,128)S(1)}, u32[]{:S(2)}, u32[]{:S(2)}) collective-permute-start(f32[64,2,8,128]{3,2,1,0:T(8,128)S(1)} %copy-done.1), channel_id=1, source_target_pairs={{0,16},{16,0},{32,48},{48,32},{64,80},{80,64},{96,112},{112,96},{1... | collective-permute-start | bytes 1572872 | tf_op jit(solution)/shard_map/ppermute | solution.py:129
  36.8 54.0 %collective-permute-start = (f32[64,2,8,128]{3,2,1,0:T(8,128)S(1)}, f32[64,2,8,128]{3,2,1,0:T(8,128)}, u32[]{:S(2)}, u32[]{:S(2)}) collective-permute-start(f32[64,2,8,128]{3,2,1,0:T(8,128)S(1)} %copy-done.1), channel_id=1, source_target_pairs={{0,752},{16,32},{32,16},{48,64},{64,48},{80,96},{96,80},{112,128},... | collective-permute-start | bytes 1572872 | tf_op jit(solution)/shard_map/ppermute | solution.py:129
  84.9 61.1 %collective-permute-start.4 = (f32[8,4,4,8,512]{4,3,2,1,0:T(8,128)S(1)}, f32[8,4,4,8,512]{4,3,2,1,0:T(8,128)S(1)}, u32[]{:S(2)}, u32[]{:S(2)}) collective-permute-start(f32[8,4,4,8,512]{4,3,2,1,0:T(8,128)S(1)} %all-to-all-done.3.own), channel_id=1, source_target_pairs={{0,16},{16,0},{1,17},{17,1},{2,18},{18,2},{3,19},{19,3},{4,20},{20... | collective-permute-start | bytes 6291464 | tf_op jit(solution)/shard_map/ppermute | solution.py:124
  93.0 7.0 %collective-permute-start.3 = (f32[64,2,8,128]{3,2,1,0:T(8,128)S(1)}, f32[64,2,8,128]{3,2,1,0:T(8,128)S(1)}, u32[]{:S(2)}, u32[]{:S(2)}) collective-permute-start(f32[64,2,8,128]{3,2,1,0:T(8,128)S(1)} %stencil.2.refs_1_), channel_id=1, source_target_pairs={{0,16},{16,0},{32,48},{48,32},{64,80},{80,64},{96,112},{112,96},{1... | collective-permute-start | bytes 1572872 | tf_op jit(solution)/shard_map/ppermute | solution.py:129
  94.9 31.6 %collective-permute-start.2 = (f32[64,2,8,128]{3,2,1,0:T(8,128)S(1)}, f32[64,2,8,128]{3,2,1,0:T(8,128)S(1)}, u32[]{:S(2)}, u32[]{:S(2)}) collective-permute-start(f32[64,2,8,128]{3,2,1,0:T(8,128)S(1)} %stencil.2.refs_1_), channel_id=1, source_target_pairs={{0,752},{16,32},{32,16},{48,64},{64,48},{80,96},{96,80},{112,128},... | collective-permute-start | bytes 1572872 | tf_op jit(solution)/shard_map/ppermute | solution.py:129

commit v7 on v6

--- a/solution.py
+++ b/solution.py
@@ -55,10 +55,10 @@
     return pltpu.with_memory_space_constraint(value, pltpu.VMEM)
 
 
-def stencil(par, own, outer, inner, pot, base=None):
+def stencil(par, own, outer, inner, pot, base=None, token=None):
     combine = base is not None
     orbs, planes, ny, nz = own.shape
-    args = (own, outer, inner, pot) + ((base,) if combine else ())
+    args = (own, outer, inner, pot) + ((base, token) if combine else ())
     shape = (planes, ny, orbs, nz) if combine else own.shape
     return pl.pallas_call(
         lambda *refs: stencil_kernel(combine, *refs),
@@ -71,9 +71,10 @@
     )(par, *map(in_vmem, args))
 
 
-def rotate_kernel(at_ref, v, own, other, out, wide):
-    core = at_ref[0]
-    ny, nx, nzl, rows, half = own.shape
+def rotate_kernel(at_ref, v, *refs):
+    pieces, out, wide = refs[:8], refs[8], refs[9]
+    core, y = at_ref[0], at_ref[1]
+    nx, nzl, rows, half = pieces[0].shape
     value = v[...]
     high = value.astype(jnp.bfloat16)
     low = (value - high.astype(jnp.float32)).astype(jnp.bfloat16)
@@ -81,7 +82,7 @@
     nz = v.shape[1]
 
     def product(piece, which):
-        piece = piece.reshape(ny * nzl * rows, half)
+        piece = piece[...].reshape(nx * nzl * rows, half)
         high = piece.astype(jnp.bfloat16)
         low = (piece - high.astype(jnp.float32)).astype(jnp.bfloat16)
         at = pl.ds(pl.multiple_of(which * half, half), half)
@@ -89,12 +90,11 @@
         rest = jnp.dot(low, wide[at, :nz], preferred_element_type=jnp.float32)
         return both[:, :nz] + both[:, nz:] + rest
 
-    for x in range(nx):
-        total = product(own[:, x], core) + product(other[:, x], 1 - core)
-        for y in range(ny):
-            for z in range(nzl):
-                at = (y * nzl + z) * rows
-                out[x * nzl + z, y * rows : (y + 1) * rows] = total[at : at + rows]
+    for j, step in enumerate((0, 3, 1, 2)):
+        total = product(pieces[2 * j], core) + product(pieces[2 * j + 1], 1 - core)
+        place = pl.ds(pl.multiple_of(lax.rem(y + step, 4) * rows, rows), rows)
+        for group in range(nx * nzl):
+            out[group, place] = total[group * rows : (group + 1) * rows]
 
 
 def rotate(at, v, pieces, shape):
@@ -116,13 +116,21 @@
 
 
 def gather_rotation(rot_t):
-    rows, cols = rot_t.shape[0] // lax.axis_size("y"), rot_t.shape[1] // 2
-    at = (lax.axis_index("y") * rows, lax.axis_index("c") * cols)
+    ny = lax.axis_size("y")
+    rows, cols = rot_t.shape[0] // 4, rot_t.shape[1] // 2
+    at = ((lax.axis_index("y") % 4) * rows, lax.axis_index("c") * cols)
+    up = [(i, (i + 1) % ny) for i in range(ny)]
+    down = [(j, i) for i, j in up]
     part = to_all(lax.dynamic_slice(rot_t, at, (rows, cols)), "zl")
-    part = to_all(part, "x")
-    own = to_all(part, "y")
-    other = lax.ppermute(own, "c", [(0, 1), (1, 0)])
-    return own, other
+    own = to_all(part, "x")
+    below = lax.ppermute(own, "y", up)
+    above = lax.ppermute(own, "y", down)
+    token = below[0, 0, :8, :128] * 2.0
+    far = lax.ppermute(below, "y", up)
+    pieces = []
+    for piece in (own, below, above, far):
+        pieces += [piece, lax.ppermute(piece, "c", [(0, 1), (1, 0)])]
+    return pieces, token
 
 
 def swap(value, pairs):
@@ -134,15 +142,15 @@
     outer_pairs = [(i, (i + 1 if i % 2 else i - 1) % devices) for i in range(devices)]
     inner_pairs = [(i, i ^ 1) for i in range(devices)]
     core = lax.axis_index("c")
-    at = core.astype(jnp.int32).reshape(1)
-    pieces = gather_rotation(rotation.T)
+    at = jnp.stack([core, lax.axis_index("y")]).astype(jnp.int32)
+    pieces, token = gather_rotation(rotation.T)
 
     outer = swap(orbitals, outer_pairs)
     inner = swap(orbitals, inner_pairs)
     first = stencil(at, orbitals, outer, inner, potential)
     outer = swap(first, outer_pairs)
     inner = swap(first, inner_pairs)
-    filtered = stencil(at, first, outer, inner, potential, orbitals)
+    filtered = stencil(at, first, outer, inner, potential, orbitals, token)
     orbs, planes, ny, nz = orbitals.shape
     groups = lax.axis_size(BAND)
     parts = filtered.reshape(groups, -1, nz)

time: 168 us -> 149 us (0.89)
  waiting for transfers between devices: 64.3 us -> 34 us
  starting transfers between devices: 35.8 us -> 64.6 us
  blocking collectives: 58.7 us -> 34.9 us
  local copies, waits for them, and re-layouts: 3.69 us -> 8.44 us
    all_to_all x1, waiting for transfers between devices: 37.8 us -> 0.01 us  [to_all(): return lax.all_to_all(copies, axis, 0, 0, tiled=True)]
    all_to_all x1 -> x0, blocking collectives: 18.3 us -> none  [per_device(): parts = lax.all_to_all(parts, BAND, 0, 0, tiled=True)]
    ppermute x1 -> x7, starting transfers between devices: 5.88 us -> 23.3 us  [the longest x4 14.5 us: gather_rotation(): pieces += [piece, lax.ppermute(piece, 'c', [(0, 1), (1, 0)])]]
    all_to_all x0 -> x1, starting transfers between devices: none -> 9.42 us  [per_device(): parts = lax.all_to_all(parts, BAND, 0, 0, tiled=True)]
    all_to_all x2 -> x1, blocking collectives: 21.5 us -> 12.4 us  [to_all(): return lax.all_to_all(copies, axis, 0, 0, tiled=True)]
    unnamed x6 -> x18, local copies, waits for them, and re-layouts: 0.96 us -> 6.47 us
    ppermute x4, starting transfers between devices: 23 us -> 27.7 us  [swap(): return lax.ppermute(value, GRID, pairs)]
    ppermute x4, waiting for transfers between devices: 26.5 us -> 31.2 us  [swap(): return lax.ppermute(value, GRID, pairs)]
  transfers between devices with their start and end apart: 6 -> 13, of which waited for: 2 -> 4; matrix products, arithmetic and copies ran while one was open for 0% -> 0% of each run, Pallas kernels for 2% -> 1%
where the time goes in v7:
time: 149 us; the launch traced here: 148 us
  starting transfers between devices  64.6 us (43%)
  blocking collectives  34.9 us (23%)
  waiting for transfers between devices  34 us (23%)
  local copies, waits for them, and re-layouts  8.44 us (6%)
  Pallas kernels  6.13 us (4%)
    ppermute x4, waiting for transfers between devices, swap(): return lax.ppermute(value, GRID, pairs)  31.2 us
    ppermute x4, starting transfers between devices, swap(): return lax.ppermute(value, GRID, pairs)  27.7 us
    all_to_all x1, blocking collectives, per_device(): back = lax.all_to_all(mixed, BAND, 0, 0, tiled=True)  22.5 us
    ppermute x4, starting transfers between devices, gather_rotation(): pieces += [piece, lax.ppermute(piece, 'c', [(0, 1), (1, 0)])]  14.5 us
    all_to_all x1, blocking collectives, to_all(): return lax.all_to_all(copies, axis, 0, 0, tiled=True)  12.4 us
    all_to_all x1, starting transfers between devices, per_device(): parts = lax.all_to_all(parts, BAND, 0, 0, tiled=True)  9.42 us
    unnamed x18, local copies, waits for them, and re-layouts  6.47 us
    ppermute x1, starting transfers between devices, gather_rotation(): above = lax.ppermute(own, 'y', down)  4.93 us
  transfers between devices with their start and end apart: 13, of which 4 were waited for; matrix products, arithmetic and copies ran while one was open for 0% of the time, Pallas kernels for 1%

profile of v7, /device:TPU:1, one launch (start us, length us, event | category | flops | bytes accessed | tf_op | source)
XLA Modules:
  0.0 148.4 jit_solution(8975301504693279499)
XLA Ops:
  0.0 0.0 copy-start
  0.0 0.9 copy-done
  1.0 12.4 %all_to_all.20 = f32[4,16,512]{2,1,0:T(8,128)S(1)} all-to-all(f32[4,16,512]{2,1,0:T(8,128)S(1)} %broadcast_in_dim.4), channel_id=1, replica_groups=mesh['y'=8,'zh'=3,'c'=2,'x'=4,'zl'=4] {'zl'}, dimensions={0} | all-to-all | bytes 262144 | tf_op jit(solution)/shard_map/all_to_all | solution.py:115
  13.3 0.9 broadcast_in_dim.5
  14.2 0.0 copy-start.1
  14.2 0.0 copy-start.8
  14.2 4.1 %all-to-all-start.1 = ((f32[4,4,16,512]{3,2,1,0:T(8,128)}), f32[4,4,16,512]{3,2,1,0:T(8,128)S(1)}, u32[]{:S(2)}, u32[]{:S(2)}) async-start(f32[4,4,16,512]{3,2,1,0:T(8,128)} %broadcast_in_dim.5), calls=%async_computation.1 | async-start | bytes 1048576 | tf_op jit(solution)/shard_map/all_to_all | solution.py:115
  18.3 0.0 copy-done.1
  18.3 12.8 %collective-permute-start = (f32[64,2,8,128]{3,2,1,0:T(8,128)S(1)}, f32[64,2,8,128]{3,2,1,0:T(8,128)S(1)}, u32[]{:S(2)}, u32[]{:S(2)}) collective-permute-start(f32[64,2,8,128]{3,2,1,0:T(8,128)S(1)} %copy-done.1), channel_id=1, source_target_pairs={{0,752},{16,32},{32,16},{48,64},{64,48},{80,96},{96,80},{112,128},... | collective-permute-start | bytes 1572872 | tf_op jit(solution)/shard_map/ppermute | solution.py:137
  31.1 4.0 %collective-permute-start.1 = (f32[64,2,8,128]{3,2,1,0:T(8,128)S(1)}, f32[64,2,8,128]{3,2,1,0:T(8,128)S(1)}, u32[]{:S(2)}, u32[]{:S(2)}) collective-permute-start(f32[64,2,8,128]{3,2,1,0:T(8,128)S(1)} %copy-done.1), channel_id=1, source_target_pairs={{0,16},{16,0},{32,48},{48,32},{64,80},{80,64},{96,112},{112,96},{1... | collective-permute-start | bytes 1572872 | tf_op jit(solution)/shard_map/ppermute | solution.py:137
  35.1 0.0 all-to-all-done.1.refs_0_
  35.1 1.9 %collective-permute-start.4 = (f32[4,4,16,512]{3,2,1,0:T(8,128)S(1)}, f32[4,4,16,512]{3,2,1,0:T(8,128)S(1)}, u32[]{:S(2)}, u32[]{:S(2)}) collective-permute-start(f32[4,4,16,512]{3,2,1,0:T(8,128)S(1)} %all-to-all-done.1.refs_0_), channel_id=1, source_target_pairs={{0,96},{96,192},{192,288},{288,384},{384,480},{480,576},{576,672},... | collective-permute-start | bytes 1572872 | tf_op jit(solution)/shard_map/ppermute | solution.py:126
  37.1 0.1 pad_add_fusion.refs_0_.at_ref
  37.1 17.8 %collective-permute-done.refs_2_ = f32[64,2,8,128]{3,2,1,0:T(8,128)S(1)} collective-permute-done((f32[64,2,8,128]{3,2,1,0:T(8,128)S(1)}, f32[64,2,8,128]{3,2,1,0:T(8,128)S(1)}, u32[]{:S(2)}, u32[]{:S(2)}) %collective-permute-start) | collective-permute-done | bytes 524320 | tf_op jit(solution)/shard_map/ppermute | solution.py:137
  54.9 0.0 collective-permute-done.1.refs_3_
  54.9 0.0 copy-done.8
  54.9 1.7 %stencil.2.refs_1_ = f32[64,2,8,128]{3,2,1,0:T(8,128)S(1)} custom-call(s32[2]{0:T(128)S(1)} %pad_add_fusion.refs_0_.at_ref, f32[64,2,8,128]{3,2,1,0:T(8,128)S(1)} %copy-done.1, f32[64,2,8,128]{3,2,1,0:T(8,128)S(1)} %collective-permute-done.refs_2_, f32[64,2,8,128]{3,2,1,0:T(8,128)S(1)} %collective-permute-done.1.refs_3_, f32[2,8,128]{2,1,0:T(8,128)S(1)} %copy-done.8), custom_call_target="tpu_custom_call" | custom-call | tf_op jit(solution)/shard_map/stencil/pallas_call | solution.py:63
  56.6 6.2 %collective-permute-start.2 = (f32[64,2,8,128]{3,2,1,0:T(8,128)S(1)}, f32[64,2,8,128]{3,2,1,0:T(8,128)S(1)}, u32[]{:S(2)}, u32[]{:S(2)}) collective-permute-start(f32[64,2,8,128]{3,2,1,0:T(8,128)S(1)} %stencil.2.refs_1_), channel_id=1, source_target_pairs={{0,752},{16,32},{32,16},{48,64},{64,48},{80,96},{96,80},{112,128},... | collective-permute-start | bytes 1572872 | tf_op jit(solution)/shard_map/ppermute | solution.py:137
  62.8 4.8 %collective-permute-start.3 = (f32[64,2,8,128]{3,2,1,0:T(8,128)S(1)}, f32[64,2,8,128]{3,2,1,0:T(8,128)S(1)}, u32[]{:S(2)}, u32[]{:S(2)}) collective-permute-start(f32[64,2,8,128]{3,2,1,0:T(8,128)S(1)} %stencil.2.refs_1_), channel_id=1, source_target_pairs={{0,16},{16,0},{32,48},{48,32},{64,80},{80,64},{96,112},{112,96},{1... | collective-permute-start | bytes 1572872 | tf_op jit(solution)/shard_map/ppermute | solution.py:137
  67.5 0.0 collective-permute-done.4.refs_2_
  67.6 13.4 %collective-permute-done.2.refs_2_ = f32[64,2,8,128]{3,2,1,0:T(8,128)S(1)} collective-permute-done((f32[64,2,8,128]{3,2,1,0:T(8,128)S(1)}, f32[64,2,8,128]{3,2,1,0:T(8,128)S(1)}, u32[]{:S(2)}, u32[]{:S(2)}) %collective-permute-start.2) | collective-permute-done | bytes 524320 | tf_op jit(solution)/shard_map/ppermute | solution.py:137
  81.0 0.0 collective-permute-done.3.refs_3_
  81.0 2.5 %stencil.3 = f32[2,8,64,128]{3,2,1,0:T(8,128)} custom-call(s32[2]{0:T(128)S(1)} %pad_add_fusion.refs_0_.at_ref, f32[64,2,8,128]{3,2,1,0:T(8,128)S(1)} %stencil.2.refs_1_, f32[64,2,8,128]{3,2,1,0:T(8,128)S(1)} %collective-permute-done.2.refs_2_, f32[64,2,8,128]{3,2,1,0:T(8,128)S(1)} %collective-permute-done.3.refs_3_, f32[2,8,128]{2,1,0:T(8,128)S(1)} %copy-done.8, ...), custom_call_target="tpu_custom_call" | custom-call | tf_op jit(solution)/shard_map/stencil/pallas_call | solution.py:63
  83.5 9.4 %all-to-all-start.2 = ((f32[16,64,128]{2,1,0:T(8,128)}), f32[16,64,128]{2,1,0:T(8,128)S(1)}, u32[]{:S(2)}, u32[]{:S(2)}) async-start(f32[16,64,128]{2,1,0:T(8,128)} %bitcast.4), calls=%async_computation.2 | async-start | bytes 1048576 | tf_op jit(solution)/shard_map/all_to_all | solution.py:157
  92.9 4.9 %collective-permute-start.7 = (f32[4,4,16,512]{3,2,1,0:T(8,128)S(1)}, f32[4,4,16,512]{3,2,1,0:T(8,128)S(1)}, u32[]{:S(2)}, u32[]{:S(2)}) collective-permute-start(f32[4,4,16,512]{3,2,1,0:T(8,128)S(1)} %all-to-all-done.1.refs_0_), channel_id=1, source_target_pairs={{96,0},{192,96},{288,192},{384,288},{480,384},{576,480},{672,576},... | collective-permute-start | bytes 1572872 | tf_op jit(solution)/shard_map/ppermute | solution.py:127
  97.9 1.9 %collective-permute-start.9 = (f32[4,4,16,512]{3,2,1,0:T(8,128)S(1)}, f32[4,4,16,512]{3,2,1,0:T(8,128)S(1)}, u32[]{:S(2)}, u32[]{:S(2)}) collective-permute-start(f32[4,4,16,512]{3,2,1,0:T(8,128)S(1)} %collective-permute-done.4.refs_2_), channel_id=1, source_target_pairs={{0,96},{96,192},{192,288},{288,384},{384,480},{480,576},{576,672},... | collective-permute-start | bytes 1572872 | tf_op jit(solution)/shard_map/ppermute | solution.py:129
  99.8 4.6 %collective-permute-start.5 = (f32[4,4,16,512]{3,2,1,0:T(8,128)S(1)}, f32[4,4,16,512]{3,2,1,0:T(8,128)S(1)}, u32[]{:S(2)}, u32[]{:S(2)}) collective-permute-start(f32[4,4,16,512]{3,2,1,0:T(8,128)S(1)} %all-to-all-done.1.refs_0_), channel_id=1, source_target_pairs={{0,16},{16,0},{1,17},{17,1},{2,18},{18,2},{3,19},{19,3},{4,20},{20... | collective-permute-start | bytes 1572872 | tf_op jit(solution)/shard_map/ppermute | solution.py:132
  104.4 1.9 %collective-permute-start.6 = (f32[4,4,16,512]{3,2,1,0:T(8,128)S(1)}, f32[4,4,16,512]{3,2,1,0:T(8,128)S(1)}, u32[]{:S(2)}, u32[]{:S(2)}) collective-permute-start(f32[4,4,16,512]{3,2,1,0:T(8,128)S(1)} %collective-permute-done.4.refs_2_), channel_id=1, source_target_pairs={{0,16},{16,0},{1,17},{17,1},{2,18},{18,2},{3,19},{19,3},{4,20},{20... | collective-permute-start | bytes 1572872 | tf_op jit(solution)/shard_map/ppermute | solution.py:132
  106.3 1.7 %collective-permute-done.7.refs_4_ = f32[4,4,16,512]{3,2,1,0:T(8,128)S(1)} collective-permute-done((f32[4,4,16,512]{3,2,1,0:T(8,128)S(1)}, f32[4,4,16,512]{3,2,1,0:T(8,128)S(1)}, u32[]{:S(2)}, u32[]{:S(2)}) %collective-permute-start.7) | collective-permute-done | bytes 524320 | tf_op jit(solution)/shard_map/ppermute | solution.py:127
  108.0 3.9 %collective-permute-start.8 = (f32[4,4,16,512]{3,2,1,0:T(8,128)S(1)}, f32[4,4,16,512]{3,2,1,0:T(8,128)S(1)}, u32[]{:S(2)}, u32[]{:S(2)}) collective-permute-start(f32[4,4,16,512]{3,2,1,0:T(8,128)S(1)} %collective-permute-done.7.refs_4_), channel_id=1, source_target_pairs={{0,16},{16,0},{1,17},{17,1},{2,18},{18,2},{3,19},{19,3},{4,20},{20... | collective-permute-start | bytes 1572872 | tf_op jit(solution)/shard_map/ppermute | solution.py:132
  111.9 1.2 collective-permute-done.9.refs_6_
  113.1 4.1 %collective-permute-start.10 = (f32[4,4,16,512]{3,2,1,0:T(8,128)S(1)}, f32[4,4,16,512]{3,2,1,0:T(8,128)S(1)}, u32[]{:S(2)}, u32[]{:S(2)}) collective-permute-start(f32[4,4,16,512]{3,2,1,0:T(8,128)S(1)} %collective-permute-done.9.refs_6_), channel_id=1, source_target_pairs={{0,16},{16,0},{1,17},{17,1},{2,18},{18,2},{3,19},{19,3},{4,20},{20... | collective-permute-start | bytes 1572872 | tf_op jit(solution)/shard_map/ppermute | solution.py:132
  117.2 0.0 collective-permute-done.5.refs_1_
  117.2 0.0 collective-permute-done.6.refs_3_
  117.2 0.0 copy-start.2
  117.2 0.8 copy-done.2
  118.0 0.0 collective-permute-done.8.refs_5_
  118.0 0.0 copy-start.4
  118.0 0.8 copy-done.4
  118.8 0.0 collective-permute-done.10.refs_7_
  118.8 0.8 copy-done.6
  119.6 0.0 all-to-all-done.2
  119.6 1.0 copy-done.3
  120.7 1.0 copy-done.5
  121.7 1.0 copy-done.7
  122.8 1.9 %rotate.1 = f32[16,64,128]{2,1,0:T(8,128)S(1)} custom-call(s32[2]{0:T(128)S(1)} %pad_add_fusion.refs_0_.at_ref, f32[1024,128]{1,0:T(8,128)S(1)} %bitcast.11, f32[4,4,16,512]{3,2,1,0:T(8,128)S(1)} %all-to-all-done.1.refs_0_, f32[4,4,16,512]{3,2,1,0:T(8,128)S(1)} %collective-permute-done.5.refs_1_, f32[4,4,16,512]{3,2,1,0:T(8,128)S(1)} %collective-permute-done.4.refs_2_, ...), custom_call_target="tpu_custom_call" | custom-call | tf_op jit(solution)/shard_map/rotate/pallas_call | solution.py:101
  124.7 22.5 %all_to_all.21 = f32[16,64,128]{2,1,0:T(8,128)S(1)} all-to-all(f32[16,64,128]{2,1,0:T(8,128)S(1)} %rotate.1), channel_id=1, replica_groups=mesh['y'=8,'zh'=3,'c'=2,'x'=4,'zl'=4] {'x','zl'}, dimensions={0} | all-to-all | bytes 1048576 | tf_op jit(solution)/shard_map/all_to_all | solution.py:159
  147.3 1.1 copy.4
  (7 shorter events, 0.0 us)
Async XLA Ops:
  0.0 1.0 copy-start
  14.2 4.2 %copy-start.1 = (f32[64,2,8,128]{3,2,1,0:T(8,128)S(1)}, f32[64,2,8,128]{3,2,1,0:T(8,128)}, u32[]{:S(2)}) copy-start(f32[64,2,8,128]{3,2,1,0:T(8,128)} %refs_5_.1) | copy-start | bytes 1572868
  14.2 40.7 %copy-start.8 = (f32[2,8,128]{2,1,0:T(8,128)S(1)}, f32[2,8,128]{2,1,0:T(8,128)}, u32[]{:S(2)}) copy-start(f32[2,8,128]{2,1,0:T(8,128)} %refs_4_.3) | copy-start | bytes 24580
  14.2 20.9 %all-to-all-start.1 = ((f32[4,4,16,512]{3,2,1,0:T(8,128)}), f32[4,4,16,512]{3,2,1,0:T(8,128)S(1)}, u32[]{:S(2)}, u32[]{:S(2)}) async-start(f32[4,4,16,512]{3,2,1,0:T(8,128)} %broadcast_in_dim.5), calls=%async_computation.1 | async-start | bytes 1048576 | tf_op jit(solution)/shard_map/all_to_all | solution.py:115
  18.3 36.6 %collective-permute-start = (f32[64,2,8,128]{3,2,1,0:T(8,128)S(1)}, f32[64,2,8,128]{3,2,1,0:T(8,128)S(1)}, u32[]{:S(2)}, u32[]{:S(2)}) collective-permute-start(f32[64,2,8,128]{3,2,1,0:T(8,128)S(1)} %copy-done.1), channel_id=1, source_target_pairs={{0,752},{16,32},{32,16},{48,64},{64,48},{80,96},{96,80},{112,128},... | collective-permute-start | bytes 1572872 | tf_op jit(solution)/shard_map/ppermute | solution.py:137
  31.1 23.8 %collective-permute-start.1 = (f32[64,2,8,128]{3,2,1,0:T(8,128)S(1)}, f32[64,2,8,128]{3,2,1,0:T(8,128)S(1)}, u32[]{:S(2)}, u32[]{:S(2)}) collective-permute-start(f32[64,2,8,128]{3,2,1,0:T(8,128)S(1)} %copy-done.1), channel_id=1, source_target_pairs={{0,16},{16,0},{32,48},{48,32},{64,80},{80,64},{96,112},{112,96},{1... | collective-permute-start | bytes 1572872 | tf_op jit(solution)/shard_map/ppermute | solution.py:137
  35.1 32.4 %collective-permute-start.4 = (f32[4,4,16,512]{3,2,1,0:T(8,128)S(1)}, f32[4,4,16,512]{3,2,1,0:T(8,128)S(1)}, u32[]{:S(2)}, u32[]{:S(2)}) collective-permute-start(f32[4,4,16,512]{3,2,1,0:T(8,128)S(1)} %all-to-all-done.1.refs_0_), channel_id=1, source_target_pairs={{0,96},{96,192},{192,288},{288,384},{384,480},{480,576},{576,672},... | collective-permute-start | bytes 1572872 | tf_op jit(solution)/shard_map/ppermute | solution.py:126
  56.6 24.4 %collective-permute-start.2 = (f32[64,2,8,128]{3,2,1,0:T(8,128)S(1)}, f32[64,2,8,128]{3,2,1,0:T(8,128)S(1)}, u32[]{:S(2)}, u32[]{:S(2)}) collective-permute-start(f32[64,2,8,128]{3,2,1,0:T(8,128)S(1)} %stencil.2.refs_1_), channel_id=1, source_target_pairs={{0,752},{16,32},{32,16},{48,64},{64,48},{80,96},{96,80},{112,128},... | collective-permute-start | bytes 1572872 | tf_op jit(solution)/shard_map/ppermute | solution.py:137
  62.8 18.2 %collective-permute-start.3 = (f32[64,2,8,128]{3,2,1,0:T(8,128)S(1)}, f32[64,2,8,128]{3,2,1,0:T(8,128)S(1)}, u32[]{:S(2)}, u32[]{:S(2)}) collective-permute-start(f32[64,2,8,128]{3,2,1,0:T(8,128)S(1)} %stencil.2.refs_1_), channel_id=1, source_target_pairs={{0,16},{16,0},{32,48},{48,32},{64,80},{80,64},{96,112},{112,96},{1... | collective-permute-start | bytes 1572872 | tf_op jit(solution)/shard_map/ppermute | solution.py:137
  83.5 36.1 %all-to-all-start.2 = ((f32[16,64,128]{2,1,0:T(8,128)}), f32[16,64,128]{2,1,0:T(8,128)S(1)}, u32[]{:S(2)}, u32[]{:S(2)}) async-start(f32[16,64,128]{2,1,0:T(8,128)} %bitcast.4), calls=%async_computation.2 | async-start | bytes 1048576 | tf_op jit(solution)/shard_map/all_to_all | solution.py:157
  92.9 15.1 %collective-permute-start.7 = (f32[4,4,16,512]{3,2,1,0:T(8,128)S(1)}, f32[4,4,16,512]{3,2,1,0:T(8,128)S(1)}, u32[]{:S(2)}, u32[]{:S(2)}) collective-permute-start(f32[4,4,16,512]{3,2,1,0:T(8,128)S(1)} %all-to-all-done.1.refs_0_), channel_id=1, source_target_pairs={{96,0},{192,96},{288,192},{384,288},{480,384},{576,480},{672,576},... | collective-permute-start | bytes 1572872 | tf_op jit(solution)/shard_map/ppermute | solution.py:127
  97.9 15.2 %collective-permute-start.9 = (f32[4,4,16,512]{3,2,1,0:T(8,128)S(1)}, f32[4,4,16,512]{3,2,1,0:T(8,128)S(1)}, u32[]{:S(2)}, u32[]{:S(2)}) collective-permute-start(f32[4,4,16,512]{3,2,1,0:T(8,128)S(1)} %collective-permute-done.4.refs_2_), channel_id=1, source_target_pairs={{0,96},{96,192},{192,288},{288,384},{384,480},{480,576},{576,672},... | collective-permute-start | bytes 1572872 | tf_op jit(solution)/shard_map/ppermute | solution.py:129
  99.8 17.4 %collective-permute-start.5 = (f32[4,4,16,512]{3,2,1,0:T(8,128)S(1)}, f32[4,4,16,512]{3,2,1,0:T(8,128)S(1)}, u32[]{:S(2)}, u32[]{:S(2)}) collective-permute-start(f32[4,4,16,512]{3,2,1,0:T(8,128)S(1)} %all-to-all-done.1.refs_0_), channel_id=1, source_target_pairs={{0,16},{16,0},{1,17},{17,1},{2,18},{18,2},{3,19},{19,3},{4,20},{20... | collective-permute-start | bytes 1572872 | tf_op jit(solution)/shard_map/ppermute | solution.py:132
  104.4 12.8 %collective-permute-start.6 = (f32[4,4,16,512]{3,2,1,0:T(8,128)S(1)}, f32[4,4,16,512]{3,2,1,0:T(8,128)S(1)}, u32[]{:S(2)}, u32[]{:S(2)}) collective-permute-start(f32[4,4,16,512]{3,2,1,0:T(8,128)S(1)} %collective-permute-done.4.refs_2_), channel_id=1, source_target_pairs={{0,16},{16,0},{1,17},{17,1},{2,18},{18,2},{3,19},{19,3},{4,20},{20... | collective-permute-start | bytes 1572872 | tf_op jit(solution)/shard_map/ppermute | solution.py:132
  108.0 10.0 %collective-permute-start.8 = (f32[4,4,16,512]{3,2,1,0:T(8,128)S(1)}, f32[4,4,16,512]{3,2,1,0:T(8,128)S(1)}, u32[]{:S(2)}, u32[]{:S(2)}) collective-permute-start(f32[4,4,16,512]{3,2,1,0:T(8,128)S(1)} %collective-permute-done.7.refs_4_), channel_id=1, source_target_pairs={{0,16},{16,0},{1,17},{17,1},{2,18},{18,2},{3,19},{19,3},{4,20},{20... | collective-permute-start | bytes 1572872 | tf_op jit(solution)/shard_map/ppermute | solution.py:132
  113.1 5.8 %collective-permute-start.10 = (f32[4,4,16,512]{3,2,1,0:T(8,128)S(1)}, f32[4,4,16,512]{3,2,1,0:T(8,128)S(1)}, u32[]{:S(2)}, u32[]{:S(2)}) collective-permute-start(f32[4,4,16,512]{3,2,1,0:T(8,128)S(1)} %collective-permute-done.9.refs_6_), channel_id=1, source_target_pairs={{0,16},{16,0},{1,17},{17,1},{2,18},{18,2},{3,19},{19,3},{4,20},{20... | collective-permute-start | bytes 1572872 | tf_op jit(solution)/shard_map/ppermute | solution.py:132
  117.2 0.8 copy-start.2
  118.0 0.8 copy-start.4
  118.8 0.8 copy-start.6
  119.6 1.0 copy-start.3
  120.7 1.0 copy-start.5
  121.7 1.0 copy-start.7

commit v8 on v7

--- a/solution.py
+++ b/solution.py
@@ -7,6 +7,7 @@
 from jax.sharding import Mesh, PartitionSpec as P
 
 GROUP = 8
+LATE = (7,)
 GRID = ("y", "zh", "c")
 BAND = ("x", "zl")
 
@@ -72,7 +73,12 @@
 
 
 def rotate_kernel(at_ref, v, *refs):
-    pieces, out, wide = refs[:8], refs[8], refs[9]
+    pieces, out, wide, landed, sems = list(refs[:8]), *refs[8:]
+    copies = {}
+    for slot, at in enumerate(LATE):
+        copies[at] = pltpu.make_async_copy(pieces[at], landed.at[slot], sems.at[slot])
+        copies[at].start()
+        pieces[at] = landed.at[slot]
     core, y = at_ref[0], at_ref[1]
     nx, nzl, rows, half = pieces[0].shape
     value = v[...]
@@ -91,7 +97,10 @@
         return both[:, :nz] + both[:, nz:] + rest
 
     for j, step in enumerate((0, 3, 1, 2)):
-        total = product(pieces[2 * j], core) + product(pieces[2 * j + 1], 1 - core)
+        total = product(pieces[2 * j], core)
+        if 2 * j + 1 in copies:
+            copies[2 * j + 1].wait()
+        total += product(pieces[2 * j + 1], 1 - core)
         place = pl.ds(pl.multiple_of(lax.rem(y + step, 4) * rows, rows), rows)
         for group in range(nx * nzl):
             out[group, place] = total[group * rows : (group + 1) * rows]
@@ -101,13 +110,42 @@
     return pl.pallas_call(
         rotate_kernel,
         out_shape=pltpu.VMEM(shape, v.dtype),
-        in_specs=[pl.BlockSpec(memory_space=pltpu.SMEM)]
-        + [pl.BlockSpec(memory_space=pltpu.VMEM)] * (1 + len(pieces)),
+        in_specs=[pl.BlockSpec(memory_space=pltpu.SMEM), pl.BlockSpec(memory_space=pltpu.VMEM)]
+        + [pl.BlockSpec(memory_space=pltpu.HBM if at in LATE else pltpu.VMEM) for at in range(len(pieces))],
         out_specs=pl.BlockSpec(memory_space=pltpu.VMEM),
-        scratch_shapes=[pltpu.VMEM((v.shape[0], 2 * v.shape[1]), jnp.bfloat16)],
+        scratch_shapes=[
+            pltpu.VMEM((v.shape[0], 2 * v.shape[1]), jnp.bfloat16),
+            pltpu.VMEM((len(LATE), *pieces[0].shape), jnp.float32),
+            pltpu.SemaphoreType.DMA((len(LATE),)),
+        ],
         compiler_params=pltpu.CompilerParams(vmem_limit_bytes=24 << 20),
         name="rotate",
-    )(at, *map(in_vmem, (v, *pieces)))
+    )(at, in_vmem(v), *(pltpu.with_memory_space_constraint(p, pltpu.HBM) if i in LATE else in_vmem(p) for i, p in enumerate(pieces)))
+
+
+def pick_kernel(at_ref, source, out, sems):
+    copies, rows, cols = out.shape
+    at = (
+        pl.ds(pl.multiple_of(lax.rem(at_ref[1], 4) * rows, rows), rows),
+        pl.ds(pl.multiple_of(at_ref[0] * cols, cols), cols),
+    )
+    moves = [pltpu.make_async_copy(source.at[at], out.at[i], sems.at[i]) for i in range(copies)]
+    for move in moves:
+        move.start()
+    for move in moves:
+        move.wait()
+
+
+def pick(at, source, shape):
+    return pl.pallas_call(
+        pick_kernel,
+        out_shape=pltpu.VMEM(shape, source.dtype),
+        in_specs=[pl.BlockSpec(memory_space=pltpu.SMEM), pl.BlockSpec(memory_space=pltpu.HBM)],
+        out_specs=pl.BlockSpec(memory_space=pltpu.VMEM),
+        scratch_shapes=[pltpu.SemaphoreType.DMA((shape[0],))],
+        compiler_params=pltpu.CompilerParams(vmem_limit_bytes=1 << 20),
+        name="pick",
+    )(at, pltpu.with_memory_space_constraint(source, pltpu.HBM))
 
 
 def to_all(value, axis):
@@ -115,13 +153,13 @@
     return lax.all_to_all(copies, axis, 0, 0, tiled=True)
 
 
-def gather_rotation(rot_t):
+def gather_rotation(at, rot_t):
     ny = lax.axis_size("y")
     rows, cols = rot_t.shape[0] // 4, rot_t.shape[1] // 2
-    at = ((lax.axis_index("y") % 4) * rows, lax.axis_index("c") * cols)
     up = [(i, (i + 1) % ny) for i in range(ny)]
     down = [(j, i) for i, j in up]
-    part = to_all(lax.dynamic_slice(rot_t, at, (rows, cols)), "zl")
+    part = pick(at, rot_t, (lax.axis_size("zl"), rows, cols))
+    part = lax.all_to_all(part, "zl", 0, 0, tiled=True)
     own = to_all(part, "x")
     below = lax.ppermute(own, "y", up)
     above = lax.ppermute(own, "y", down)
@@ -143,7 +181,7 @@
     inner_pairs = [(i, i ^ 1) for i in range(devices)]
     core = lax.axis_index("c")
     at = jnp.stack([core, lax.axis_index("y")]).astype(jnp.int32)
-    pieces, token = gather_rotation(rotation.T)
+    pieces, token = gather_rotation(at, rotation.T)
 
     outer = swap(orbitals, outer_pairs)
     inner = swap(orbitals, inner_pairs)

time: 149 us -> 149 us (level)
  local copies, waits for them, and re-layouts: 8.44 us -> 5.65 us
  Pallas kernels: 6.13 us -> 8.74 us
    unnamed x18 -> x12, local copies, waits for them, and re-layouts: 6.47 us -> 3.69 us
    pallas_call x0 -> x1, Pallas kernels: none -> 1.51 us  [pick(): pl.pallas_call(pick_kernel, out_shape=pltpu.VMEM(shape, source.dtype), in...]
where the time goes in v8:
time: 149 us; the launch traced here: 148 us
  starting transfers between devices  64.6 us (43%)
  blocking collectives  34.9 us (23%)
  waiting for transfers between devices  34.1 us (23%)
  Pallas kernels  8.74 us (6%)
  local copies, waits for them, and re-layouts  5.65 us (4%)
    ppermute x4, waiting for transfers between devices, swap(): return lax.ppermute(value, GRID, pairs)  31.2 us
    ppermute x4, starting transfers between devices, swap(): return lax.ppermute(value, GRID, pairs)  27.7 us
    all_to_all x1, blocking collectives, per_device(): back = lax.all_to_all(mixed, BAND, 0, 0, tiled=True)  22.5 us
    ppermute x4, starting transfers between devices, gather_rotation(): pieces += [piece, lax.ppermute(piece, 'c', [(0, 1), (1, 0)])]  14.5 us
    all_to_all x1, blocking collectives, gather_rotation(): part = lax.all_to_all(part, 'zl', 0, 0, tiled=True)  12.4 us
    all_to_all x1, starting transfers between devices, per_device(): parts = lax.all_to_all(parts, BAND, 0, 0, tiled=True)  9.5 us
    ppermute x1, starting transfers between devices, gather_rotation(): above = lax.ppermute(own, 'y', down)  4.85 us
    pallas_call x2, Pallas kernels, stencil(): pl.pallas_call(lambda *refs: stencil_kernel(combine, *refs), out_shape=pl...  4.19 us
  transfers between devices with their start and end apart: 13, of which 4 were waited for; matrix products, arithmetic and copies ran while one was open for 0% of the time, Pallas kernels for 1%

profile of v8, /device:TPU:1, one launch (start us, length us, event | category | flops | bytes accessed | tf_op | source)
XLA Modules:
  0.0 148.2 jit_solution(10779447029253070731)
XLA Ops:
  0.0 0.1 pad_add_fusion.refs_0_.at_ref
  0.1 1.5 %pick.1 = f32[4,16,512]{2,1,0:T(8,128)S(1)} custom-call(s32[2]{0:T(128)S(1)} %pad_add_fusion.refs_0_.at_ref, f32[64,1024]{1,0:T(8,128)} %bitcast.12), custom_call_target="tpu_custom_call" | custom-call | tf_op jit(solution)/shard_map/pick/pallas_call | solution.py:140
  1.6 12.4 %all_to_all.20 = f32[4,16,512]{2,1,0:T(8,128)S(1)} all-to-all(f32[4,16,512]{2,1,0:T(8,128)S(1)} %pick.1), channel_id=1, replica_groups=mesh['y'=8,'zh'=3,'c'=2,'x'=4,'zl'=4] {'zl'}, dimensions={0} | all-to-all | bytes 262144 | tf_op jit(solution)/shard_map/all_to_all | solution.py:162
  14.0 0.9 broadcast_in_dim.2
  14.8 0.0 copy-start
  14.8 0.0 copy-start.5
  14.8 4.1 %all-to-all-start.1 = ((f32[4,4,16,512]{3,2,1,0:T(8,128)}), f32[4,4,16,512]{3,2,1,0:T(8,128)S(1)}, u32[]{:S(2)}, u32[]{:S(2)}) async-start(f32[4,4,16,512]{3,2,1,0:T(8,128)} %broadcast_in_dim.2), calls=%async_computation.1 | async-start | bytes 1048576 | tf_op jit(solution)/shard_map/all_to_all | solution.py:153
  19.0 0.0 copy-done
  19.0 12.8 %collective-permute-start = (f32[64,2,8,128]{3,2,1,0:T(8,128)S(1)}, f32[64,2,8,128]{3,2,1,0:T(8,128)S(1)}, u32[]{:S(2)}, u32[]{:S(2)}) collective-permute-start(f32[64,2,8,128]{3,2,1,0:T(8,128)S(1)} %copy-done), channel_id=1, source_target_pairs={{0,752},{16,32},{32,16},{48,64},{64,48},{80,96},{96,80},{112,128},... | collective-permute-start | bytes 1572872 | tf_op jit(solution)/shard_map/ppermute | solution.py:175
  31.7 4.0 %collective-permute-start.1 = (f32[64,2,8,128]{3,2,1,0:T(8,128)S(1)}, f32[64,2,8,128]{3,2,1,0:T(8,128)S(1)}, u32[]{:S(2)}, u32[]{:S(2)}) collective-permute-start(f32[64,2,8,128]{3,2,1,0:T(8,128)S(1)} %copy-done), channel_id=1, source_target_pairs={{0,16},{16,0},{32,48},{48,32},{64,80},{80,64},{96,112},{112,96},{1... | collective-permute-start | bytes 1572872 | tf_op jit(solution)/shard_map/ppermute | solution.py:175
  35.8 0.0 all-to-all-done.1.refs_0_
  35.8 1.9 %collective-permute-start.4 = (f32[4,4,16,512]{3,2,1,0:T(8,128)S(1)}, f32[4,4,16,512]{3,2,1,0:T(8,128)S(1)}, u32[]{:S(2)}, u32[]{:S(2)}) collective-permute-start(f32[4,4,16,512]{3,2,1,0:T(8,128)S(1)} %all-to-all-done.1.refs_0_), channel_id=1, source_target_pairs={{0,96},{96,192},{192,288},{288,384},{384,480},{480,576},{576,672},... | collective-permute-start | bytes 1572872 | tf_op jit(solution)/shard_map/ppermute | solution.py:164
  37.7 17.8 %collective-permute-done.refs_2_ = f32[64,2,8,128]{3,2,1,0:T(8,128)S(1)} collective-permute-done((f32[64,2,8,128]{3,2,1,0:T(8,128)S(1)}, f32[64,2,8,128]{3,2,1,0:T(8,128)S(1)}, u32[]{:S(2)}, u32[]{:S(2)}) %collective-permute-start) | collective-permute-done | bytes 524320 | tf_op jit(solution)/shard_map/ppermute | solution.py:175
  55.5 0.0 collective-permute-done.1.refs_3_
  55.5 0.0 copy-done.5
  55.5 1.7 %stencil.2.refs_1_ = f32[64,2,8,128]{3,2,1,0:T(8,128)S(1)} custom-call(s32[2]{0:T(128)S(1)} %pad_add_fusion.refs_0_.at_ref, f32[64,2,8,128]{3,2,1,0:T(8,128)S(1)} %copy-done, f32[64,2,8,128]{3,2,1,0:T(8,128)S(1)} %collective-permute-done.refs_2_, f32[64,2,8,128]{3,2,1,0:T(8,128)S(1)} %collective-permute-done.1.refs_3_, f32[2,8,128]{2,1,0:T(8,128)S(1)} %copy-done.5), custom_call_target="tpu_custom_call" | custom-call | tf_op jit(solution)/shard_map/stencil/pallas_call | solution.py:64
  57.2 6.2 %collective-permute-start.2 = (f32[64,2,8,128]{3,2,1,0:T(8,128)S(1)}, f32[64,2,8,128]{3,2,1,0:T(8,128)S(1)}, u32[]{:S(2)}, u32[]{:S(2)}) collective-permute-start(f32[64,2,8,128]{3,2,1,0:T(8,128)S(1)} %stencil.2.refs_1_), channel_id=1, source_target_pairs={{0,752},{16,32},{32,16},{48,64},{64,48},{80,96},{96,80},{112,128},... | collective-permute-start | bytes 1572872 | tf_op jit(solution)/shard_map/ppermute | solution.py:175
  63.4 4.8 %collective-permute-start.3 = (f32[64,2,8,128]{3,2,1,0:T(8,128)S(1)}, f32[64,2,8,128]{3,2,1,0:T(8,128)S(1)}, u32[]{:S(2)}, u32[]{:S(2)}) collective-permute-start(f32[64,2,8,128]{3,2,1,0:T(8,128)S(1)} %stencil.2.refs_1_), channel_id=1, source_target_pairs={{0,16},{16,0},{32,48},{48,32},{64,80},{80,64},{96,112},{112,96},{1... | collective-permute-start | bytes 1572872 | tf_op jit(solution)/shard_map/ppermute | solution.py:175
  68.2 0.0 collective-permute-done.4.refs_2_
  68.2 13.4 %collective-permute-done.2.refs_2_ = f32[64,2,8,128]{3,2,1,0:T(8,128)S(1)} collective-permute-done((f32[64,2,8,128]{3,2,1,0:T(8,128)S(1)}, f32[64,2,8,128]{3,2,1,0:T(8,128)S(1)}, u32[]{:S(2)}, u32[]{:S(2)}) %collective-permute-start.2) | collective-permute-done | bytes 524320 | tf_op jit(solution)/shard_map/ppermute | solution.py:175
  81.6 0.0 collective-permute-done.3.refs_3_
  81.6 2.5 %stencil.3 = f32[2,8,64,128]{3,2,1,0:T(8,128)} custom-call(s32[2]{0:T(128)S(1)} %pad_add_fusion.refs_0_.at_ref, f32[64,2,8,128]{3,2,1,0:T(8,128)S(1)} %stencil.2.refs_1_, f32[64,2,8,128]{3,2,1,0:T(8,128)S(1)} %collective-permute-done.2.refs_2_, f32[64,2,8,128]{3,2,1,0:T(8,128)S(1)} %collective-permute-done.3.refs_3_, f32[2,8,128]{2,1,0:T(8,128)S(1)} %copy-done.5, ...), custom_call_target="tpu_custom_call" | custom-call | tf_op jit(solution)/shard_map/stencil/pallas_call | solution.py:64
  84.1 9.5 %all-to-all-start.2 = ((f32[16,64,128]{2,1,0:T(8,128)}), f32[16,64,128]{2,1,0:T(8,128)S(1)}, u32[]{:S(2)}, u32[]{:S(2)}) async-start(f32[16,64,128]{2,1,0:T(8,128)} %bitcast.4), calls=%async_computation.2 | async-start | bytes 1048576 | tf_op jit(solution)/shard_map/all_to_all | solution.py:195
  93.6 4.8 %collective-permute-start.7 = (f32[4,4,16,512]{3,2,1,0:T(8,128)S(1)}, f32[4,4,16,512]{3,2,1,0:T(8,128)S(1)}, u32[]{:S(2)}, u32[]{:S(2)}) collective-permute-start(f32[4,4,16,512]{3,2,1,0:T(8,128)S(1)} %all-to-all-done.1.refs_0_), channel_id=1, source_target_pairs={{96,0},{192,96},{288,192},{384,288},{480,384},{576,480},{672,576},... | collective-permute-start | bytes 1572872 | tf_op jit(solution)/shard_map/ppermute | solution.py:165
  98.5 1.9 %collective-permute-start.9 = (f32[4,4,16,512]{3,2,1,0:T(8,128)S(1)}, f32[4,4,16,512]{3,2,1,0:T(8,128)S(1)}, u32[]{:S(2)}, u32[]{:S(2)}) collective-permute-start(f32[4,4,16,512]{3,2,1,0:T(8,128)S(1)} %collective-permute-done.4.refs_2_), channel_id=1, source_target_pairs={{0,96},{96,192},{192,288},{288,384},{384,480},{480,576},{576,672},... | collective-permute-start | bytes 1572872 | tf_op jit(solution)/shard_map/ppermute | solution.py:167
  100.4 4.6 %collective-permute-start.5 = (f32[4,4,16,512]{3,2,1,0:T(8,128)S(1)}, f32[4,4,16,512]{3,2,1,0:T(8,128)S(1)}, u32[]{:S(2)}, u32[]{:S(2)}) collective-permute-start(f32[4,4,16,512]{3,2,1,0:T(8,128)S(1)} %all-to-all-done.1.refs_0_), channel_id=1, source_target_pairs={{0,16},{16,0},{1,17},{17,1},{2,18},{18,2},{3,19},{19,3},{4,20},{20... | collective-permute-start | bytes 1572872 | tf_op jit(solution)/shard_map/ppermute | solution.py:170
  105.0 1.9 %collective-permute-start.6 = (f32[4,4,16,512]{3,2,1,0:T(8,128)S(1)}, f32[4,4,16,512]{3,2,1,0:T(8,128)S(1)}, u32[]{:S(2)}, u32[]{:S(2)}) collective-permute-start(f32[4,4,16,512]{3,2,1,0:T(8,128)S(1)} %collective-permute-done.4.refs_2_), channel_id=1, source_target_pairs={{0,16},{16,0},{1,17},{17,1},{2,18},{18,2},{3,19},{19,3},{4,20},{20... | collective-permute-start | bytes 1572872 | tf_op jit(solution)/shard_map/ppermute | solution.py:170
  106.9 1.7 %collective-permute-done.7.refs_4_ = f32[4,4,16,512]{3,2,1,0:T(8,128)S(1)} collective-permute-done((f32[4,4,16,512]{3,2,1,0:T(8,128)S(1)}, f32[4,4,16,512]{3,2,1,0:T(8,128)S(1)}, u32[]{:S(2)}, u32[]{:S(2)}) %collective-permute-start.7) | collective-permute-done | bytes 524320 | tf_op jit(solution)/shard_map/ppermute | solution.py:165
  108.6 3.9 %collective-permute-start.8 = (f32[4,4,16,512]{3,2,1,0:T(8,128)S(1)}, f32[4,4,16,512]{3,2,1,0:T(8,128)S(1)}, u32[]{:S(2)}, u32[]{:S(2)}) collective-permute-start(f32[4,4,16,512]{3,2,1,0:T(8,128)S(1)} %collective-permute-done.7.refs_4_), channel_id=1, source_target_pairs={{0,16},{16,0},{1,17},{17,1},{2,18},{18,2},{3,19},{19,3},{4,20},{20... | collective-permute-start | bytes 1572872 | tf_op jit(solution)/shard_map/ppermute | solution.py:170
  112.5 1.2 collective-permute-done.9.refs_6_
  113.7 4.1 %collective-permute-start.10 = (f32[4,4,16,512]{3,2,1,0:T(8,128)S(1)}, f32[4,4,16,512]{3,2,1,0:T(8,128)}, u32[]{:S(2)}, u32[]{:S(2)}) collective-permute-start(f32[4,4,16,512]{3,2,1,0:T(8,128)S(1)} %collective-permute-done.9.refs_6_), channel_id=1, source_target_pairs={{0,16},{16,0},{1,17},{17,1},{2,18},{18,2},{3,19},{19,3},{4,20},{20... | collective-permute-start | bytes 1572872 | tf_op jit(solution)/shard_map/ppermute | solution.py:170
  117.8 0.0 collective-permute-done.5.refs_1_
  117.8 0.0 collective-permute-done.6.refs_3_
  117.8 0.0 copy-start.1
  117.8 0.8 copy-done.1
  118.6 0.0 collective-permute-done.8.refs_5_
  118.6 0.0 copy-start.3
  118.6 0.8 copy-done.3
  119.4 0.0 collective-permute-done.10.refs_7_
  119.4 0.0 all-to-all-done.2
  119.5 0.0 copy-start.2
  119.5 1.0 copy-done.2
  120.5 0.0 copy-start.4
  120.5 1.0 copy-done.4
  121.5 3.0 %rotate.1 = f32[16,64,128]{2,1,0:T(8,128)S(1)} custom-call(s32[2]{0:T(128)S(1)} %pad_add_fusion.refs_0_.at_ref, f32[1024,128]{1,0:T(8,128)S(1)} %bitcast.10, f32[4,4,16,512]{3,2,1,0:T(8,128)S(1)} %all-to-all-done.1.refs_0_, f32[4,4,16,512]{3,2,1,0:T(8,128)S(1)} %collective-permute-done.5.refs_1_, f32[4,4,16,512]{3,2,1,0:T(8,128)S(1)} %collective-permute-done.4.refs_2_, ...), custom_call_target="tpu_custom_call" | custom-call | tf_op jit(solution)/shard_map/rotate/pallas_call | solution.py:110
  124.6 22.5 %all_to_all.21 = f32[16,64,128]{2,1,0:T(8,128)S(1)} all-to-all(f32[16,64,128]{2,1,0:T(8,128)S(1)} %rotate.1), channel_id=1, replica_groups=mesh['y'=8,'zh'=3,'c'=2,'x'=4,'zl'=4] {'x','zl'}, dimensions={0} | all-to-all | bytes 1048576 | tf_op jit(solution)/shard_map/all_to_all | solution.py:197
  147.1 1.1 copy.4
  (1 shorter events, 0.0 us)
Async XLA Ops:
  14.8 4.2 %copy-start = (f32[64,2,8,128]{3,2,1,0:T(8,128)S(1)}, f32[64,2,8,128]{3,2,1,0:T(8,128)}, u32[]{:S(2)}) copy-start(f32[64,2,8,128]{3,2,1,0:T(8,128)} %refs_5_.1) | copy-start | bytes 1572868
  14.8 40.7 %copy-start.5 = (f32[2,8,128]{2,1,0:T(8,128)S(1)}, f32[2,8,128]{2,1,0:T(8,128)}, u32[]{:S(2)}) copy-start(f32[2,8,128]{2,1,0:T(8,128)} %refs_4_.3) | copy-start | bytes 24580
  14.8 21.0 %all-to-all-start.1 = ((f32[4,4,16,512]{3,2,1,0:T(8,128)}), f32[4,4,16,512]{3,2,1,0:T(8,128)S(1)}, u32[]{:S(2)}, u32[]{:S(2)}) async-start(f32[4,4,16,512]{3,2,1,0:T(8,128)} %broadcast_in_dim.2), calls=%async_computation.1 | async-start | bytes 1048576 | tf_op jit(solution)/shard_map/all_to_all | solution.py:153
  19.0 36.6 %collective-permute-start = (f32[64,2,8,128]{3,2,1,0:T(8,128)S(1)}, f32[64,2,8,128]{3,2,1,0:T(8,128)S(1)}, u32[]{:S(2)}, u32[]{:S(2)}) collective-permute-start(f32[64,2,8,128]{3,2,1,0:T(8,128)S(1)} %copy-done), channel_id=1, source_target_pairs={{0,752},{16,32},{32,16},{48,64},{64,48},{80,96},{96,80},{112,128},... | collective-permute-start | bytes 1572872 | tf_op jit(solution)/shard_map/ppermute | solution.py:175
  31.7 23.8 %collective-permute-start.1 = (f32[64,2,8,128]{3,2,1,0:T(8,128)S(1)}, f32[64,2,8,128]{3,2,1,0:T(8,128)S(1)}, u32[]{:S(2)}, u32[]{:S(2)}) collective-permute-start(f32[64,2,8,128]{3,2,1,0:T(8,128)S(1)} %copy-done), channel_id=1, source_target_pairs={{0,16},{16,0},{32,48},{48,32},{64,80},{80,64},{96,112},{112,96},{1... | collective-permute-start | bytes 1572872 | tf_op jit(solution)/shard_map/ppermute | solution.py:175
  35.8 32.4 %collective-permute-start.4 = (f32[4,4,16,512]{3,2,1,0:T(8,128)S(1)}, f32[4,4,16,512]{3,2,1,0:T(8,128)S(1)}, u32[]{:S(2)}, u32[]{:S(2)}) collective-permute-start(f32[4,4,16,512]{3,2,1,0:T(8,128)S(1)} %all-to-all-done.1.refs_0_), channel_id=1, source_target_pairs={{0,96},{96,192},{192,288},{288,384},{384,480},{480,576},{576,672},... | collective-permute-start | bytes 1572872 | tf_op jit(solution)/shard_map/ppermute | solution.py:164
  57.2 24.3 %collective-permute-start.2 = (f32[64,2,8,128]{3,2,1,0:T(8,128)S(1)}, f32[64,2,8,128]{3,2,1,0:T(8,128)S(1)}, u32[]{:S(2)}, u32[]{:S(2)}) collective-permute-start(f32[64,2,8,128]{3,2,1,0:T(8,128)S(1)} %stencil.2.refs_1_), channel_id=1, source_target_pairs={{0,752},{16,32},{32,16},{48,64},{64,48},{80,96},{96,80},{112,128},... | collective-permute-start | bytes 1572872 | tf_op jit(solution)/shard_map/ppermute | solution.py:175
  63.4 18.1 %collective-permute-start.3 = (f32[64,2,8,128]{3,2,1,0:T(8,128)S(1)}, f32[64,2,8,128]{3,2,1,0:T(8,128)S(1)}, u32[]{:S(2)}, u32[]{:S(2)}) collective-permute-start(f32[64,2,8,128]{3,2,1,0:T(8,128)S(1)} %stencil.2.refs_1_), channel_id=1, source_target_pairs={{0,16},{16,0},{32,48},{48,32},{64,80},{80,64},{96,112},{112,96},{1... | collective-permute-start | bytes 1572872 | tf_op jit(solution)/shard_map/ppermute | solution.py:175
  84.1 35.4 %all-to-all-start.2 = ((f32[16,64,128]{2,1,0:T(8,128)}), f32[16,64,128]{2,1,0:T(8,128)S(1)}, u32[]{:S(2)}, u32[]{:S(2)}) async-start(f32[16,64,128]{2,1,0:T(8,128)} %bitcast.4), calls=%async_computation.2 | async-start | bytes 1048576 | tf_op jit(solution)/shard_map/all_to_all | solution.py:195
  93.6 15.0 %collective-permute-start.7 = (f32[4,4,16,512]{3,2,1,0:T(8,128)S(1)}, f32[4,4,16,512]{3,2,1,0:T(8,128)S(1)}, u32[]{:S(2)}, u32[]{:S(2)}) collective-permute-start(f32[4,4,16,512]{3,2,1,0:T(8,128)S(1)} %all-to-all-done.1.refs_0_), channel_id=1, source_target_pairs={{96,0},{192,96},{288,192},{384,288},{480,384},{576,480},{672,576},... | collective-permute-start | bytes 1572872 | tf_op jit(solution)/shard_map/ppermute | solution.py:165
  98.5 15.2 %collective-permute-start.9 = (f32[4,4,16,512]{3,2,1,0:T(8,128)S(1)}, f32[4,4,16,512]{3,2,1,0:T(8,128)S(1)}, u32[]{:S(2)}, u32[]{:S(2)}) collective-permute-start(f32[4,4,16,512]{3,2,1,0:T(8,128)S(1)} %collective-permute-done.4.refs_2_), channel_id=1, source_target_pairs={{0,96},{96,192},{192,288},{288,384},{384,480},{480,576},{576,672},... | collective-permute-start | bytes 1572872 | tf_op jit(solution)/shard_map/ppermute | solution.py:167
  100.4 17.4 %collective-permute-start.5 = (f32[4,4,16,512]{3,2,1,0:T(8,128)S(1)}, f32[4,4,16,512]{3,2,1,0:T(8,128)S(1)}, u32[]{:S(2)}, u32[]{:S(2)}) collective-permute-start(f32[4,4,16,512]{3,2,1,0:T(8,128)S(1)} %all-to-all-done.1.refs_0_), channel_id=1, source_target_pairs={{0,16},{16,0},{1,17},{17,1},{2,18},{18,2},{3,19},{19,3},{4,20},{20... | collective-permute-start | bytes 1572872 | tf_op jit(solution)/shard_map/ppermute | solution.py:170
  105.0 12.8 %collective-permute-start.6 = (f32[4,4,16,512]{3,2,1,0:T(8,128)S(1)}, f32[4,4,16,512]{3,2,1,0:T(8,128)S(1)}, u32[]{:S(2)}, u32[]{:S(2)}) collective-permute-start(f32[4,4,16,512]{3,2,1,0:T(8,128)S(1)} %collective-permute-done.4.refs_2_), channel_id=1, source_target_pairs={{0,16},{16,0},{1,17},{17,1},{2,18},{18,2},{3,19},{19,3},{4,20},{20... | collective-permute-start | bytes 1572872 | tf_op jit(solution)/shard_map/ppermute | solution.py:170
  108.6 10.0 %collective-permute-start.8 = (f32[4,4,16,512]{3,2,1,0:T(8,128)S(1)}, f32[4,4,16,512]{3,2,1,0:T(8,128)S(1)}, u32[]{:S(2)}, u32[]{:S(2)}) collective-permute-start(f32[4,4,16,512]{3,2,1,0:T(8,128)S(1)} %collective-permute-done.7.refs_4_), channel_id=1, source_target_pairs={{0,16},{16,0},{1,17},{17,1},{2,18},{18,2},{3,19},{19,3},{4,20},{20... | collective-permute-start | bytes 1572872 | tf_op jit(solution)/shard_map/ppermute | solution.py:170
  113.7 5.8 %collective-permute-start.10 = (f32[4,4,16,512]{3,2,1,0:T(8,128)S(1)}, f32[4,4,16,512]{3,2,1,0:T(8,128)}, u32[]{:S(2)}, u32[]{:S(2)}) collective-permute-start(f32[4,4,16,512]{3,2,1,0:T(8,128)S(1)} %collective-permute-done.9.refs_6_), channel_id=1, source_target_pairs={{0,16},{16,0},{1,17},{17,1},{2,18},{18,2},{3,19},{19,3},{4,20},{20... | collective-permute-start | bytes 1572872 | tf_op jit(solution)/shard_map/ppermute | solution.py:170
  117.8 0.8 copy-start.1
  118.6 0.8 copy-start.3
  119.5 1.0 copy-start.2
  120.5 1.0 copy-start.4

commit v9 on v7

--- a/solution.py
+++ b/solution.py
@@ -7,6 +7,7 @@
 from jax.sharding import Mesh, PartitionSpec as P
 
 GROUP = 8
+LATE = (1, 5, 7)
 GRID = ("y", "zh", "c")
 BAND = ("x", "zl")
 
@@ -72,7 +73,12 @@
 
 
 def rotate_kernel(at_ref, v, *refs):
-    pieces, out, wide = refs[:8], refs[8], refs[9]
+    pieces, out, wide, landed, sems = list(refs[:8]), *refs[8:]
+    copies = {}
+    for slot, at in enumerate(LATE):
+        copies[at] = pltpu.make_async_copy(pieces[at], landed.at[slot], sems.at[slot])
+        copies[at].start()
+        pieces[at] = landed.at[slot]
     core, y = at_ref[0], at_ref[1]
     nx, nzl, rows, half = pieces[0].shape
     value = v[...]
@@ -90,8 +96,11 @@
         rest = jnp.dot(low, wide[at, :nz], preferred_element_type=jnp.float32)
         return both[:, :nz] + both[:, nz:] + rest
 
-    for j, step in enumerate((0, 3, 1, 2)):
-        total = product(pieces[2 * j], core) + product(pieces[2 * j + 1], 1 - core)
+    for j, step in ((1, 3), (0, 0), (2, 1), (3, 2)):
+        total = product(pieces[2 * j], core)
+        if 2 * j + 1 in copies:
+            copies[2 * j + 1].wait()
+        total += product(pieces[2 * j + 1], 1 - core)
         place = pl.ds(pl.multiple_of(lax.rem(y + step, 4) * rows, rows), rows)
         for group in range(nx * nzl):
             out[group, place] = total[group * rows : (group + 1) * rows]
@@ -101,13 +110,17 @@
     return pl.pallas_call(
         rotate_kernel,
         out_shape=pltpu.VMEM(shape, v.dtype),
-        in_specs=[pl.BlockSpec(memory_space=pltpu.SMEM)]
-        + [pl.BlockSpec(memory_space=pltpu.VMEM)] * (1 + len(pieces)),
+        in_specs=[pl.BlockSpec(memory_space=pltpu.SMEM), pl.BlockSpec(memory_space=pltpu.VMEM)]
+        + [pl.BlockSpec(memory_space=pltpu.HBM if at in LATE else pltpu.VMEM) for at in range(len(pieces))],
         out_specs=pl.BlockSpec(memory_space=pltpu.VMEM),
-        scratch_shapes=[pltpu.VMEM((v.shape[0], 2 * v.shape[1]), jnp.bfloat16)],
+        scratch_shapes=[
+            pltpu.VMEM((v.shape[0], 2 * v.shape[1]), jnp.bfloat16),
+            pltpu.VMEM((len(LATE), *pieces[0].shape), jnp.float32),
+            pltpu.SemaphoreType.DMA((len(LATE),)),
+        ],
         compiler_params=pltpu.CompilerParams(vmem_limit_bytes=24 << 20),
         name="rotate",
-    )(at, *map(in_vmem, (v, *pieces)))
+    )(at, in_vmem(v), *(pltpu.with_memory_space_constraint(p, pltpu.HBM) if i in LATE else in_vmem(p) for i, p in enumerate(pieces)))
 
 
 def to_all(value, axis):

time: 149 us -> 147 us (0.987)
  local copies, waits for them, and re-layouts: 8.44 us -> 4.49 us
    unnamed x18 -> x10, local copies, waits for them, and re-layouts: 6.47 us -> 2.52 us
where the time goes in v9:
time: 147 us; the launch traced here: 146 us
  starting transfers between devices  64.6 us (44%)
  blocking collectives  34.9 us (24%)
  waiting for transfers between devices  34.1 us (23%)
  Pallas kernels  7.55 us (5%)
  local copies, waits for them, and re-layouts  4.49 us (3%)
    ppermute x4, waiting for transfers between devices, swap(): return lax.ppermute(value, GRID, pairs)  31.2 us
    ppermute x4, starting transfers between devices, swap(): return lax.ppermute(value, GRID, pairs)  27.7 us
    all_to_all x1, blocking collectives, per_device(): back = lax.all_to_all(mixed, BAND, 0, 0, tiled=True)  22.5 us
    ppermute x4, starting transfers between devices, gather_rotation(): pieces += [piece, lax.ppermute(piece, 'c', [(0, 1), (1, 0)])]  14.5 us
    all_to_all x1, blocking collectives, to_all(): return lax.all_to_all(copies, axis, 0, 0, tiled=True)  12.4 us
    all_to_all x1, starting transfers between devices, per_device(): parts = lax.all_to_all(parts, BAND, 0, 0, tiled=True)  9.42 us
    ppermute x1, starting transfers between devices, gather_rotation(): above = lax.ppermute(own, 'y', down)  4.93 us
    pallas_call x2, Pallas kernels, stencil(): pl.pallas_call(lambda *refs: stencil_kernel(combine, *refs), out_shape=pl...  4.19 us
  transfers between devices with their start and end apart: 13, of which 4 were waited for; matrix products, arithmetic and copies ran while one was open for 0% of the time, Pallas kernels for 1%

profile of v9, /device:TPU:1, one launch (start us, length us, event | category | flops | bytes accessed | tf_op | source)
XLA Modules:
  0.0 145.8 jit_solution(7897759203607829150)
XLA Ops:
  0.0 0.0 copy-start
  0.0 0.9 copy-done
  1.0 12.4 %all_to_all.20 = f32[4,16,512]{2,1,0:T(8,128)S(1)} all-to-all(f32[4,16,512]{2,1,0:T(8,128)S(1)} %broadcast_in_dim.4), channel_id=1, replica_groups=mesh['y'=8,'zh'=3,'c'=2,'x'=4,'zl'=4] {'zl'}, dimensions={0} | all-to-all | bytes 262144 | tf_op jit(solution)/shard_map/all_to_all | solution.py:128
  13.3 0.9 broadcast_in_dim.5
  14.2 0.0 copy-start.1
  14.2 0.0 copy-start.2
  14.2 4.1 %all-to-all-start.1 = ((f32[4,4,16,512]{3,2,1,0:T(8,128)}), f32[4,4,16,512]{3,2,1,0:T(8,128)S(1)}, u32[]{:S(2)}, u32[]{:S(2)}) async-start(f32[4,4,16,512]{3,2,1,0:T(8,128)} %broadcast_in_dim.5), calls=%async_computation.1 | async-start | bytes 1048576 | tf_op jit(solution)/shard_map/all_to_all | solution.py:128
  18.3 0.0 copy-done.1
  18.3 12.8 %collective-permute-start = (f32[64,2,8,128]{3,2,1,0:T(8,128)S(1)}, f32[64,2,8,128]{3,2,1,0:T(8,128)S(1)}, u32[]{:S(2)}, u32[]{:S(2)}) collective-permute-start(f32[64,2,8,128]{3,2,1,0:T(8,128)S(1)} %copy-done.1), channel_id=1, source_target_pairs={{0,752},{16,32},{32,16},{48,64},{64,48},{80,96},{96,80},{112,128},... | collective-permute-start | bytes 1572872 | tf_op jit(solution)/shard_map/ppermute | solution.py:150
  31.1 4.0 %collective-permute-start.1 = (f32[64,2,8,128]{3,2,1,0:T(8,128)S(1)}, f32[64,2,8,128]{3,2,1,0:T(8,128)S(1)}, u32[]{:S(2)}, u32[]{:S(2)}) collective-permute-start(f32[64,2,8,128]{3,2,1,0:T(8,128)S(1)} %copy-done.1), channel_id=1, source_target_pairs={{0,16},{16,0},{32,48},{48,32},{64,80},{80,64},{96,112},{112,96},{1... | collective-permute-start | bytes 1572872 | tf_op jit(solution)/shard_map/ppermute | solution.py:150
  35.1 0.0 all-to-all-done.1.refs_0_
  35.1 1.9 %collective-permute-start.4 = (f32[4,4,16,512]{3,2,1,0:T(8,128)S(1)}, f32[4,4,16,512]{3,2,1,0:T(8,128)S(1)}, u32[]{:S(2)}, u32[]{:S(2)}) collective-permute-start(f32[4,4,16,512]{3,2,1,0:T(8,128)S(1)} %all-to-all-done.1.refs_0_), channel_id=1, source_target_pairs={{0,96},{96,192},{192,288},{288,384},{384,480},{480,576},{576,672},... | collective-permute-start | bytes 1572872 | tf_op jit(solution)/shard_map/ppermute | solution.py:139
  37.1 0.1 pad_add_fusion.refs_0_.at_ref
  37.1 17.8 %collective-permute-done.refs_2_ = f32[64,2,8,128]{3,2,1,0:T(8,128)S(1)} collective-permute-done((f32[64,2,8,128]{3,2,1,0:T(8,128)S(1)}, f32[64,2,8,128]{3,2,1,0:T(8,128)S(1)}, u32[]{:S(2)}, u32[]{:S(2)}) %collective-permute-start) | collective-permute-done | bytes 524320 | tf_op jit(solution)/shard_map/ppermute | solution.py:150
  54.9 0.0 collective-permute-done.1.refs_3_
  54.9 0.0 copy-done.2
  54.9 1.7 %stencil.2.refs_1_ = f32[64,2,8,128]{3,2,1,0:T(8,128)S(1)} custom-call(s32[2]{0:T(128)S(1)} %pad_add_fusion.refs_0_.at_ref, f32[64,2,8,128]{3,2,1,0:T(8,128)S(1)} %copy-done.1, f32[64,2,8,128]{3,2,1,0:T(8,128)S(1)} %collective-permute-done.refs_2_, f32[64,2,8,128]{3,2,1,0:T(8,128)S(1)} %collective-permute-done.1.refs_3_, f32[2,8,128]{2,1,0:T(8,128)S(1)} %copy-done.2), custom_call_target="tpu_custom_call" | custom-call | tf_op jit(solution)/shard_map/stencil/pallas_call | solution.py:64
  56.6 6.2 %collective-permute-start.2 = (f32[64,2,8,128]{3,2,1,0:T(8,128)S(1)}, f32[64,2,8,128]{3,2,1,0:T(8,128)S(1)}, u32[]{:S(2)}, u32[]{:S(2)}) collective-permute-start(f32[64,2,8,128]{3,2,1,0:T(8,128)S(1)} %stencil.2.refs_1_), channel_id=1, source_target_pairs={{0,752},{16,32},{32,16},{48,64},{64,48},{80,96},{96,80},{112,128},... | collective-permute-start | bytes 1572872 | tf_op jit(solution)/shard_map/ppermute | solution.py:150
  62.8 4.8 %collective-permute-start.3 = (f32[64,2,8,128]{3,2,1,0:T(8,128)S(1)}, f32[64,2,8,128]{3,2,1,0:T(8,128)S(1)}, u32[]{:S(2)}, u32[]{:S(2)}) collective-permute-start(f32[64,2,8,128]{3,2,1,0:T(8,128)S(1)} %stencil.2.refs_1_), channel_id=1, source_target_pairs={{0,16},{16,0},{32,48},{48,32},{64,80},{80,64},{96,112},{112,96},{1... | collective-permute-start | bytes 1572872 | tf_op jit(solution)/shard_map/ppermute | solution.py:150
  67.5 0.0 collective-permute-done.4.refs_2_
  67.6 13.4 %collective-permute-done.2.refs_2_ = f32[64,2,8,128]{3,2,1,0:T(8,128)S(1)} collective-permute-done((f32[64,2,8,128]{3,2,1,0:T(8,128)S(1)}, f32[64,2,8,128]{3,2,1,0:T(8,128)S(1)}, u32[]{:S(2)}, u32[]{:S(2)}) %collective-permute-start.2) | collective-permute-done | bytes 524320 | tf_op jit(solution)/shard_map/ppermute | solution.py:150
  81.0 0.0 collective-permute-done.3.refs_3_
  81.0 2.5 %stencil.3 = f32[2,8,64,128]{3,2,1,0:T(8,128)} custom-call(s32[2]{0:T(128)S(1)} %pad_add_fusion.refs_0_.at_ref, f32[64,2,8,128]{3,2,1,0:T(8,128)S(1)} %stencil.2.refs_1_, f32[64,2,8,128]{3,2,1,0:T(8,128)S(1)} %collective-permute-done.2.refs_2_, f32[64,2,8,128]{3,2,1,0:T(8,128)S(1)} %collective-permute-done.3.refs_3_, f32[2,8,128]{2,1,0:T(8,128)S(1)} %copy-done.2, ...), custom_call_target="tpu_custom_call" | custom-call | tf_op jit(solution)/shard_map/stencil/pallas_call | solution.py:64
  83.5 9.4 %all-to-all-start.2 = ((f32[16,64,128]{2,1,0:T(8,128)}), f32[16,64,128]{2,1,0:T(8,128)S(1)}, u32[]{:S(2)}, u32[]{:S(2)}) async-start(f32[16,64,128]{2,1,0:T(8,128)} %bitcast.4), calls=%async_computation.2 | async-start | bytes 1048576 | tf_op jit(solution)/shard_map/all_to_all | solution.py:170
  92.9 4.9 %collective-permute-start.7 = (f32[4,4,16,512]{3,2,1,0:T(8,128)S(1)}, f32[4,4,16,512]{3,2,1,0:T(8,128)S(1)}, u32[]{:S(2)}, u32[]{:S(2)}) collective-permute-start(f32[4,4,16,512]{3,2,1,0:T(8,128)S(1)} %all-to-all-done.1.refs_0_), channel_id=1, source_target_pairs={{96,0},{192,96},{288,192},{384,288},{480,384},{576,480},{672,576},... | collective-permute-start | bytes 1572872 | tf_op jit(solution)/shard_map/ppermute | solution.py:140
  97.9 1.9 %collective-permute-start.9 = (f32[4,4,16,512]{3,2,1,0:T(8,128)S(1)}, f32[4,4,16,512]{3,2,1,0:T(8,128)S(1)}, u32[]{:S(2)}, u32[]{:S(2)}) collective-permute-start(f32[4,4,16,512]{3,2,1,0:T(8,128)S(1)} %collective-permute-done.4.refs_2_), channel_id=1, source_target_pairs={{0,96},{96,192},{192,288},{288,384},{384,480},{480,576},{576,672},... | collective-permute-start | bytes 1572872 | tf_op jit(solution)/shard_map/ppermute | solution.py:142
  99.8 4.6 %collective-permute-start.5 = (f32[4,4,16,512]{3,2,1,0:T(8,128)S(1)}, f32[4,4,16,512]{3,2,1,0:T(8,128)S(1)}, u32[]{:S(2)}, u32[]{:S(2)}) collective-permute-start(f32[4,4,16,512]{3,2,1,0:T(8,128)S(1)} %all-to-all-done.1.refs_0_), channel_id=1, source_target_pairs={{0,16},{16,0},{1,17},{17,1},{2,18},{18,2},{3,19},{19,3},{4,20},{20... | collective-permute-start | bytes 1572872 | tf_op jit(solution)/shard_map/ppermute | solution.py:145
  104.4 1.9 %collective-permute-start.6 = (f32[4,4,16,512]{3,2,1,0:T(8,128)S(1)}, f32[4,4,16,512]{3,2,1,0:T(8,128)S(1)}, u32[]{:S(2)}, u32[]{:S(2)}) collective-permute-start(f32[4,4,16,512]{3,2,1,0:T(8,128)S(1)} %collective-permute-done.4.refs_2_), channel_id=1, source_target_pairs={{0,16},{16,0},{1,17},{17,1},{2,18},{18,2},{3,19},{19,3},{4,20},{20... | collective-permute-start | bytes 1572872 | tf_op jit(solution)/shard_map/ppermute | solution.py:145
  106.3 1.7 %collective-permute-done.7.refs_4_ = f32[4,4,16,512]{3,2,1,0:T(8,128)S(1)} collective-permute-done((f32[4,4,16,512]{3,2,1,0:T(8,128)S(1)}, f32[4,4,16,512]{3,2,1,0:T(8,128)S(1)}, u32[]{:S(2)}, u32[]{:S(2)}) %collective-permute-start.7) | collective-permute-done | bytes 524320 | tf_op jit(solution)/shard_map/ppermute | solution.py:140
  108.0 3.9 %collective-permute-start.8 = (f32[4,4,16,512]{3,2,1,0:T(8,128)S(1)}, f32[4,4,16,512]{3,2,1,0:T(8,128)S(1)}, u32[]{:S(2)}, u32[]{:S(2)}) collective-permute-start(f32[4,4,16,512]{3,2,1,0:T(8,128)S(1)} %collective-permute-done.7.refs_4_), channel_id=1, source_target_pairs={{0,16},{16,0},{1,17},{17,1},{2,18},{18,2},{3,19},{19,3},{4,20},{20... | collective-permute-start | bytes 1572872 | tf_op jit(solution)/shard_map/ppermute | solution.py:145
  111.9 1.2 collective-permute-done.9.refs_6_
  113.1 4.1 %collective-permute-start.10 = (f32[4,4,16,512]{3,2,1,0:T(8,128)S(1)}, f32[4,4,16,512]{3,2,1,0:T(8,128)}, u32[]{:S(2)}, u32[]{:S(2)}) collective-permute-start(f32[4,4,16,512]{3,2,1,0:T(8,128)S(1)} %collective-permute-done.9.refs_6_), channel_id=1, source_target_pairs={{0,16},{16,0},{1,17},{17,1},{2,18},{18,2},{3,19},{19,3},{4,20},{20... | collective-permute-start | bytes 1572872 | tf_op jit(solution)/shard_map/ppermute | solution.py:145
  117.2 0.0 collective-permute-done.5.refs_1_
  117.2 0.0 copy-start.3
  117.2 0.0 collective-permute-done.6.refs_3_
  117.2 0.0 collective-permute-done.8.refs_5_
  117.2 0.8 copy-done.3
  118.0 0.0 copy-start.4
  118.0 0.8 copy-done.4
  118.8 0.0 collective-permute-done.10.refs_7_
  118.8 0.0 all-to-all-done.2
  118.9 3.4 %rotate.1 = f32[16,64,128]{2,1,0:T(8,128)S(1)} custom-call(s32[2]{0:T(128)S(1)} %pad_add_fusion.refs_0_.at_ref, f32[1024,128]{1,0:T(8,128)S(1)} %bitcast.11, f32[4,4,16,512]{3,2,1,0:T(8,128)S(1)} %all-to-all-done.1.refs_0_, f32[4,4,16,512]{3,2,1,0:T(8,128)} %copy-done.3, f32[4,4,16,512]{3,2,1,0:T(8,128)S(1)} %collective-permute-done.4.refs_2_, ...), custom_call_target="tpu_custom_call" | custom-call | tf_op jit(solution)/shard_map/rotate/pallas_call | solution.py:110
  122.2 22.5 %all_to_all.21 = f32[16,64,128]{2,1,0:T(8,128)S(1)} all-to-all(f32[16,64,128]{2,1,0:T(8,128)S(1)} %rotate.1), channel_id=1, replica_groups=mesh['y'=8,'zh'=3,'c'=2,'x'=4,'zl'=4] {'x','zl'}, dimensions={0} | all-to-all | bytes 1048576 | tf_op jit(solution)/shard_map/all_to_all | solution.py:172
  144.7 1.1 copy.4
  (3 shorter events, 0.0 us)
Async XLA Ops:
  0.0 1.0 copy-start
  14.2 4.2 %copy-start.1 = (f32[64,2,8,128]{3,2,1,0:T(8,128)S(1)}, f32[64,2,8,128]{3,2,1,0:T(8,128)}, u32[]{:S(2)}) copy-start(f32[64,2,8,128]{3,2,1,0:T(8,128)} %refs_5_.1) | copy-start | bytes 1572868
  14.2 40.7 %copy-start.2 = (f32[2,8,128]{2,1,0:T(8,128)S(1)}, f32[2,8,128]{2,1,0:T(8,128)}, u32[]{:S(2)}) copy-start(f32[2,8,128]{2,1,0:T(8,128)} %refs_4_.3) | copy-start | bytes 24580
  14.2 20.9 %all-to-all-start.1 = ((f32[4,4,16,512]{3,2,1,0:T(8,128)}), f32[4,4,16,512]{3,2,1,0:T(8,128)S(1)}, u32[]{:S(2)}, u32[]{:S(2)}) async-start(f32[4,4,16,512]{3,2,1,0:T(8,128)} %broadcast_in_dim.5), calls=%async_computation.1 | async-start | bytes 1048576 | tf_op jit(solution)/shard_map/all_to_all | solution.py:128
  18.3 36.6 %collective-permute-start = (f32[64,2,8,128]{3,2,1,0:T(8,128)S(1)}, f32[64,2,8,128]{3,2,1,0:T(8,128)S(1)}, u32[]{:S(2)}, u32[]{:S(2)}) collective-permute-start(f32[64,2,8,128]{3,2,1,0:T(8,128)S(1)} %copy-done.1), channel_id=1, source_target_pairs={{0,752},{16,32},{32,16},{48,64},{64,48},{80,96},{96,80},{112,128},... | collective-permute-start | bytes 1572872 | tf_op jit(solution)/shard_map/ppermute | solution.py:150
  31.1 23.8 %collective-permute-start.1 = (f32[64,2,8,128]{3,2,1,0:T(8,128)S(1)}, f32[64,2,8,128]{3,2,1,0:T(8,128)S(1)}, u32[]{:S(2)}, u32[]{:S(2)}) collective-permute-start(f32[64,2,8,128]{3,2,1,0:T(8,128)S(1)} %copy-done.1), channel_id=1, source_target_pairs={{0,16},{16,0},{32,48},{48,32},{64,80},{80,64},{96,112},{112,96},{1... | collective-permute-start | bytes 1572872 | tf_op jit(solution)/shard_map/ppermute | solution.py:150
  35.1 32.4 %collective-permute-start.4 = (f32[4,4,16,512]{3,2,1,0:T(8,128)S(1)}, f32[4,4,16,512]{3,2,1,0:T(8,128)S(1)}, u32[]{:S(2)}, u32[]{:S(2)}) collective-permute-start(f32[4,4,16,512]{3,2,1,0:T(8,128)S(1)} %all-to-all-done.1.refs_0_), channel_id=1, source_target_pairs={{0,96},{96,192},{192,288},{288,384},{384,480},{480,576},{576,672},... | collective-permute-start | bytes 1572872 | tf_op jit(solution)/shard_map/ppermute | solution.py:139
  56.6 24.4 %collective-permute-start.2 = (f32[64,2,8,128]{3,2,1,0:T(8,128)S(1)}, f32[64,2,8,128]{3,2,1,0:T(8,128)S(1)}, u32[]{:S(2)}, u32[]{:S(2)}) collective-permute-start(f32[64,2,8,128]{3,2,1,0:T(8,128)S(1)} %stencil.2.refs_1_), channel_id=1, source_target_pairs={{0,752},{16,32},{32,16},{48,64},{64,48},{80,96},{96,80},{112,128},... | collective-permute-start | bytes 1572872 | tf_op jit(solution)/shard_map/ppermute | solution.py:150
  62.8 18.2 %collective-permute-start.3 = (f32[64,2,8,128]{3,2,1,0:T(8,128)S(1)}, f32[64,2,8,128]{3,2,1,0:T(8,128)S(1)}, u32[]{:S(2)}, u32[]{:S(2)}) collective-permute-start(f32[64,2,8,128]{3,2,1,0:T(8,128)S(1)} %stencil.2.refs_1_), channel_id=1, source_target_pairs={{0,16},{16,0},{32,48},{48,32},{64,80},{80,64},{96,112},{112,96},{1... | collective-permute-start | bytes 1572872 | tf_op jit(solution)/shard_map/ppermute | solution.py:150
  83.5 35.4 %all-to-all-start.2 = ((f32[16,64,128]{2,1,0:T(8,128)}), f32[16,64,128]{2,1,0:T(8,128)S(1)}, u32[]{:S(2)}, u32[]{:S(2)}) async-start(f32[16,64,128]{2,1,0:T(8,128)} %bitcast.4), calls=%async_computation.2 | async-start | bytes 1048576 | tf_op jit(solution)/shard_map/all_to_all | solution.py:170
  92.9 15.1 %collective-permute-start.7 = (f32[4,4,16,512]{3,2,1,0:T(8,128)S(1)}, f32[4,4,16,512]{3,2,1,0:T(8,128)S(1)}, u32[]{:S(2)}, u32[]{:S(2)}) collective-permute-start(f32[4,4,16,512]{3,2,1,0:T(8,128)S(1)} %all-to-all-done.1.refs_0_), channel_id=1, source_target_pairs={{96,0},{192,96},{288,192},{384,288},{480,384},{576,480},{672,576},... | collective-permute-start | bytes 1572872 | tf_op jit(solution)/shard_map/ppermute | solution.py:140
  97.9 15.2 %collective-permute-start.9 = (f32[4,4,16,512]{3,2,1,0:T(8,128)S(1)}, f32[4,4,16,512]{3,2,1,0:T(8,128)S(1)}, u32[]{:S(2)}, u32[]{:S(2)}) collective-permute-start(f32[4,4,16,512]{3,2,1,0:T(8,128)S(1)} %collective-permute-done.4.refs_2_), channel_id=1, source_target_pairs={{0,96},{96,192},{192,288},{288,384},{384,480},{480,576},{576,672},... | collective-permute-start | bytes 1572872 | tf_op jit(solution)/shard_map/ppermute | solution.py:142
  99.8 17.4 %collective-permute-start.5 = (f32[4,4,16,512]{3,2,1,0:T(8,128)S(1)}, f32[4,4,16,512]{3,2,1,0:T(8,128)S(1)}, u32[]{:S(2)}, u32[]{:S(2)}) collective-permute-start(f32[4,4,16,512]{3,2,1,0:T(8,128)S(1)} %all-to-all-done.1.refs_0_), channel_id=1, source_target_pairs={{0,16},{16,0},{1,17},{17,1},{2,18},{18,2},{3,19},{19,3},{4,20},{20... | collective-permute-start | bytes 1572872 | tf_op jit(solution)/shard_map/ppermute | solution.py:145
  104.4 12.8 %collective-permute-start.6 = (f32[4,4,16,512]{3,2,1,0:T(8,128)S(1)}, f32[4,4,16,512]{3,2,1,0:T(8,128)S(1)}, u32[]{:S(2)}, u32[]{:S(2)}) collective-permute-start(f32[4,4,16,512]{3,2,1,0:T(8,128)S(1)} %collective-permute-done.4.refs_2_), channel_id=1, source_target_pairs={{0,16},{16,0},{1,17},{17,1},{2,18},{18,2},{3,19},{19,3},{4,20},{20... | collective-permute-start | bytes 1572872 | tf_op jit(solution)/shard_map/ppermute | solution.py:145
  108.0 9.2 %collective-permute-start.8 = (f32[4,4,16,512]{3,2,1,0:T(8,128)S(1)}, f32[4,4,16,512]{3,2,1,0:T(8,128)S(1)}, u32[]{:S(2)}, u32[]{:S(2)}) collective-permute-start(f32[4,4,16,512]{3,2,1,0:T(8,128)S(1)} %collective-permute-done.7.refs_4_), channel_id=1, source_target_pairs={{0,16},{16,0},{1,17},{17,1},{2,18},{18,2},{3,19},{19,3},{4,20},{20... | collective-permute-start | bytes 1572872 | tf_op jit(solution)/shard_map/ppermute | solution.py:145
  113.1 5.8 %collective-permute-start.10 = (f32[4,4,16,512]{3,2,1,0:T(8,128)S(1)}, f32[4,4,16,512]{3,2,1,0:T(8,128)}, u32[]{:S(2)}, u32[]{:S(2)}) collective-permute-start(f32[4,4,16,512]{3,2,1,0:T(8,128)S(1)} %collective-permute-done.9.refs_6_), channel_id=1, source_target_pairs={{0,16},{16,0},{1,17},{17,1},{2,18},{18,2},{3,19},{19,3},{4,20},{20... | collective-permute-start | bytes 1572872 | tf_op jit(solution)/shard_map/ppermute | solution.py:145
  117.2 0.8 copy-start.3
  118.0 0.8 copy-start.4
